TPU v7x, 768 devices: a whole 4x8x12 slice. The times are simulated.
768 devices in a mesh: seq: 128 (over x, z_hi, y, core), wt: 6 (over z_lo).
Axes of the slice: x: 4, y: 8, z: 12 (z_hi: 2, z_lo: 6; z = z_hi * 6 + z_lo), core: 2. Of those that a mesh axis runs over, the one named last changes fastest.
Arguments:
- hidden_rows: bfloat16 [32768, 2688], P('seq'), may hold values from -24 to 24
- value_weight: bfloat16 [2688, 1536], P('seq', 'wt'), may hold values from -0.125 to 0.125
- queries: bfloat16 [32768, 3072], P('seq', 'wt'), may hold values from -60 to 60
- key_rows: bfloat16 [32768, 1536], P('seq', 'wt'), may hold values from -4.1 to 4.1
- out_grad: bfloat16 [32768, 3072], P('seq', 'wt'), may hold values from -6 to 6
- segments: int32 [32768], replicated, may hold values from 0 to 15, never falling along the last dimension, each value on 1 to 4096 neighbouring positions
Outputs:
- attention: bfloat16 [32768, 3072], P('seq', 'wt')
- weight_grad: float32 [2688, 1536], P('seq', 'wt')
Inputs may be any that keep to these rules, and one draw needn't show every extreme that they name: `segments`: never falling along the slab.
All inputs are finite; a program needn't handle non-finite values.
Results may differ from a plain program's by a relative error of at most 0.0057.
Values may be sent and summed in bfloat16 or wider, within the bound.
No kernel may reach another device: no remote copies, remote signals or barrier semaphores. Data moves between devices by JAX's collectives and lax.ppermute only.
A program may use at most 32 MiB of HBM per device.

v0:
```python
import math

import jax
import jax.numpy as jnp
from jax import lax
from jax.sharding import PartitionSpec as P

HD = 128
WINDOW = 1024


def passed_along(block, axis, distance):
    devices = range(lax.axis_size(axis))
    route = [(i - distance, i) for i in devices if i - distance in devices]
    return lax.ppermute(block, axis, route)


def attend(query_four, grad_four, key_three, value_three, allowed, scale):
    scores = (
        jnp.einsum("tkgd,lkd->kgtl", query_four, key_three, preferred_element_type=jnp.float32)
        * scale
    )
    scores = jnp.where(allowed[None, None], scores, -1e30)
    highest = jnp.max(scores, axis=-1, keepdims=True)
    weights = jnp.exp(scores - highest)
    probs = (weights / jnp.sum(weights, axis=-1, keepdims=True)).astype(jnp.bfloat16)
    output = jnp.einsum("kgtl,lkd->tkgd", probs, value_three, preferred_element_type=jnp.float32)
    partial_value = jnp.einsum(
        "kgtl,tkgd->lkd", probs, grad_four, preferred_element_type=jnp.float32
    )
    return (output, partial_value)


def per_device(hidden_rows, value_weight, queries, key_rows, out_grad, segments):
    rows_here = hidden_rows.shape[0]
    kv_width = value_weight.shape[1]
    kv_heads = kv_width // HD
    group_size = queries.shape[1] // kv_width
    blocks_back = (WINDOW + rows_here - 2) // rows_here
    key_span = (blocks_back + 1) * rows_here
    padding = blocks_back * rows_here
    scale = 1.0 / math.sqrt(HD)
    columns = hidden_rows
    values = jnp.dot(
        columns,
        lax.all_gather(value_weight, "seq", axis=0, tiled=True),
        preferred_element_type=jnp.float32,
    ).astype(jnp.bfloat16)
    earlier = [passed_along((key_rows, values), "seq", offset + 1) for offset in range(blocks_back)]
    ordered = list(reversed(earlier))
    key_window = jnp.concatenate([member[0] for member in ordered] + [key_rows], axis=0)
    value_window = jnp.concatenate([member[1] for member in ordered] + [values], axis=0)
    position = lax.axis_index("seq")
    segs_padded = jnp.concatenate([jnp.full((padding,), -1, jnp.int32), segments], axis=0)
    key_seg = lax.dynamic_slice_in_dim(segs_padded, position * rows_here, key_span, 0)
    query_seg = lax.dynamic_slice_in_dim(segments, position * rows_here, rows_here, 0)
    distance = (
        jnp.arange(rows_here, dtype=jnp.int32)[:, None]
        + padding
        - jnp.arange(key_span, dtype=jnp.int32)[None, :]
    )
    allowed = (distance >= 0) & (distance < WINDOW) & (query_seg[:, None] == key_seg[None, :])
    query_four = queries.reshape(rows_here, kv_heads, group_size, HD)
    grad_four = out_grad.reshape(rows_here, kv_heads, group_size, HD)
    key_three = key_window.reshape(key_span, kv_heads, HD)
    value_three = value_window.reshape(key_span, kv_heads, HD)
    output, partial_value = attend(query_four, grad_four, key_three, value_three, allowed, scale)
    attention = output.reshape(rows_here, kv_width * group_size).astype(jnp.bfloat16)
    partial_value = partial_value.reshape(key_span, kv_width).astype(jnp.bfloat16)
    gathered = partial_value[padding:].astype(jnp.float32)
    for offset in range(1, blocks_back + 1):
        portion = partial_value[
            (blocks_back - offset) * rows_here : (blocks_back - offset + 1) * rows_here
        ]
        gathered = gathered + passed_along(portion, "seq", -offset).astype(jnp.float32)
    value_grad = gathered.astype(jnp.bfloat16)
    columns = hidden_rows
    weight_grad = lax.psum_scatter(
        lax.dot_general(
            columns, value_grad, (((0,), (0,)), ((), ())), preferred_element_type=jnp.float32
        ),
        "seq",
        scatter_dimension=0,
        tiled=True,
    )
    return (attention, weight_grad)


def solution(mesh):
    in_specs = (P("seq", None), P("seq", "wt"), P("seq", "wt"), P("seq", "wt"), P("seq", "wt"), P())
    out_specs = (P("seq", "wt"), P("seq", "wt"))
    return jax.shard_map(
        per_device, mesh=mesh, in_specs=in_specs, out_specs=out_specs, check_vma=False
    )
```

profile of v0, /device:TPU:64, one launch (start us, length us, event | category | flops | bytes accessed | tf_op | source)
XLA Modules:
  0.0 2026.5 jit_solution(5066872668831850386)
XLA Ops:
  7.2 1.1 copy.28
  8.3 4.5 collective-permute-start.4
  12.8 2.6 collective-permute-start.5
  15.5 4.7 collective-permute-start.6
  20.2 2.7 collective-permute-start.7
  27.2 4.3 exponential_reduce_fusion
  31.5 3.8 divide_convert_fusion
  35.4 1.5 copy-done.1
  37.9 1.3 collective-permute-start.10
  39.2 1.3 collective-permute-start.11
  40.5 1.3 collective-permute-start.8
  41.8 1.3 collective-permute-start.9
  44.2 5.6 collective-permute-done.11
  49.8 3.7 collective-permute-done.9
  53.6 2.2 convolution_bitcast_fusion
  55.7 113.8 %all-gather.3.cloned.1.call-done = bf16[128,21,256]{2,1,0:T(8,128)(2,1)} async-done(((bf16[1,21,256]{2,1,0:T(8,128)(2,1)}), bf16[128,21,256]{2,1,0:T(8,128)(2,1)}) %all-gather.3.cloned.1.call-update) | async-done | bytes 1376272 | tf_op jit(solution)/shard_map/all_gather | solution.py:46
  169.6 2.4 reshape.90
  172.5 3.4 collective-permute-start
  175.9 2.4 collective-permute-start.1
  178.3 1.3 dynamic-slice
  180.2 3.4 collective-permute-start.2
  183.6 3.1 collective-permute-start.3
  187.9 2.3 convolution_convert_fusion
  191.0 1826.9 %all-reduce.4.cloned.1.call-done = f32[2688,256]{0,1:T(8,128)} async-done(((f32[2688,256]{0,1:T(8,128)}), f32[2688,256]{0,1:T(8,128)}) %all-reduce.4.cloned.1.call-update) | async-done | bytes 2752528
  (40 shorter events, 10.7 us)
Async XLA Ops:
  7.2 46.4 %copy-start = (bf16[256,2688]{1,0:T(8,128)(2,1)S(1)}, bf16[256,2688]{1,0:T(8,128)(2,1)}, u32[]{:S(2)}) copy-start(bf16[256,2688]{1,0:T(8,128)(2,1)} %param.6) | copy-start | bytes 4128772
  7.2 162.4 %all-gather.3.cloned.1.call-start = ((), (), s32[]{:S(2)}) async-start(), calls=%async_computation | async-start | bytes 1585152 | tf_op jit(solution)/shard_map/all_gather | solution.py:46
  8.3 18.8 collective-permute-start.4
  12.8 14.3 collective-permute-start.5
  15.5 11.7 collective-permute-start.6
  20.2 7.0 collective-permute-start.7
  22.9 1995.0 %all-reduce.4.cloned.1.call-start = ((), (), s32[]{:S(2)}) async-start(), calls=%async_computation.1 | async-start | bytes 5505024
  35.4 1.5 copy-start.1
  37.9 6.3 collective-permute-start.10
  39.2 10.6 collective-permute-start.11
  40.5 9.3 collective-permute-start.8
  41.8 11.8 collective-permute-start.9
  172.5 14.2 collective-permute-start
  175.9 10.8 collective-permute-start.1
  180.2 7.0 collective-permute-start.2
  183.6 4.0 collective-permute-start.3
Sparse Core Ops, SparseCore 0:
  23.0 146.4 all-gather.2
  172.8 1845.1 all-reduce.3
where the time goes:
time: 2030 us
  waiting for transfers between devices  1950 us (96%)
  starting transfers between devices  32 us (2%)
    unnamed x3, waiting for transfers between devices  1830 us
    all_gather x1, waiting for transfers between devices, per_device(): lax.all_gather(value_weight, 'seq', axis=0, tiled=True)  114 us
  transfers between devices with their start and end apart: 14, of which 7 were waited for; matrix products, arithmetic and copies ran while one was open for 1% of the time, Pallas kernels for 0%

commit v1 on v0

v1 whole, which is shorter than its diff:
```python
import math

import jax
import jax.numpy as jnp
from jax import lax
from jax.sharding import Mesh, PartitionSpec as P

HD = 128
WINDOW = 1024
GRID = ("x", "zh", "y", "c")
CHIPS = ("x", "zh", "y")
SWAP = [(0, 1), (1, 0)]
SIZES = (4, 2, 8, 2)


def chip_shift(block, distance):
    chips = lax.axis_size("x") * lax.axis_size("zh") * lax.axis_size("y")
    route = [(i - distance, i) for i in range(chips) if 0 <= i - distance < chips]
    return lax.ppermute(block, CHIPS, route)


def ordered(first, own, other, axis=0):
    return jnp.concatenate(
        [jnp.where(first, own, other), jnp.where(first, other, own)], axis=axis
    )


def per_device(hidden, weight, queries, keys, grads, segments):
    rows = hidden.shape[0]
    chip_rows = 2 * rows
    kv = weight.shape[1] // 2
    qw = queries.shape[1] // 2
    group = qw // kv
    nx, nz, ny = (lax.axis_size(a) for a in CHIPS)
    first = lax.axis_index("c") == 0
    low = lax.axis_index("zh") == 0
    chip = (lax.axis_index("x") * nz + lax.axis_index("zh")) * ny + lax.axis_index("y")
    scale = 1.0 / math.sqrt(HD)

    def halves(a):
        w = a.shape[1] // 2
        return jnp.where(first, a[:, :w], a[:, w:]), jnp.where(first, a[:, w:], a[:, :w])

    k_own, k_send = halves(keys)
    q_own, q_send = halves(queries)
    g_own, g_send = halves(grads)
    w_own, w_send = halves(weight)

    own = jnp.concatenate([k_own, q_own, g_own], axis=1)
    got = lax.ppermute(jnp.concatenate([k_send, q_send, g_send], axis=1), "c", SWAP)
    both = ordered(first, own, got)
    k_chip, q_chip, g_chip = both[:, :kv], both[:, kv : kv + qw], both[:, kv + qw :]
    k_win = jnp.concatenate([chip_shift(k_chip, 2), chip_shift(k_chip, 1), k_chip], axis=0)

    w_chip = ordered(first, w_own, lax.ppermute(w_send, "c", SWAP))
    w_pair = ordered(low, w_chip[None], lax.ppermute(w_chip, "zh", SWAP)[None])
    w_y = lax.all_to_all(jnp.broadcast_to(w_pair[None], (ny, *w_pair.shape)), "y", 0, 0)
    w_all = lax.all_to_all(jnp.broadcast_to(w_y[None], (nx, *w_y.shape)), "x", 0, 0)
    w_full = w_all.transpose(0, 2, 1, 3, 4).reshape(-1, kv)

    hidden_got = lax.ppermute(hidden, "c", SWAP)

    span = WINDOW + rows
    start = chip * chip_rows
    padding = 2 * chip_rows
    padded = jnp.concatenate([jnp.full((padding,), -1, jnp.int32), segments], axis=0)
    seg_win = lax.dynamic_slice_in_dim(padded, start, padding + chip_rows, 0)
    q_seg = seg_win[padding:].reshape(2, rows)
    k_seg = jnp.stack([seg_win[:span], seg_win[rows : rows + span]])
    distance = (
        jnp.arange(rows, dtype=jnp.int32)[:, None]
        + WINDOW
        - jnp.arange(span, dtype=jnp.int32)[None, :]
    )
    near = (distance >= 0) & (distance < WINDOW)
    allowed = near[None] & (q_seg[:, :, None] == k_seg[:, None, :])
    k_two = jnp.stack([k_win[:span], k_win[rows : rows + span]])
    q_four = q_chip.reshape(2, rows, group, HD)
    g_four = g_chip.reshape(2, rows, group, HD)
    scores = jnp.einsum("btgd,bld->bgtl", q_four, k_two, preferred_element_type=jnp.float32) * scale
    scores = jnp.where(allowed[:, None], scores, -1e30)
    highest = jnp.max(scores, axis=-1, keepdims=True)
    weights = jnp.exp(scores - highest)
    probs = (weights / jnp.sum(weights, axis=-1, keepdims=True)).astype(jnp.bfloat16)
    part = jnp.einsum("bgtl,btgd->bld", probs, g_four, preferred_element_type=jnp.float32)
    part = jnp.pad(part[0], ((0, rows), (0, 0))) + jnp.pad(part[1], ((rows, 0), (0, 0)))

    back2 = chip_shift(part[:chip_rows].astype(jnp.bfloat16), -2)
    back1 = chip_shift(part[chip_rows : 2 * chip_rows].astype(jnp.bfloat16), -1)
    value_grad = (
        part[2 * chip_rows :] + back1.astype(jnp.float32) + back2.astype(jnp.float32)
    ).astype(jnp.bfloat16)
    vg_own = jnp.where(first, value_grad[:rows], value_grad[rows:])
    vg_other = jnp.where(first, value_grad[rows:], value_grad[:rows])

    def outer(a, b):
        return lax.dot_general(a, b, (((0,), (0,)), ((), ())), preferred_element_type=jnp.float32)

    term = outer(hidden, vg_own) + outer(hidden_got, vg_other)

    term = term.astype(jnp.bfloat16).reshape(nx, nz * ny, -1, kv)
    term = jnp.sum(lax.all_to_all(term, "x", 0, 0).astype(jnp.float32), axis=0)
    term = term.astype(jnp.bfloat16).reshape(nz, ny, -1, kv).transpose(1, 0, 2, 3)
    term = jnp.sum(lax.all_to_all(term, "y", 0, 0).astype(jnp.float32), axis=0)
    keep = jnp.where(low, term[0], term[1])
    term = keep + lax.ppermute(jnp.where(low, term[1], term[0]), "zh", SWAP)
    cut = term.shape[0] // 2
    mine = jnp.where(first, term[:cut], term[cut:])
    theirs = lax.ppermute(jnp.where(first, term[cut:], term[:cut]), "c", SWAP)
    weight_grad = ordered(first, mine, theirs, axis=1)

    def project(a):
        return jnp.dot(a, w_full, preferred_element_type=jnp.float32).astype(jnp.bfloat16)

    v_chip = ordered(first, project(hidden), project(hidden_got))
    v_win = jnp.concatenate([chip_shift(v_chip, 2), chip_shift(v_chip, 1), v_chip], axis=0)
    v_two = jnp.stack([v_win[:span], v_win[rows : rows + span]])
    output = jnp.einsum("bgtl,bld->btgd", probs, v_two, preferred_element_type=jnp.float32)
    output = output.astype(jnp.bfloat16).reshape(2, rows, qw)
    out_own = jnp.where(first, output[0], output[1])
    out_got = lax.ppermute(jnp.where(first, output[1], output[0]), "c", SWAP)
    attention = ordered(first, out_own, out_got, axis=1)
    return attention, weight_grad


def solution(mesh):
    sizes = SIZES
    fine = Mesh(mesh.devices.reshape(*sizes, mesh.devices.shape[1]), (*GRID, "wt"))
    both = P(GRID, "wt")
    return jax.shard_map(
        per_device,
        mesh=fine,
        in_specs=(P(GRID, None), both, both, both, both, P()),
        out_specs=(both, both),
        check_vma=False,
    )
```

time: 2030 us -> 172 us (0.08)
  the two profiles are of different devices: /device:TPU:64 before, /device:TPU:71 now
where the time goes in v1:
time: 172 us; the launch traced here: 171 us
  starting transfers between devices  90.1 us (52%)
  waiting for transfers between devices  38.6 us (22%)
  matrix products  14.9 us (9%)
  local copies, waits for them, and re-layouts  14.7 us (9%)
  other arithmetic  11.2 us (7%)
    ppermute x6, waiting for transfers between devices, chip_shift(): return lax.ppermute(block, CHIPS, route)  31.4 us
    ppermute x6, starting transfers between devices, chip_shift(): return lax.ppermute(block, CHIPS, route)  16.9 us
    ppermute x1, starting transfers between devices, per_device(): w_pair = ordered(low, w_chip[None], lax.ppermute(w_chip, 'zh', SWAP)[None])  14 us
    all_to_all x1, starting transfers between devices, per_device(): term = jnp.sum(lax.all_to_all(term, 'y', 0, 0).astype(jnp.float32), axis=0)  13.8 us
    ppermute x1, starting transfers between devices, per_device(): term = keep + lax.ppermute(jnp.where(low, term[1], term[0]), 'zh', SWAP)  12 us
    all_to_all x1, starting transfers between devices, per_device(): lax.all_to_all(jnp.broadcast_to(w_pair[None], (ny, *w_pair.shape)), 'y',...  10.1 us
    dot_general x2, matrix products, outer(): lax.dot_general(a, b, (((0,), (0,)), ((), ())), preferred_element_type=jn...  5.4 us
    ppermute x1, starting transfers between devices, per_device(): theirs = lax.ppermute(jnp.where(first, term[cut:], term[:cut]), 'c', SWAP)  5.29 us
  transfers between devices with their start and end apart: 17, of which 10 were waited for; matrix products, arithmetic and copies ran while one was open for 15% of the time, Pallas kernels for 0%

profile of v1, /device:TPU:71, one launch (start us, length us, event | category | flops | bytes accessed | tf_op | source)
XLA Modules:
  0.0 170.5 jit_solution(17553908709782815261)
XLA Ops:
  2.8 2.6 %collective-permute-start.5 = (bf16[256,640]{1,0:T(8,128)(2,1)S(1)}, bf16[256,640]{1,0:T(8,128)(2,1)S(1)}, u32[]{:S(2)}, u32[]{:S(2)}) collective-permute-start(bf16[256,640]{1,0:T(8,128)(2,1)S(1)} %pad_maximum_fusion.5), channel_id=1, source_target_pairs={{0,6},{6,0},{1,7},{7,1},{2,8},{8,2},{3,9},{9,3},{4,10},{10,4},{5,1... | collective-permute-start | bytes 983048 | tf_op jit(solution)/shard_map/ppermute | solution.py:50
  7.3 2.4 %collective-permute-start = (bf16[21,128]{1,0:T(8,128)(2,1)S(1)}, bf16[21,128]{1,0:T(8,128)(2,1)S(1)}, u32[]{:S(2)}, u32[]{:S(2)}) collective-permute-start(bf16[21,128]{1,0:T(8,128)(2,1)S(1)} %broadcast_select_fusion.17), channel_id=1, source_target_pairs={{0,6},{6,0},{1,7},{7,1},{2,8},{8,2},{3,9},{9,3},{4,10},{10,4},{5,1... | collective-permute-start | bytes 16136 | tf_op jit(solution)/shard_map/ppermute | solution.py:55
  10.8 14.0 %collective-permute-start.1 = (bf16[42,128]{1,0:T(8,128)(2,1)S(1)}, bf16[42,128]{1,0:T(8,128)(2,1)S(1)}, u32[]{:S(2)}, u32[]{:S(2)}) collective-permute-start(bf16[42,128]{1,0:T(8,128)(2,1)S(1)} %pad_maximum_fusion.13), channel_id=1, source_target_pairs={{0,96},{96,0},{1,97},{97,1},{2,98},{98,2},{3,99},{99,3},{4,100},{1... | collective-permute-start | bytes 32264 | tf_op jit(solution)/shard_map/ppermute | solution.py:56
  26.0 4.2 %collective-permute-start.6 = (bf16[512,128]{1,0:T(8,128)(2,1)S(1)}, bf16[512,128]{1,0:T(8,128)(2,1)S(1)}, u32[]{:S(2)}, u32[]{:S(2)}) collective-permute-start(bf16[512,128]{1,0:T(8,128)(2,1)S(1)} %pad_maximum_fusion.9), channel_id=1, source_target_pairs={{0,24},{12,36},{24,48},{36,60},{48,72},{60,84},{72,96},{84,108},{9... | collective-permute-start | bytes 393224 | tf_op jit(solution)/shard_map/ppermute | solution.py:19
  30.2 3.2 %collective-permute-start.7 = (bf16[512,128]{1,0:T(8,128)(2,1)S(1)}, bf16[512,128]{1,0:T(8,128)(2,1)S(1)}, u32[]{:S(2)}, u32[]{:S(2)}) collective-permute-start(bf16[512,128]{1,0:T(8,128)(2,1)S(1)} %pad_maximum_fusion.9), channel_id=1, source_target_pairs={{0,12},{12,24},{24,36},{36,48},{48,60},{60,72},{72,84},{84,96},{96... | collective-permute-start | bytes 393224 | tf_op jit(solution)/shard_map/ppermute | solution.py:19
  34.2 10.1 %all-to-all-start = ((bf16[8,2,42,128]{3,1,2,0:T(2,128)(2,1)}), bf16[8,2,42,128]{3,1,2,0:T(2,128)(2,1)S(1)}, u32[]{:S(2)}, u32[]{:S(2)}) async-start(bf16[8,2,42,128]{3,1,2,0:T(2,128)(2,1)} %broadcast_in_dim.12), calls=%async_computation | async-start | bytes 344064 | tf_op jit(solution)/shard_map/all_to_all | solution.py:57
  44.5 9.0 %collective-permute-done.7 = bf16[512,128]{1,0:T(8,128)(2,1)S(1)} collective-permute-done((bf16[512,128]{1,0:T(8,128)(2,1)S(1)}, bf16[512,128]{1,0:T(8,128)(2,1)S(1)}, u32[]{:S(2)}, u32[]{:S(2)}) %collective-permute-start.7) | collective-permute-done | bytes 131104 | tf_op jit(solution)/shard_map/ppermute | solution.py:19
  53.7 4.1 %exponential_reduce_fusion = (f32[2,2,256]{2,1,0:T(2,128)S(1)}, f32[2,2,256,1280]{2,3,1,0:T(8,128)}) fusion(pred[2,256,1280]{1,2,0:T(8,128)(4,1)S(1)} %compare_and_fusion, bf16[1,1280,128]{2,1,0:T(8,128)(2,1)S(1)} %get-tuple-element.11, bf16[1,1280,128]{2,1,0:T(8,128)(2,1)S(1)} %get-tuple-element.10, bf16[2,256,2,128]{3,2,1,0:T(2,128)(2,1)S(1)} %reshape.78), kind=kOutput, calls=%fused_computation.4 | convolution fusion | flops 342099200 | bytes 6819840 | tf_op jit(solution)/shard_map/sub | solution.py:83
  57.8 3.8 %divide_convert_fusion = bf16[2,2,256,1280]{2,3,1,0:T(8,128)(2,1)S(1)} fusion(f32[2,2,256,1280]{2,3,1,0:T(8,128)} %get-tuple-element.38, f32[2,2,256]{2,1,0:T(2,128)S(1)} %get-tuple-element.37), kind=kLoop, calls=%fused_computation.3 | loop fusion | flops 2621440 | bytes 7868416 | tf_op jit(solution)/shard_map/convert_element_type | solution.py:84
  69.0 4.2 %all-to-all-start.1 = ((bf16[4,8,2,42,128]{4,1,3,2,0:T(8,128)(2,1)}), bf16[4,8,2,42,128]{4,1,3,2,0:T(8,128)(2,1)}, u32[]{:S(2)}, u32[]{:S(2)}) async-start(bf16[4,8,2,42,128]{4,1,3,2,0:T(8,128)(2,1)} %broadcast_in_dim.13), calls=%async_computation.1 | async-start | bytes 1376256 | tf_op jit(solution)/shard_map/all_to_all | solution.py:58
  74.6 4.3 %collective-permute-done.9 = bf16[512,128]{1,0:T(8,128)(2,1)} collective-permute-done((bf16[512,128]{1,0:T(8,128)(2,1)}, bf16[512,128]{1,0:T(8,128)(2,1)}, u32[]{:S(2)}, u32[]{:S(2)}) %collective-permute-start.9) | collective-permute-done | bytes 131104 | tf_op jit(solution)/shard_map/ppermute | solution.py:19
  80.0 2.8 %fusion.26 = f32[128,2688]{1,0:T(8,128)} fusion(bf16[256,2688]{1,0:T(8,128)(2,1)} %param.6, pred[]{:T(512)S(6)} %eq.23, bf16[512,128]{1,0:T(8,128)(2,1)S(1)} %fusion.17), kind=kOutput, calls=%fused_computation.68 | convolution fusion | flops 176193536 | bytes 2883585 | tf_op jit(solution)/shard_map/dot_general | solution.py:97
  88.3 2.6 %fusion.3 = bf16[2688,128]{0,1:T(8,128)(2,1)} fusion(f32[128,2688]{1,0:T(8,128)S(1)} %copy-done.1, bf16[256,2688]{1,0:T(8,128)(2,1)} %collective-permute-done.2, pred[]{:T(512)S(6)} %eq.23, bf16[512,128]{1,0:T(8,128)(2,1)S(1)} %fusion.17), kind=kOutput, calls=%fused_computation.7 | convolution fusion | flops 176881664 | bytes 3571713 | tf_op jit(solution)/shard_map/dot_general | solution.py:97
  90.9 2.2 %copy.47 = bf16[2688,128]{1,0:T(8,128)(2,1)} copy(bf16[2688,128]{0,1:T(8,128)(2,1)} %fusion.3) | data formatting | bytes 1376256 | tf_op jit(solution)/shard_map/convert_element_type | solution.py:101
  97.4 4.2 %all-to-all-start.2 = ((bf16[4,16,42,128]{3,1,2,0:T(8,128)(2,1)}), bf16[4,16,42,128]{3,1,2,0:T(8,128)(2,1)}, u32[]{:S(2)}, u32[]{:S(2)}) async-start(bf16[4,16,42,128]{3,1,2,0:T(8,128)(2,1)} %copy.48), calls=%async_computation.2 | async-start | bytes 1376256 | tf_op jit(solution)/shard_map/all_to_all | solution.py:102
  103.5 2.3 %collective-permute-start.3 = (bf16[512,128]{0,1:T(8,128)(2,1)S(1)}, bf16[512,128]{0,1:T(8,128)(2,1)S(1)}, u32[]{:S(2)}, u32[]{:S(2)}) collective-permute-start(bf16[512,128]{0,1:T(8,128)(2,1)S(1)} %pad_maximum_fusion.10), channel_id=1, source_target_pairs={{0,24},{12,36},{24,48},{36,60},{48,72},{60,84},{72,96},{84,108},{9... | collective-permute-start | bytes 393224 | tf_op jit(solution)/shard_map/ppermute | solution.py:19
  105.9 3.4 %collective-permute-start.4 = (bf16[512,128]{0,1:T(8,128)(2,1)S(1)}, bf16[512,128]{0,1:T(8,128)(2,1)S(1)}, u32[]{:S(2)}, u32[]{:S(2)}) collective-permute-start(bf16[512,128]{0,1:T(8,128)(2,1)S(1)} %pad_maximum_fusion.10), channel_id=1, source_target_pairs={{0,12},{12,24},{24,36},{36,48},{48,60},{60,72},{72,84},{84,96},{96... | collective-permute-start | bytes 393224 | tf_op jit(solution)/shard_map/ppermute | solution.py:19
  109.2 12.1 %collective-permute-done.3 = bf16[512,128]{0,1:T(8,128)(2,1)S(1)} collective-permute-done((bf16[512,128]{0,1:T(8,128)(2,1)S(1)}, bf16[512,128]{0,1:T(8,128)(2,1)S(1)}, u32[]{:S(2)}, u32[]{:S(2)}) %collective-permute-start.3) | collective-permute-done | bytes 131104 | tf_op jit(solution)/shard_map/ppermute | solution.py:19
  121.3 4.7 %collective-permute-done.4 = bf16[512,128]{0,1:T(8,128)(2,1)S(1)} collective-permute-done((bf16[512,128]{0,1:T(8,128)(2,1)S(1)}, bf16[512,128]{0,1:T(8,128)(2,1)S(1)}, u32[]{:S(2)}, u32[]{:S(2)}) %collective-permute-start.4) | collective-permute-done | bytes 131104 | tf_op jit(solution)/shard_map/ppermute | solution.py:19
  128.1 13.8 %all-to-all-start.3 = ((bf16[8,2,42,128]{3,1,2,0:T(2,128)(2,1)}), bf16[8,2,42,128]{3,1,2,0:T(2,128)(2,1)S(1)}, u32[]{:S(2)}, u32[]{:S(2)}) async-start(bf16[8,2,42,128]{3,1,2,0:T(2,128)(2,1)} %copy.49), calls=%async_computation.3 | async-start | bytes 344064 | tf_op jit(solution)/shard_map/all_to_all | solution.py:104
  142.5 2.8 %collective-permute-start.8 = (bf16[256,256]{1,0:T(8,128)(2,1)S(1)}, bf16[256,256]{1,0:T(8,128)(2,1)S(1)}, u32[]{:S(2)}, u32[]{:S(2)}) collective-permute-start(bf16[256,256]{1,0:T(8,128)(2,1)S(1)} %copy.59), channel_id=1, source_target_pairs={{0,6},{6,0},{1,7},{7,1},{2,8},{8,2},{3,9},{9,3},{4,10},{10,4},{5,1... | collective-permute-start | bytes 393224 | tf_op jit(solution)/shard_map/ppermute | solution.py:121
  145.3 5.1 %all-to-all-done.3 = bf16[8,2,42,128]{3,1,2,0:T(2,128)(2,1)S(1)} async-done(((bf16[8,2,42,128]{3,1,2,0:T(2,128)(2,1)}), bf16[8,2,42,128]{3,1,2,0:T(2,128)(2,1)S(1)}, u32[]{:S(2)}, u32[]{:S(2)}) %all-to-all-start.3) | async-done | bytes 172064 | tf_op jit(solution)/shard_map/all_to_all | solution.py:104
  150.6 12.0 %collective-permute-start.11 = (f32[42,128]{1,0:T(8,128)S(1)}, f32[42,128]{1,0:T(8,128)S(1)}, u32[]{:S(2)}, u32[]{:S(2)}) collective-permute-start(f32[42,128]{1,0:T(8,128)S(1)} %bitcast.75), channel_id=1, source_target_pairs={{0,96},{96,0},{1,97},{97,1},{2,98},{98,2},{3,99},{99,3},{4,100},{1... | collective-permute-start | bytes 64520 | tf_op jit(solution)/shard_map/ppermute | solution.py:106
  163.8 5.3 %collective-permute-start.12 = (f32[21,128]{1,0:T(8,128)S(1)}, f32[21,128]{1,0:T(8,128)S(1)}, u32[]{:S(2)}, u32[]{:S(2)}) collective-permute-start(f32[21,128]{1,0:T(8,128)S(1)} %slice_select_fusion), channel_id=1, source_target_pairs={{0,6},{6,0},{1,7},{7,1},{2,8},{8,2},{3,9},{9,3},{4,10},{10,4},{5,1... | collective-permute-start | bytes 32264 | tf_op jit(solution)/shard_map/ppermute | solution.py:109
  (79 shorter events, 34.4 us)
Async XLA Ops:
  0.6 6.7 %copy-start.3 = (bf16[21,256]{1,0:T(8,128)(2,1)S(1)}, bf16[21,256]{1,0:T(8,128)(2,1)}, u32[]{:S(2)}) copy-start(bf16[21,256]{1,0:T(8,128)(2,1)} %param.7) | copy-start | bytes 32260
  0.6 9.1 %copy-start.2 = (s32[32768]{0:T(1024)S(1)}, s32[32768]{0:T(1024)}, u32[]{:S(2)}) copy-start(s32[32768]{0:T(1024)} %param.11) | copy-start | bytes 393220
  2.8 23.0 %collective-permute-start.5 = (bf16[256,640]{1,0:T(8,128)(2,1)S(1)}, bf16[256,640]{1,0:T(8,128)(2,1)S(1)}, u32[]{:S(2)}, u32[]{:S(2)}) collective-permute-start(bf16[256,640]{1,0:T(8,128)(2,1)S(1)} %pad_maximum_fusion.5), channel_id=1, source_target_pairs={{0,6},{6,0},{1,7},{7,1},{2,8},{8,2},{3,9},{9,3},{4,10},{10,4},{5,1... | collective-permute-start | bytes 983048 | tf_op jit(solution)/shard_map/ppermute | solution.py:50
  5.4 82.9 %collective-permute-start.2 = (bf16[256,2688]{1,0:T(8,128)(2,1)}, bf16[256,2688]{1,0:T(8,128)(2,1)}, u32[]{:S(2)}, u32[]{:S(2)}) collective-permute-start(bf16[256,2688]{1,0:T(8,128)(2,1)} %param.6), channel_id=1, source_target_pairs={{0,6},{6,0},{1,7},{7,1},{2,8},{8,2},{3,9},{9,3},{4,10},{10,4},{5,1... | collective-permute-start | bytes 4128776 | tf_op jit(solution)/shard_map/ppermute | solution.py:61
  7.3 3.4 %collective-permute-start = (bf16[21,128]{1,0:T(8,128)(2,1)S(1)}, bf16[21,128]{1,0:T(8,128)(2,1)S(1)}, u32[]{:S(2)}, u32[]{:S(2)}) collective-permute-start(bf16[21,128]{1,0:T(8,128)(2,1)S(1)} %broadcast_select_fusion.17), channel_id=1, source_target_pairs={{0,6},{6,0},{1,7},{7,1},{2,8},{8,2},{3,9},{9,3},{4,10},{10,4},{5,1... | collective-permute-start | bytes 16136 | tf_op jit(solution)/shard_map/ppermute | solution.py:55
  10.8 15.0 %collective-permute-start.1 = (bf16[42,128]{1,0:T(8,128)(2,1)S(1)}, bf16[42,128]{1,0:T(8,128)(2,1)S(1)}, u32[]{:S(2)}, u32[]{:S(2)}) collective-permute-start(bf16[42,128]{1,0:T(8,128)(2,1)S(1)} %pad_maximum_fusion.13), channel_id=1, source_target_pairs={{0,96},{96,0},{1,97},{97,1},{2,98},{98,2},{3,99},{99,3},{4,100},{1... | collective-permute-start | bytes 32264 | tf_op jit(solution)/shard_map/ppermute | solution.py:56
  26.0 18.6 %collective-permute-start.6 = (bf16[512,128]{1,0:T(8,128)(2,1)S(1)}, bf16[512,128]{1,0:T(8,128)(2,1)S(1)}, u32[]{:S(2)}, u32[]{:S(2)}) collective-permute-start(bf16[512,128]{1,0:T(8,128)(2,1)S(1)} %pad_maximum_fusion.9), channel_id=1, source_target_pairs={{0,24},{12,36},{24,48},{36,60},{48,72},{60,84},{72,96},{84,108},{9... | collective-permute-start | bytes 393224 | tf_op jit(solution)/shard_map/ppermute | solution.py:19
  30.2 23.4 %collective-permute-start.7 = (bf16[512,128]{1,0:T(8,128)(2,1)S(1)}, bf16[512,128]{1,0:T(8,128)(2,1)S(1)}, u32[]{:S(2)}, u32[]{:S(2)}) collective-permute-start(bf16[512,128]{1,0:T(8,128)(2,1)S(1)} %pad_maximum_fusion.9), channel_id=1, source_target_pairs={{0,12},{12,24},{24,36},{36,48},{48,60},{60,72},{72,84},{84,96},{96... | collective-permute-start | bytes 393224 | tf_op jit(solution)/shard_map/ppermute | solution.py:19
  34.2 33.8 %all-to-all-start = ((bf16[8,2,42,128]{3,1,2,0:T(2,128)(2,1)}), bf16[8,2,42,128]{3,1,2,0:T(2,128)(2,1)S(1)}, u32[]{:S(2)}, u32[]{:S(2)}) async-start(bf16[8,2,42,128]{3,1,2,0:T(2,128)(2,1)} %broadcast_in_dim.12), calls=%async_computation | async-start | bytes 344064 | tf_op jit(solution)/shard_map/all_to_all | solution.py:57
  62.6 0.8 copy-start
  64.2 10.4 %collective-permute-start.10 = (bf16[512,128]{1,0:T(8,128)(2,1)}, bf16[512,128]{1,0:T(8,128)(2,1)}, u32[]{:S(2)}, u32[]{:S(2)}) collective-permute-start(bf16[512,128]{1,0:T(8,128)(2,1)} %get-tuple-element.9), channel_id=1, source_target_pairs={{24,0},{36,12},{48,24},{60,36},{72,48},{84,60},{96,72},{108,84},{1... | collective-permute-start | bytes 393224 | tf_op jit(solution)/shard_map/ppermute | solution.py:19
  66.1 12.8 %collective-permute-start.9 = (bf16[512,128]{1,0:T(8,128)(2,1)}, bf16[512,128]{1,0:T(8,128)(2,1)}, u32[]{:S(2)}, u32[]{:S(2)}) collective-permute-start(bf16[512,128]{1,0:T(8,128)(2,1)} %get-tuple-element.8), channel_id=1, source_target_pairs={{12,0},{24,12},{36,24},{48,36},{60,48},{72,60},{84,72},{96,84},{10... | collective-permute-start | bytes 393224 | tf_op jit(solution)/shard_map/ppermute | solution.py:19
  69.0 13.8 %all-to-all-start.1 = ((bf16[4,8,2,42,128]{4,1,3,2,0:T(8,128)(2,1)}), bf16[4,8,2,42,128]{4,1,3,2,0:T(8,128)(2,1)}, u32[]{:S(2)}, u32[]{:S(2)}) async-start(bf16[4,8,2,42,128]{4,1,3,2,0:T(8,128)(2,1)} %broadcast_in_dim.13), calls=%async_computation.1 | async-start | bytes 1376256 | tf_op jit(solution)/shard_map/all_to_all | solution.py:58
  86.2 2.1 %copy-start.1 = (f32[128,2688]{1,0:T(8,128)S(1)}, f32[128,2688]{1,0:T(8,128)}, u32[]{:S(2)}) copy-start(f32[128,2688]{1,0:T(8,128)} %fusion.26) | copy-start | bytes 4128772
  97.4 28.6 %all-to-all-start.2 = ((bf16[4,16,42,128]{3,1,2,0:T(8,128)(2,1)}), bf16[4,16,42,128]{3,1,2,0:T(8,128)(2,1)}, u32[]{:S(2)}, u32[]{:S(2)}) async-start(bf16[4,16,42,128]{3,1,2,0:T(8,128)(2,1)} %copy.48), calls=%async_computation.2 | async-start | bytes 1376256 | tf_op jit(solution)/shard_map/all_to_all | solution.py:102
  103.5 17.8 %collective-permute-start.3 = (bf16[512,128]{0,1:T(8,128)(2,1)S(1)}, bf16[512,128]{0,1:T(8,128)(2,1)S(1)}, u32[]{:S(2)}, u32[]{:S(2)}) collective-permute-start(bf16[512,128]{0,1:T(8,128)(2,1)S(1)} %pad_maximum_fusion.10), channel_id=1, source_target_pairs={{0,24},{12,36},{24,48},{36,60},{48,72},{60,84},{72,96},{84,108},{9... | collective-permute-start | bytes 393224 | tf_op jit(solution)/shard_map/ppermute | solution.py:19
  105.9 20.1 %collective-permute-start.4 = (bf16[512,128]{0,1:T(8,128)(2,1)S(1)}, bf16[512,128]{0,1:T(8,128)(2,1)S(1)}, u32[]{:S(2)}, u32[]{:S(2)}) collective-permute-start(bf16[512,128]{0,1:T(8,128)(2,1)S(1)} %pad_maximum_fusion.10), channel_id=1, source_target_pairs={{0,12},{12,24},{24,36},{36,48},{48,60},{60,72},{72,84},{84,96},{96... | collective-permute-start | bytes 393224 | tf_op jit(solution)/shard_map/ppermute | solution.py:19
  128.1 22.3 %all-to-all-start.3 = ((bf16[8,2,42,128]{3,1,2,0:T(2,128)(2,1)}), bf16[8,2,42,128]{3,1,2,0:T(2,128)(2,1)S(1)}, u32[]{:S(2)}, u32[]{:S(2)}) async-start(bf16[8,2,42,128]{3,1,2,0:T(2,128)(2,1)} %copy.49), calls=%async_computation.3 | async-start | bytes 344064 | tf_op jit(solution)/shard_map/all_to_all | solution.py:104
  142.5 20.1 %collective-permute-start.8 = (bf16[256,256]{1,0:T(8,128)(2,1)S(1)}, bf16[256,256]{1,0:T(8,128)(2,1)S(1)}, u32[]{:S(2)}, u32[]{:S(2)}) collective-permute-start(bf16[256,256]{1,0:T(8,128)(2,1)S(1)} %copy.59), channel_id=1, source_target_pairs={{0,6},{6,0},{1,7},{7,1},{2,8},{8,2},{3,9},{9,3},{4,10},{10,4},{5,1... | collective-permute-start | bytes 393224 | tf_op jit(solution)/shard_map/ppermute | solution.py:121
  150.6 13.2 %collective-permute-start.11 = (f32[42,128]{1,0:T(8,128)S(1)}, f32[42,128]{1,0:T(8,128)S(1)}, u32[]{:S(2)}, u32[]{:S(2)}) collective-permute-start(f32[42,128]{1,0:T(8,128)S(1)} %bitcast.75), channel_id=1, source_target_pairs={{0,96},{96,0},{1,97},{97,1},{2,98},{98,2},{3,99},{99,3},{4,100},{1... | collective-permute-start | bytes 64520 | tf_op jit(solution)/shard_map/ppermute | solution.py:106
  163.8 6.1 %collective-permute-start.12 = (f32[21,128]{1,0:T(8,128)S(1)}, f32[21,128]{1,0:T(8,128)S(1)}, u32[]{:S(2)}, u32[]{:S(2)}) collective-permute-start(f32[21,128]{1,0:T(8,128)S(1)} %slice_select_fusion), channel_id=1, source_target_pairs={{0,6},{6,0},{1,7},{7,1},{2,8},{8,2},{3,9},{9,3},{4,10},{10,4},{5,1... | collective-permute-start | bytes 32264 | tf_op jit(solution)/shard_map/ppermute | solution.py:109

commit v2 on v1

v2 whole, which is shorter than its diff:
```python
import functools
import math

import jax
import jax.numpy as jnp
from jax import lax
from jax.experimental import pallas as pl
from jax.experimental.pallas import tpu as pltpu
from jax.sharding import Mesh, PartitionSpec as P

HD = 128
WINDOW = 1024
GRID = ("x", "zh", "y", "c")
CHIPS = ("x", "zh", "y")
SWAP = [(0, 1), (1, 0)]
SIZES = (4, 2, 8, 2)
BF16, F32 = jnp.bfloat16, jnp.float32
VMEM = pl.BlockSpec(memory_space=pltpu.VMEM)
SMEM = pl.BlockSpec(memory_space=pltpu.SMEM)


def struct(shape, dtype):
    return jax.ShapeDtypeStruct(shape, dtype)


def dot(a, b, over_a, over_b):
    return lax.dot_general(a, b, (((over_a,), (over_b,)), ((), ())), preferred_element_type=F32)


def chip_shift(block, distance):
    chips = lax.axis_size("x") * lax.axis_size("zh") * lax.axis_size("y")
    route = [(i - distance, i) for i in range(chips) if 0 <= i - distance < chips]
    return lax.ppermute(block, CHIPS, route)


def ordered(first, own, other, axis=0):
    return jnp.concatenate(
        [jnp.where(first, own, other), jnp.where(first, other, own)], axis=axis
    )


def attend_kernel(rows, factor, q_ref, k2_ref, k1_ref, k0_ref, g_ref, low_ref, *rest):
    probs_ref, part2_ref, part1_ref, part0_ref, win, total = rest
    chip_rows = 2 * rows
    span = win.shape[0] - rows
    group = q_ref.shape[1] // HD
    for i, ref in enumerate((k2_ref, k1_ref, k0_ref)):
        win[i * chip_rows : (i + 1) * chip_rows] = ref[...]
    total[span:] = jnp.zeros((rows, HD), F32)
    for j in range(2):
        at = slice(j * rows, j * rows + span)
        keys = win[at]
        u = lax.broadcasted_iota(jnp.int32, (span, rows), 0) + j * rows
        t = lax.broadcasted_iota(jnp.int32, (span, rows), 1) + (2 * chip_rows + j * rows)
        allowed = (u <= t) & (u >= low_ref[:, j * rows : (j + 1) * rows])
        for h in range(group):
            tile = (slice(j * rows, (j + 1) * rows), slice(h * HD, (h + 1) * HD))
            s = jnp.where(allowed, dot(keys, q_ref[tile], 1, 1), -1e30)
            w = jnp.exp2((s - jnp.max(s, axis=0, keepdims=True)) * factor)
            p = (w * (1.0 / jnp.sum(w, axis=0, keepdims=True))).astype(BF16)
            probs_ref[j, h] = p
            part = jnp.dot(p, g_ref[tile], preferred_element_type=F32)
            if j == 0 and h == 0:
                total[at] = part
            else:
                total[at] += part
    part2_ref[...] = total[:chip_rows].astype(BF16)
    part1_ref[...] = total[chip_rows : 2 * chip_rows].astype(BF16)
    part0_ref[...] = total[2 * chip_rows :]


def output_kernel(rows, core_ref, probs_ref, v2_ref, v1_ref, v0_ref, out_ref, win):
    chip_rows = 2 * rows
    span = win.shape[0] - rows
    for i, ref in enumerate((v2_ref, v1_ref, v0_ref)):
        win[i * chip_rows : (i + 1) * chip_rows] = ref[...]
    for j in range(2):
        slot = core_ref[0] if j == 0 else 1 - core_ref[0]
        values = win[j * rows : j * rows + span]
        for h in range(probs_ref.shape[1]):
            o = dot(values, probs_ref[j, h], 0, 0)
            out_ref[slot, :, h * HD : (h + 1) * HD] = o.T.astype(BF16)


def outer_kernel(rows, core_ref, own_ref, got_ref, part_ref, back1_ref, back2_ref, out_ref, vg):
    vg[...] = (part_ref[...] + back1_ref[...].astype(F32) + back2_ref[...].astype(F32)).astype(BF16)
    mine = pl.multiple_of(core_ref[0] * rows, rows)
    a = vg[pl.ds(mine, rows)]
    b = vg[pl.ds(pl.multiple_of(rows - mine, rows), rows)]
    width = 3 * HD
    for i in range(0, own_ref.shape[1], width):
        at = slice(i, min(i + width, own_ref.shape[1]))
        t = dot(a, own_ref[:, at], 0, 0) + dot(b, got_ref[:, at], 0, 0)
        out_ref[at] = t.T.astype(BF16)


def per_device(hidden, weight, queries, keys, grads, segments):
    rows = hidden.shape[0]
    chip_rows = 2 * rows
    kv = weight.shape[1] // 2
    qw = queries.shape[1] // 2
    group = qw // kv
    cut = weight.shape[0]
    nx, nz, ny = (lax.axis_size(a) for a in CHIPS)
    core = lax.axis_index("c")
    first = core == 0
    low = lax.axis_index("zh") == 0
    chip = (lax.axis_index("x") * nz + lax.axis_index("zh")) * ny + lax.axis_index("y")
    factor = math.log2(math.e) / math.sqrt(HD)
    span = WINDOW + rows
    whole = span + rows
    core_arg = core.astype(jnp.int32)[None]

    def halves(a):
        w = a.shape[1] // 2
        return jnp.where(first, a[:, :w], a[:, w:]), jnp.where(first, a[:, w:], a[:, :w])

    k_own, k_send = halves(keys)
    q_own, q_send = halves(queries)
    g_own, g_send = halves(grads)
    w_own, w_send = halves(weight)
    tall = ((0, rows - cut), (0, 0))

    send = jnp.concatenate([k_send, q_send, g_send, jnp.pad(w_send, tall)], axis=1)
    got = lax.ppermute(send, "c", SWAP)
    k_chip = ordered(first, k_own, got[:, :kv])
    k_two = chip_shift(k_chip, 2)
    k_one = chip_shift(k_chip, 1)
    q_chip = ordered(first, q_own, got[:, kv : kv + qw])
    g_chip = ordered(first, g_own, got[:, kv + qw : kv + 2 * qw])

    w_chip = ordered(first, w_own, got[:cut, kv + 2 * qw :])
    w_far = lax.ppermute(w_chip, "zh", SWAP)
    w_pair = ordered(low, w_chip[None], w_far[None])
    w_y = lax.all_to_all(jnp.broadcast_to(w_pair[None], (ny, *w_pair.shape)), "y", 0, 0)
    w_y = w_y.transpose(1, 0, 2, 3).reshape(-1, kv)
    w_x = lax.all_to_all(jnp.broadcast_to(w_y[None], (nx, *w_y.shape)), "x", 0, 0)
    w_full = w_x.reshape(-1, kv)

    hidden_got = lax.ppermute(hidden, "c", SWAP)

    padding = 2 * chip_rows
    padded = jnp.concatenate([jnp.full((padding,), -1, jnp.int32), segments], axis=0)
    seg_win = lax.dynamic_slice_in_dim(padded, chip * chip_rows, whole, 0)
    begin = jnp.sum((seg_win[:, None] < seg_win[None, padding:]).astype(jnp.int32), axis=0)
    begin = jnp.maximum(begin, jnp.arange(chip_rows, dtype=jnp.int32) + (padding - WINDOW + 1))

    probs, part2, part1, part0 = pl.pallas_call(
        functools.partial(attend_kernel, rows, factor),
        out_shape=(
            struct((2, group, span, rows), BF16),
            struct((chip_rows, kv), BF16),
            struct((chip_rows, kv), BF16),
            struct((chip_rows, kv), F32),
        ),
        in_specs=[VMEM] * 6,
        out_specs=[VMEM] * 4,
        scratch_shapes=[pltpu.VMEM((whole, kv), BF16), pltpu.VMEM((whole, kv), F32)],
    )(q_chip, k_two, k_one, k_chip, g_chip, begin[None])
    back2 = chip_shift(part2, -2)
    back1 = chip_shift(part1, -1)

    v_own = jnp.dot(hidden, w_full, preferred_element_type=F32).astype(BF16)
    v_other = jnp.dot(hidden_got, w_full, preferred_element_type=F32).astype(BF16)
    v_chip = ordered(first, v_own, v_other)
    v_two = chip_shift(v_chip, 2)
    v_one = chip_shift(v_chip, 1)

    term = pl.pallas_call(
        functools.partial(outer_kernel, rows),
        out_shape=struct((hidden.shape[1], kv), BF16),
        in_specs=[SMEM] + [VMEM] * 5,
        out_specs=VMEM,
        scratch_shapes=[pltpu.VMEM((chip_rows, kv), BF16)],
    )(core_arg, hidden, hidden_got, part0, back1, back2)

    term = lax.all_to_all(term.reshape(nx, -1, kv), "x", 0, 0)
    term = jnp.sum(term.astype(F32), axis=0).astype(BF16)
    term = term.reshape(nz, ny, 2 * cut, kv).transpose(1, 0, 2, 3)
    term = lax.all_to_all(term, "y", 0, 0)
    term = jnp.sum(term.astype(F32), axis=0)
    keep = jnp.where(low, term[0], term[1])
    far = lax.ppermute(jnp.where(low, term[1], term[0]), "zh", SWAP)
    term = keep + far
    mine = jnp.where(first, term[:cut], term[cut:])
    theirs = lax.ppermute(jnp.where(first, term[cut:], term[:cut]), "c", SWAP)
    weight_grad = ordered(first, mine, theirs, axis=1)

    output = pl.pallas_call(
        functools.partial(output_kernel, rows),
        out_shape=struct((2, rows, qw), BF16),
        in_specs=[SMEM] + [VMEM] * 4,
        out_specs=VMEM,
        scratch_shapes=[pltpu.VMEM((whole, kv), BF16)],
    )(core_arg, probs, v_two, v_one, v_chip)
    out_got = lax.ppermute(output[1], "c", SWAP)
    attention = ordered(first, output[0], out_got, axis=1)
    return attention, weight_grad


def solution(mesh):
    fine = Mesh(mesh.devices.reshape(*SIZES, mesh.devices.shape[1]), (*GRID, "wt"))
    both = P(GRID, "wt")
    return jax.shard_map(
        per_device,
        mesh=fine,
        in_specs=(P(GRID, None), both, both, both, both, P()),
        out_specs=(both, both),
        check_vma=False,
    )
```

time: 172 us -> 148 us (0.86)
  the two profiles are of different devices: /device:TPU:71 before, /device:TPU:64 now
where the time goes in v2:
time: 148 us; the launch traced here: 147 us
  starting transfers between devices  94.3 us (64%)
  waiting for transfers between devices  20.5 us (14%)
  Pallas kernels  12.2 us (8%)
  other arithmetic  11.4 us (8%)
  local copies, waits for them, and re-layouts  6.44 us (4%)
    all_to_all x1, starting transfers between devices, per_device(): term = lax.all_to_all(term, 'y', 0, 0)  21.3 us
    ppermute x6, starting transfers between devices, chip_shift(): return lax.ppermute(block, CHIPS, route)  16.3 us
    all_to_all x1, starting transfers between devices, per_device(): term = lax.all_to_all(term.reshape(nx, -1, kv), 'x', 0, 0)  15.5 us
    ppermute x1, starting transfers between devices, per_device(): w_far = lax.ppermute(w_chip, 'zh', SWAP)  14.2 us
    ppermute x6, waiting for transfers between devices, chip_shift(): return lax.ppermute(block, CHIPS, route)  10.4 us
    ppermute x1, starting transfers between devices, per_device(): far = lax.ppermute(jnp.where(low, term[1], term[0]), 'zh', SWAP)  8.15 us
    all_to_all x1, starting transfers between devices, per_device(): lax.all_to_all(jnp.broadcast_to(w_pair[None], (ny, *w_pair.shape)), 'y',...  7.1 us
    pallas_call x1, Pallas kernels, per_device(): pl.pallas_call(functools.partial(attend_kernel, rows, factor), out_shape=...  5.47 us
  transfers between devices with their start and end apart: 16, of which 7 were waited for; matrix products, arithmetic and copies ran while one was open for 9% of the time, Pallas kernels for 8%

profile of v2, /device:TPU:64, one launch (start us, length us, event | category | flops | bytes accessed | tf_op | source)
XLA Modules:
  0.0 146.8 jit_solution(6650022483712619642)
XLA Ops:
  3.6 1.9 %collective-permute-start = (bf16[256,768]{1,0:T(8,128)(2,1)S(1)}, bf16[256,768]{1,0:T(8,128)(2,1)}, u32[]{:S(2)}, u32[]{:S(2)}) collective-permute-start(bf16[256,768]{1,0:T(8,128)(2,1)S(1)} %fusion.1), channel_id=1, source_target_pairs={{0,6},{6,0},{1,7},{7,1},{2,8},{8,2},{3,9},{9,3},{4,10},{10,4},{5,1... | collective-permute-start | bytes 1179656 | tf_op jit(solution)/shard_map/ppermute | solution.py:125
  5.5 2.4 %collective-permute-start.4 = (bf16[256,2688]{1,0:T(8,128)(2,1)S(1)}, bf16[256,2688]{1,0:T(8,128)(2,1)S(1)}, u32[]{:S(2)}, u32[]{:S(2)}) collective-permute-start(bf16[256,2688]{1,0:T(8,128)(2,1)S(1)} %copy-done), channel_id=1, source_target_pairs={{0,6},{6,0},{1,7},{7,1},{2,8},{8,2},{3,9},{9,3},{4,10},{10,4},{5,1... | collective-permute-start | bytes 4128776 | tf_op jit(solution)/shard_map/ppermute | solution.py:140
  9.3 14.2 %collective-permute-start.3 = (bf16[42,128]{1,0:T(8,128)(2,1)S(1)}, bf16[42,128]{1,0:T(8,128)(2,1)S(1)}, u32[]{:S(2)}, u32[]{:S(2)}) collective-permute-start(bf16[42,128]{1,0:T(8,128)(2,1)S(1)} %pad_maximum_fusion.7), channel_id=1, source_target_pairs={{0,96},{96,0},{1,97},{97,1},{2,98},{98,2},{3,99},{99,3},{4,100},{1... | collective-permute-start | bytes 32264 | tf_op jit(solution)/shard_map/ppermute | solution.py:133
  26.0 7.1 %all-to-all-start = ((bf16[8,2,42,128]{3,1,2,0:T(2,128)(2,1)}), bf16[8,2,42,128]{3,1,2,0:T(2,128)(2,1)S(1)}, u32[]{:S(2)}, u32[]{:S(2)}) async-start(bf16[8,2,42,128]{3,1,2,0:T(2,128)(2,1)} %broadcast_in_dim.9), calls=%async_computation | async-start | bytes 344064 | tf_op jit(solution)/shard_map/all_to_all | solution.py:135
  34.6 5.5 %collective-permute-start.1 = (bf16[512,128]{1,0:T(8,128)(2,1)}, bf16[512,128]{1,0:T(8,128)(2,1)}, u32[]{:S(2)}, u32[]{:S(2)}) collective-permute-start(bf16[512,128]{1,0:T(8,128)(2,1)} %pad_maximum_fusion.3.k0_ref), channel_id=1, source_target_pairs={{0,24},{12,36},{24,48},{36,60},{48,72},{60,84},{72,96},{84,108},{9... | collective-permute-start | bytes 393224 | tf_op jit(solution)/shard_map/ppermute | solution.py:33
  40.1 4.0 %collective-permute-start.2 = (bf16[512,128]{1,0:T(8,128)(2,1)}, bf16[512,128]{1,0:T(8,128)(2,1)}, u32[]{:S(2)}, u32[]{:S(2)}) collective-permute-start(bf16[512,128]{1,0:T(8,128)(2,1)} %pad_maximum_fusion.3.k0_ref), channel_id=1, source_target_pairs={{0,12},{12,24},{24,36},{36,48},{48,60},{60,72},{72,84},{84,96},{96... | collective-permute-start | bytes 393224 | tf_op jit(solution)/shard_map/ppermute | solution.py:33
  45.2 3.5 %all-to-all-start.1 = ((bf16[4,672,128]{2,1,0:T(8,128)(2,1)}), bf16[4,672,128]{2,1,0:T(8,128)(2,1)S(1)}, u32[]{:S(2)}, u32[]{:S(2)}) async-start(bf16[4,672,128]{2,1,0:T(8,128)(2,1)} %broadcast_in_dim.11), calls=%async_computation.1 | async-start | bytes 1376256 | tf_op jit(solution)/shard_map/all_to_all | solution.py:137
  51.4 5.5 %shard_map.77 = (bf16[2,2,1280,256]{3,2,1,0:T(8,128)(2,1)}, bf16[512,128]{1,0:T(8,128)(2,1)}, bf16[512,128]{1,0:T(8,128)(2,1)}, f32[512,128]{1,0:T(8,128)}) custom-call(bf16[512,256]{1,0:T(8,128)(2,1)} %pad_maximum_fusion.q_ref, bf16[512,128]{1,0:T(8,128)(2,1)} %collective-permute-done.1.k2_ref, bf16[512,128]{1,0:T(8,128)(2,1)} %collective-permute-done.2.k1_ref, ...), custom_call_target="tpu_custom_call" | custom-call | tf_op jit(solution)/shard_map/pallas_call | solution.py:148
  56.8 1.3 collective-permute-start.8
  58.1 1.3 collective-permute-start.9
  59.4 5.9 %collective-permute-done.8.back1_ref = bf16[512,128]{1,0:T(8,128)(2,1)S(1)} collective-permute-done((bf16[512,128]{1,0:T(8,128)(2,1)}, bf16[512,128]{1,0:T(8,128)(2,1)S(1)}, u32[]{:S(2)}, u32[]{:S(2)}) %collective-permute-start.8) | collective-permute-done | bytes 131104 | tf_op jit(solution)/shard_map/ppermute | solution.py:33
  65.3 4.5 %collective-permute-done.9.back2_ref = bf16[512,128]{1,0:T(8,128)(2,1)S(1)} collective-permute-done((bf16[512,128]{1,0:T(8,128)(2,1)}, bf16[512,128]{1,0:T(8,128)(2,1)S(1)}, u32[]{:S(2)}, u32[]{:S(2)}) %collective-permute-start.9) | collective-permute-done | bytes 131104 | tf_op jit(solution)/shard_map/ppermute | solution.py:33
  71.0 3.5 %shard_map.79 = bf16[2688,128]{1,0:T(8,128)(2,1)} custom-call(s32[1]{0:T(128)} %bitcast.core_ref, bf16[256,2688]{1,0:T(8,128)(2,1)} %own_ref.1, bf16[256,2688]{1,0:T(8,128)(2,1)} %copy-done.2, f32[512,128]{1,0:T(8,128)} %get-tuple-element.7.part_ref, bf16[512,128]{1,0:T(8,128)(2,1)} %copy-done.9, bf16[512,128]{1,0:T(8,128)(2,1)} %copy-done.10), custom_call_target="tpu_custom_call" | custom-call | tf_op jit(solution)/shard_map/pallas_call | solution.py:169
  74.5 15.5 %all-to-all-start.2 = ((bf16[4,672,128]{2,1,0:T(8,128)(2,1)}), bf16[4,672,128]{2,1,0:T(8,128)(2,1)S(1)}, u32[]{:S(2)}, u32[]{:S(2)}) async-start(bf16[4,672,128]{2,1,0:T(8,128)(2,1)} %bitcast.34), calls=%async_computation.2 | async-start | bytes 1376256 | tf_op jit(solution)/shard_map/all_to_all | solution.py:177
  91.9 1.3 collective-permute-start.5
  93.2 3.0 %collective-permute-start.6 = (bf16[512,128]{1,0:T(8,128)(2,1)S(1)}, bf16[512,128]{1,0:T(8,128)(2,1)S(1)}, u32[]{:S(2)}, u32[]{:S(2)}) collective-permute-start(bf16[512,128]{1,0:T(8,128)(2,1)S(1)} %pad_maximum_fusion.4.v0_ref), channel_id=1, source_target_pairs={{0,12},{12,24},{24,36},{36,48},{48,60},{60,72},{72,84},{84,96},{96... | collective-permute-start | bytes 393224 | tf_op jit(solution)/shard_map/ppermute | solution.py:33
  96.2 2.8 %all-to-all-done.2 = bf16[4,672,128]{2,1,0:T(8,128)(2,1)S(1)} async-done(((bf16[4,672,128]{2,1,0:T(8,128)(2,1)}), bf16[4,672,128]{2,1,0:T(8,128)(2,1)S(1)}, u32[]{:S(2)}, u32[]{:S(2)}) %all-to-all-start.2) | async-done | bytes 688160 | tf_op jit(solution)/shard_map/all_to_all | solution.py:177
  100.0 21.3 %all-to-all-start.3 = ((bf16[8,2,42,128]{3,1,2,0:T(2,128)(2,1)}), bf16[8,2,42,128]{3,1,2,0:T(2,128)(2,1)S(1)}, u32[]{:S(2)}, u32[]{:S(2)}) async-start(bf16[8,2,42,128]{3,1,2,0:T(2,128)(2,1)} %copy.28), calls=%async_computation.3 | async-start | bytes 344064 | tf_op jit(solution)/shard_map/all_to_all | solution.py:180
  122.1 3.1 %shard_map.78 = bf16[2,256,256]{2,1,0:T(8,128)(2,1)} custom-call(s32[1]{0:T(128)} %bitcast.core_ref, bf16[2,2,1280,256]{3,2,1,0:T(8,128)(2,1)} %get-tuple-element.6.probs_ref, bf16[512,128]{1,0:T(8,128)(2,1)} %copy-done.7, bf16[512,128]{1,0:T(8,128)(2,1)} %copy-done.8, bf16[512,128]{1,0:T(8,128)(2,1)} %copy-done.5), custom_call_target="tpu_custom_call" | custom-call | tf_op jit(solution)/shard_map/pallas_call | solution.py:189
  126.1 1.9 %collective-permute-start.7 = (bf16[256,256]{1,0:T(8,128)(2,1)S(1)}, bf16[256,256]{1,0:T(8,128)(2,1)S(1)}, u32[]{:S(2)}, u32[]{:S(2)}) collective-permute-start(bf16[256,256]{1,0:T(8,128)(2,1)S(1)} %slice_bitcast_fusion), channel_id=1, source_target_pairs={{0,6},{6,0},{1,7},{7,1},{2,8},{8,2},{3,9},{9,3},{4,10},{10,4},{5,1... | collective-permute-start | bytes 393224 | tf_op jit(solution)/shard_map/ppermute | solution.py:196
  128.1 2.8 %all-to-all-done.3 = bf16[8,2,42,128]{3,1,2,0:T(2,128)(2,1)S(1)} async-done(((bf16[8,2,42,128]{3,1,2,0:T(2,128)(2,1)}), bf16[8,2,42,128]{3,1,2,0:T(2,128)(2,1)S(1)}, u32[]{:S(2)}, u32[]{:S(2)}) %all-to-all-start.3) | async-done | bytes 172064 | tf_op jit(solution)/shard_map/all_to_all | solution.py:180
  131.1 8.2 %collective-permute-start.10 = (f32[42,128]{1,0:T(8,128)S(1)}, f32[42,128]{1,0:T(8,128)S(1)}, u32[]{:S(2)}, u32[]{:S(2)}) collective-permute-start(f32[42,128]{1,0:T(8,128)S(1)} %fusion.4), channel_id=1, source_target_pairs={{0,96},{96,0},{1,97},{97,1},{2,98},{98,2},{3,99},{99,3},{4,100},{1... | collective-permute-start | bytes 64520 | tf_op jit(solution)/shard_map/ppermute | solution.py:183
  140.2 2.9 %collective-permute-done.10 = f32[42,128]{1,0:T(8,128)S(1)} collective-permute-done((f32[42,128]{1,0:T(8,128)S(1)}, f32[42,128]{1,0:T(8,128)S(1)}, u32[]{:S(2)}, u32[]{:S(2)}) %collective-permute-start.10) | collective-permute-done | bytes 21536 | tf_op jit(solution)/shard_map/ppermute | solution.py:183
  143.1 1.9 %collective-permute-start.11 = (f32[21,128]{1,0:T(8,128)S(1)}, f32[21,128]{1,0:T(8,128)S(1)}, u32[]{:S(2)}, u32[]{:S(2)}) collective-permute-start(f32[21,128]{1,0:T(8,128)S(1)} %slice_select_fusion), channel_id=1, source_target_pairs={{0,6},{6,0},{1,7},{7,1},{2,8},{8,2},{3,9},{9,3},{4,10},{10,4},{5,1... | collective-permute-start | bytes 32264 | tf_op jit(solution)/shard_map/ppermute | solution.py:186
  (73 shorter events, 20.4 us)
Async XLA Ops:
  0.6 7.9 %copy-start.11 = (bf16[21,256]{1,0:T(8,128)(2,1)S(1)}, bf16[21,256]{1,0:T(8,128)(2,1)}, u32[]{:S(2)}) copy-start(bf16[21,256]{1,0:T(8,128)(2,1)} %param.7) | copy-start | bytes 32260
  0.6 4.9 %copy-start = (bf16[256,2688]{1,0:T(8,128)(2,1)S(1)}, bf16[256,2688]{1,0:T(8,128)(2,1)}, u32[]{:S(2)}) copy-start(bf16[256,2688]{1,0:T(8,128)(2,1)} %own_ref.1) | copy-start | bytes 4128772
  0.7 7.3 %copy-start.6 = (s32[32768]{0:T(1024)S(1)}, s32[32768]{0:T(1024)}, u32[]{:S(2)}) copy-start(s32[32768]{0:T(1024)} %param.11) | copy-start | bytes 393220
  1.5 31.6 %copy-start.4 = (bf16[256,256]{1,0:T(8,128)(2,1)S(1)}, bf16[256,256]{1,0:T(8,128)(2,1)}, u32[]{:S(2)}) copy-start(bf16[256,256]{1,0:T(8,128)(2,1)} %param.9) | copy-start | bytes 393220
  3.6 4.9 %collective-permute-start = (bf16[256,768]{1,0:T(8,128)(2,1)S(1)}, bf16[256,768]{1,0:T(8,128)(2,1)}, u32[]{:S(2)}, u32[]{:S(2)}) collective-permute-start(bf16[256,768]{1,0:T(8,128)(2,1)S(1)} %fusion.1), channel_id=1, source_target_pairs={{0,6},{6,0},{1,7},{7,1},{2,8},{8,2},{3,9},{9,3},{4,10},{10,4},{5,1... | collective-permute-start | bytes 1179656 | tf_op jit(solution)/shard_map/ppermute | solution.py:125
  5.5 64.3 %collective-permute-start.4 = (bf16[256,2688]{1,0:T(8,128)(2,1)S(1)}, bf16[256,2688]{1,0:T(8,128)(2,1)S(1)}, u32[]{:S(2)}, u32[]{:S(2)}) collective-permute-start(bf16[256,2688]{1,0:T(8,128)(2,1)S(1)} %copy-done), channel_id=1, source_target_pairs={{0,6},{6,0},{1,7},{7,1},{2,8},{8,2},{3,9},{9,3},{4,10},{10,4},{5,1... | collective-permute-start | bytes 4128776 | tf_op jit(solution)/shard_map/ppermute | solution.py:140
  9.3 15.9 %collective-permute-start.3 = (bf16[42,128]{1,0:T(8,128)(2,1)S(1)}, bf16[42,128]{1,0:T(8,128)(2,1)S(1)}, u32[]{:S(2)}, u32[]{:S(2)}) collective-permute-start(bf16[42,128]{1,0:T(8,128)(2,1)S(1)} %pad_maximum_fusion.7), channel_id=1, source_target_pairs={{0,96},{96,0},{1,97},{97,1},{2,98},{98,2},{3,99},{99,3},{4,100},{1... | collective-permute-start | bytes 32264 | tf_op jit(solution)/shard_map/ppermute | solution.py:133
  26.0 18.1 %all-to-all-start = ((bf16[8,2,42,128]{3,1,2,0:T(2,128)(2,1)}), bf16[8,2,42,128]{3,1,2,0:T(2,128)(2,1)S(1)}, u32[]{:S(2)}, u32[]{:S(2)}) async-start(bf16[8,2,42,128]{3,1,2,0:T(2,128)(2,1)} %broadcast_in_dim.9), calls=%async_computation | async-start | bytes 344064 | tf_op jit(solution)/shard_map/all_to_all | solution.py:135
  34.6 16.7 %collective-permute-start.1 = (bf16[512,128]{1,0:T(8,128)(2,1)}, bf16[512,128]{1,0:T(8,128)(2,1)}, u32[]{:S(2)}, u32[]{:S(2)}) collective-permute-start(bf16[512,128]{1,0:T(8,128)(2,1)} %pad_maximum_fusion.3.k0_ref), channel_id=1, source_target_pairs={{0,24},{12,36},{24,48},{36,60},{48,72},{60,84},{72,96},{84,108},{9... | collective-permute-start | bytes 393224 | tf_op jit(solution)/shard_map/ppermute | solution.py:33
  40.1 11.3 %collective-permute-start.2 = (bf16[512,128]{1,0:T(8,128)(2,1)}, bf16[512,128]{1,0:T(8,128)(2,1)}, u32[]{:S(2)}, u32[]{:S(2)}) collective-permute-start(bf16[512,128]{1,0:T(8,128)(2,1)} %pad_maximum_fusion.3.k0_ref), channel_id=1, source_target_pairs={{0,12},{12,24},{24,36},{36,48},{48,60},{60,72},{72,84},{84,96},{96... | collective-permute-start | bytes 393224 | tf_op jit(solution)/shard_map/ppermute | solution.py:33
  45.2 29.4 %all-to-all-start.1 = ((bf16[4,672,128]{2,1,0:T(8,128)(2,1)}), bf16[4,672,128]{2,1,0:T(8,128)(2,1)S(1)}, u32[]{:S(2)}, u32[]{:S(2)}) async-start(bf16[4,672,128]{2,1,0:T(8,128)(2,1)} %broadcast_in_dim.11), calls=%async_computation.1 | async-start | bytes 1376256 | tf_op jit(solution)/shard_map/all_to_all | solution.py:137
  56.8 8.5 %collective-permute-start.8 = (bf16[512,128]{1,0:T(8,128)(2,1)}, bf16[512,128]{1,0:T(8,128)(2,1)S(1)}, u32[]{:S(2)}, u32[]{:S(2)}) collective-permute-start(bf16[512,128]{1,0:T(8,128)(2,1)} %get-tuple-element.8), channel_id=1, source_target_pairs={{12,0},{24,12},{36,24},{48,36},{60,48},{72,60},{84,72},{96,84},{10... | collective-permute-start | bytes 393224 | tf_op jit(solution)/shard_map/ppermute | solution.py:33
  58.1 11.7 %collective-permute-start.9 = (bf16[512,128]{1,0:T(8,128)(2,1)}, bf16[512,128]{1,0:T(8,128)(2,1)S(1)}, u32[]{:S(2)}, u32[]{:S(2)}) collective-permute-start(bf16[512,128]{1,0:T(8,128)(2,1)} %get-tuple-element.9), channel_id=1, source_target_pairs={{24,0},{36,12},{48,24},{60,36},{72,48},{84,60},{96,72},{108,84},{1... | collective-permute-start | bytes 393224 | tf_op jit(solution)/shard_map/ppermute | solution.py:33
  65.3 4.5 %copy-start.9 = (bf16[512,128]{1,0:T(8,128)(2,1)}, bf16[512,128]{1,0:T(8,128)(2,1)S(1)}, u32[]{:S(2)}) copy-start(bf16[512,128]{1,0:T(8,128)(2,1)S(1)} %collective-permute-done.8.back1_ref) | copy-start | bytes 393220
  74.5 15.5 %copy-start.1 = (bf16[256,2688]{1,0:T(8,128)(2,1)S(1)}, bf16[256,2688]{1,0:T(8,128)(2,1)}, u32[]{:S(2)}) copy-start(bf16[256,2688]{1,0:T(8,128)(2,1)} %own_ref.1) | copy-start | bytes 4128772
  74.5 24.5 %all-to-all-start.2 = ((bf16[4,672,128]{2,1,0:T(8,128)(2,1)}), bf16[4,672,128]{2,1,0:T(8,128)(2,1)S(1)}, u32[]{:S(2)}, u32[]{:S(2)}) async-start(bf16[4,672,128]{2,1,0:T(8,128)(2,1)} %bitcast.34), calls=%async_computation.2 | async-start | bytes 1376256 | tf_op jit(solution)/shard_map/all_to_all | solution.py:177
  90.0 1.3 copy-start.3
  91.9 29.5 %copy-start.5 = (bf16[512,128]{1,0:T(8,128)(2,1)}, bf16[512,128]{1,0:T(8,128)(2,1)S(1)}, u32[]{:S(2)}) copy-start(bf16[512,128]{1,0:T(8,128)(2,1)S(1)} %pad_maximum_fusion.4.v0_ref) | copy-start | bytes 393220
  91.9 29.4 %collective-permute-start.5 = (bf16[512,128]{1,0:T(8,128)(2,1)S(1)}, bf16[512,128]{1,0:T(8,128)(2,1)S(1)}, u32[]{:S(2)}, u32[]{:S(2)}) collective-permute-start(bf16[512,128]{1,0:T(8,128)(2,1)S(1)} %pad_maximum_fusion.4.v0_ref), channel_id=1, source_target_pairs={{0,24},{12,36},{24,48},{36,60},{48,72},{60,84},{72,96},{84,108},{9... | collective-permute-start | bytes 393224 | tf_op jit(solution)/shard_map/ppermute | solution.py:33
  93.2 28.1 %collective-permute-start.6 = (bf16[512,128]{1,0:T(8,128)(2,1)S(1)}, bf16[512,128]{1,0:T(8,128)(2,1)S(1)}, u32[]{:S(2)}, u32[]{:S(2)}) collective-permute-start(bf16[512,128]{1,0:T(8,128)(2,1)S(1)} %pad_maximum_fusion.4.v0_ref), channel_id=1, source_target_pairs={{0,12},{12,24},{24,36},{36,48},{48,60},{60,72},{72,84},{84,96},{96... | collective-permute-start | bytes 393224 | tf_op jit(solution)/shard_map/ppermute | solution.py:33
  100.0 30.8 %all-to-all-start.3 = ((bf16[8,2,42,128]{3,1,2,0:T(2,128)(2,1)}), bf16[8,2,42,128]{3,1,2,0:T(2,128)(2,1)S(1)}, u32[]{:S(2)}, u32[]{:S(2)}) async-start(bf16[8,2,42,128]{3,1,2,0:T(2,128)(2,1)} %copy.28), calls=%async_computation.3 | async-start | bytes 344064 | tf_op jit(solution)/shard_map/all_to_all | solution.py:180
  126.1 13.1 %collective-permute-start.7 = (bf16[256,256]{1,0:T(8,128)(2,1)S(1)}, bf16[256,256]{1,0:T(8,128)(2,1)S(1)}, u32[]{:S(2)}, u32[]{:S(2)}) collective-permute-start(bf16[256,256]{1,0:T(8,128)(2,1)S(1)} %slice_bitcast_fusion), channel_id=1, source_target_pairs={{0,6},{6,0},{1,7},{7,1},{2,8},{8,2},{3,9},{9,3},{4,10},{10,4},{5,1... | collective-permute-start | bytes 393224 | tf_op jit(solution)/shard_map/ppermute | solution.py:196
  131.1 12.0 %collective-permute-start.10 = (f32[42,128]{1,0:T(8,128)S(1)}, f32[42,128]{1,0:T(8,128)S(1)}, u32[]{:S(2)}, u32[]{:S(2)}) collective-permute-start(f32[42,128]{1,0:T(8,128)S(1)} %fusion.4), channel_id=1, source_target_pairs={{0,96},{96,0},{1,97},{97,1},{2,98},{98,2},{3,99},{99,3},{4,100},{1... | collective-permute-start | bytes 64520 | tf_op jit(solution)/shard_map/ppermute | solution.py:183
  143.1 3.1 %collective-permute-start.11 = (f32[21,128]{1,0:T(8,128)S(1)}, f32[21,128]{1,0:T(8,128)S(1)}, u32[]{:S(2)}, u32[]{:S(2)}) collective-permute-start(f32[21,128]{1,0:T(8,128)S(1)} %slice_select_fusion), channel_id=1, source_target_pairs={{0,6},{6,0},{1,7},{7,1},{2,8},{8,2},{3,9},{9,3},{4,10},{10,4},{5,1... | collective-permute-start | bytes 32264 | tf_op jit(solution)/shard_map/ppermute | solution.py:186
  (4 other events, 3.1 us)

commit v3 on v2

--- a/solution.py
+++ b/solution.py
@@ -39,31 +39,54 @@
     )
 
 
-def attend_kernel(rows, factor, q_ref, k2_ref, k1_ref, k0_ref, g_ref, low_ref, *rest):
-    probs_ref, part2_ref, part1_ref, part0_ref, win, total = rest
+def prepare_kernel(core_ref, k_ref, q_ref, g_ref, w_ref, out_ref):
+    other = 1 - core_ref[0]
+    at = 0
+    for ref in (k_ref, q_ref, g_ref, w_ref):
+        width = ref.shape[1] // 2
+        out_ref[: ref.shape[0], at : at + width] = ref[:, part_of(other, width)]
+        at += width
+    out_ref[w_ref.shape[0] :, at - width :] = jnp.zeros(
+        (out_ref.shape[0] - w_ref.shape[0], width), out_ref.dtype
+    )
+
+
+def part_of(index, size):
+    return pl.ds(pl.multiple_of(index * size, size), size)
+
+
+def attend_kernel(rows, factor, core_ref, *refs):
+    k_ref, q_ref, g_ref, got_ref, k2_ref, k1_ref, low_ref = refs[:7]
+    probs_ref, part2_ref, part1_ref, part0_ref, win, total = refs[7:]
     chip_rows = 2 * rows
     span = win.shape[0] - rows
-    group = q_ref.shape[1] // HD
-    for i, ref in enumerate((k2_ref, k1_ref, k0_ref)):
-        win[i * chip_rows : (i + 1) * chip_rows] = ref[...]
-    total[span:] = jnp.zeros((rows, HD), F32)
-    for j in range(2):
-        at = slice(j * rows, j * rows + span)
+    kv, qw = k_ref.shape[1] // 2, q_ref.shape[1] // 2
+    core = core_ref[0]
+    win[:chip_rows] = k2_ref[...]
+    win[chip_rows : 2 * chip_rows] = k1_ref[...]
+    home = win.at[2 * chip_rows :]
+    home[part_of(core, rows)] = k_ref[:, part_of(core, kv)]
+    home[part_of(1 - core, rows)] = got_ref[:, :kv]
+    total[...] = jnp.zeros_like(total)
+    u = lax.broadcasted_iota(jnp.int32, (span, rows), 0)
+    t = lax.broadcasted_iota(jnp.int32, (span, rows), 1) + (span - rows)
+    for slot in range(2):
+        j = core if slot == 0 else 1 - core
+        at = pl.ds(pl.multiple_of(j * rows, rows), span)
         keys = win[at]
-        u = lax.broadcasted_iota(jnp.int32, (span, rows), 0) + j * rows
-        t = lax.broadcasted_iota(jnp.int32, (span, rows), 1) + (2 * chip_rows + j * rows)
-        allowed = (u <= t) & (u >= low_ref[:, j * rows : (j + 1) * rows])
-        for h in range(group):
-            tile = (slice(j * rows, (j + 1) * rows), slice(h * HD, (h + 1) * HD))
-            s = jnp.where(allowed, dot(keys, q_ref[tile], 1, 1), -1e30)
+        allowed = (u <= t) & (u >= low_ref[slot : slot + 1])
+        for h in range(qw // HD):
+            if slot == 0:
+                q = q_ref[:, part_of(core * (qw // HD) + h, HD)]
+                g = g_ref[:, part_of(core * (qw // HD) + h, HD)]
+            else:
+                q = got_ref[:, kv + h * HD : kv + (h + 1) * HD]
+                g = got_ref[:, kv + qw + h * HD : kv + qw + (h + 1) * HD]
+            s = jnp.where(allowed, dot(keys, q, 1, 1), -1e30)
             w = jnp.exp2((s - jnp.max(s, axis=0, keepdims=True)) * factor)
             p = (w * (1.0 / jnp.sum(w, axis=0, keepdims=True))).astype(BF16)
-            probs_ref[j, h] = p
-            part = jnp.dot(p, g_ref[tile], preferred_element_type=F32)
-            if j == 0 and h == 0:
-                total[at] = part
-            else:
-                total[at] += part
+            probs_ref[slot, h] = p
+            total[at] += dot(p, g, 1, 0)
     part2_ref[...] = total[:chip_rows].astype(BF16)
     part1_ref[...] = total[chip_rows : 2 * chip_rows].astype(BF16)
     part0_ref[...] = total[2 * chip_rows :]
@@ -74,11 +97,11 @@
     span = win.shape[0] - rows
     for i, ref in enumerate((v2_ref, v1_ref, v0_ref)):
         win[i * chip_rows : (i + 1) * chip_rows] = ref[...]
-    for j in range(2):
-        slot = core_ref[0] if j == 0 else 1 - core_ref[0]
-        values = win[j * rows : j * rows + span]
+    for slot in range(2):
+        j = core_ref[0] if slot == 0 else 1 - core_ref[0]
+        values = win[pl.ds(pl.multiple_of(j * rows, rows), span)]
         for h in range(probs_ref.shape[1]):
-            o = dot(values, probs_ref[j, h], 0, 0)
+            o = dot(values, probs_ref[slot, h], 0, 0)
             out_ref[slot, :, h * HD : (h + 1) * HD] = o.T.astype(BF16)
 
 
@@ -111,25 +134,22 @@
     whole = span + rows
     core_arg = core.astype(jnp.int32)[None]
 
-    def halves(a):
+    def mine_of(a):
         w = a.shape[1] // 2
-        return jnp.where(first, a[:, :w], a[:, w:]), jnp.where(first, a[:, w:], a[:, :w])
-
-    k_own, k_send = halves(keys)
-    q_own, q_send = halves(queries)
-    g_own, g_send = halves(grads)
-    w_own, w_send = halves(weight)
-    tall = ((0, rows - cut), (0, 0))
-
-    send = jnp.concatenate([k_send, q_send, g_send, jnp.pad(w_send, tall)], axis=1)
+        return jnp.where(first, a[:, :w], a[:, w:])
+
+    send = pl.pallas_call(
+        prepare_kernel,
+        out_shape=struct((rows, 2 * kv + 2 * qw), BF16),
+        in_specs=[SMEM] + [VMEM] * 4,
+        out_specs=VMEM,
+    )(core_arg, keys, queries, grads, weight)
     got = lax.ppermute(send, "c", SWAP)
-    k_chip = ordered(first, k_own, got[:, :kv])
+    k_chip = ordered(first, mine_of(keys), got[:, :kv])
     k_two = chip_shift(k_chip, 2)
     k_one = chip_shift(k_chip, 1)
-    q_chip = ordered(first, q_own, got[:, kv : kv + qw])
-    g_chip = ordered(first, g_own, got[:, kv + qw : kv + 2 * qw])
-
-    w_chip = ordered(first, w_own, got[:cut, kv + 2 * qw :])
+
+    w_chip = ordered(first, mine_of(weight), got[:cut, kv + 2 * qw :])
     w_far = lax.ppermute(w_chip, "zh", SWAP)
     w_pair = ordered(low, w_chip[None], w_far[None])
     w_y = lax.all_to_all(jnp.broadcast_to(w_pair[None], (ny, *w_pair.shape)), "y", 0, 0)
@@ -143,7 +163,9 @@
     padded = jnp.concatenate([jnp.full((padding,), -1, jnp.int32), segments], axis=0)
     seg_win = lax.dynamic_slice_in_dim(padded, chip * chip_rows, whole, 0)
     begin = jnp.sum((seg_win[:, None] < seg_win[None, padding:]).astype(jnp.int32), axis=0)
-    begin = jnp.maximum(begin, jnp.arange(chip_rows, dtype=jnp.int32) + (padding - WINDOW + 1))
+    begin = begin.reshape(2, rows) - rows * jnp.arange(2, dtype=jnp.int32)[:, None]
+    begin = jnp.maximum(begin, jnp.arange(1, rows + 1, dtype=jnp.int32)[None])
+    begin = jnp.where(first, begin, begin[::-1])
 
     probs, part2, part1, part0 = pl.pallas_call(
         functools.partial(attend_kernel, rows, factor),
@@ -153,10 +175,10 @@
             struct((chip_rows, kv), BF16),
             struct((chip_rows, kv), F32),
         ),
-        in_specs=[VMEM] * 6,
+        in_specs=[SMEM] + [VMEM] * 7,
         out_specs=[VMEM] * 4,
         scratch_shapes=[pltpu.VMEM((whole, kv), BF16), pltpu.VMEM((whole, kv), F32)],
-    )(q_chip, k_two, k_one, k_chip, g_chip, begin[None])
+    )(core_arg, keys, queries, grads, got, k_two, k_one, begin)
     back2 = chip_shift(part2, -2)
     back1 = chip_shift(part1, -1)
 
@@ -176,15 +198,9 @@
 
     term = lax.all_to_all(term.reshape(nx, -1, kv), "x", 0, 0)
     term = jnp.sum(term.astype(F32), axis=0).astype(BF16)
-    term = term.reshape(nz, ny, 2 * cut, kv).transpose(1, 0, 2, 3)
-    term = lax.all_to_all(term, "y", 0, 0)
-    term = jnp.sum(term.astype(F32), axis=0)
-    keep = jnp.where(low, term[0], term[1])
-    far = lax.ppermute(jnp.where(low, term[1], term[0]), "zh", SWAP)
-    term = keep + far
-    mine = jnp.where(first, term[:cut], term[cut:])
-    theirs = lax.ppermute(jnp.where(first, term[cut:], term[:cut]), "c", SWAP)
-    weight_grad = ordered(first, mine, theirs, axis=1)
+    term = lax.all_to_all(term.reshape(nz * ny * 2, cut, kv), ("zh", "y", "c"), 0, 0)
+    term = jnp.sum(term.astype(F32).reshape(nz * ny, 2, cut, kv), axis=0)
+    weight_grad = jnp.concatenate([term[0], term[1]], axis=1)
 
     output = pl.pallas_call(
         functools.partial(output_kernel, rows),

time: 148 us -> 163 us (1.10)
  the two profiles are of different devices: /device:TPU:64 before, /device:TPU:67 now
where the time goes in v3:
time: 163 us; the launch traced here: 162 us
  waiting for transfers between devices  70.9 us (43%)
  starting transfers between devices  64.9 us (40%)
  Pallas kernels  14.3 us (9%)
  local copies, waits for them, and re-layouts  5.94 us (4%)
  other arithmetic  3.62 us (2%)
    ppermute x6, waiting for transfers between devices, chip_shift(): return lax.ppermute(block, CHIPS, route)  46.2 us
    all_to_all x1, waiting for transfers between devices, per_device(): lax.all_to_all(term.reshape(nz * ny * 2, cut, kv), ('zh', 'y', 'c'), 0, 0)  14.3 us
    ppermute x1, starting transfers between devices, per_device(): w_far = lax.ppermute(w_chip, 'zh', SWAP)  14 us
    ppermute x6, starting transfers between devices, chip_shift(): return lax.ppermute(block, CHIPS, route)  11.9 us
    all_to_all x1, starting transfers between devices, per_device(): lax.all_to_all(term.reshape(nz * ny * 2, cut, kv), ('zh', 'y', 'c'), 0, 0)  10.7 us
    all_to_all x1, starting transfers between devices, per_device(): term = lax.all_to_all(term.reshape(nx, -1, kv), 'x', 0, 0)  10.5 us
    all_to_all x1, waiting for transfers between devices, per_device(): lax.all_to_all(jnp.broadcast_to(w_pair[None], (ny, *w_pair.shape)), 'y',...  8.33 us
    all_to_all x1, starting transfers between devices, per_device(): lax.all_to_all(jnp.broadcast_to(w_pair[None], (ny, *w_pair.shape)), 'y',...  6.82 us
  transfers between devices with their start and end apart: 14, of which 10 were waited for; matrix products, arithmetic and copies ran while one was open for 5% of the time, Pallas kernels for 5%

profile of v3, /device:TPU:67, one launch (start us, length us, event | category | flops | bytes accessed | tf_op | source)
XLA Modules:
  0.0 161.7 jit_solution(3544959510412492120)
XLA Ops:
  2.5 2.6 %collective-permute-start = (bf16[256,768]{1,0:T(8,128)(2,1)}, bf16[256,768]{1,0:T(8,128)(2,1)S(1)}, u32[]{:S(2)}, u32[]{:S(2)}) collective-permute-start(bf16[256,768]{1,0:T(8,128)(2,1)} %shard_map.77), channel_id=1, source_target_pairs={{0,6},{6,0},{1,7},{7,1},{2,8},{8,2},{3,9},{9,3},{4,10},{10,4},{5,1... | collective-permute-start | bytes 1179656 | tf_op jit(solution)/shard_map/ppermute | solution.py:147
  5.1 1.9 %collective-permute-start.4 = (bf16[256,2688]{1,0:T(8,128)(2,1)}, bf16[256,2688]{1,0:T(8,128)(2,1)S(1)}, u32[]{:S(2)}, u32[]{:S(2)}) collective-permute-start(bf16[256,2688]{1,0:T(8,128)(2,1)} %own_ref.1), channel_id=1, source_target_pairs={{0,6},{6,0},{1,7},{7,1},{2,8},{8,2},{3,9},{9,3},{4,10},{10,4},{5,1... | collective-permute-start | bytes 4128776 | tf_op jit(solution)/shard_map/ppermute | solution.py:160
  9.0 14.0 %collective-permute-start.3 = (bf16[42,128]{1,0:T(8,128)(2,1)S(1)}, bf16[42,128]{1,0:T(8,128)(2,1)S(1)}, u32[]{:S(2)}, u32[]{:S(2)}) collective-permute-start(bf16[42,128]{1,0:T(8,128)(2,1)S(1)} %pad_maximum_fusion.5), channel_id=1, source_target_pairs={{0,96},{96,0},{1,97},{97,1},{2,98},{98,2},{3,99},{99,3},{4,100},{1... | collective-permute-start | bytes 32264 | tf_op jit(solution)/shard_map/ppermute | solution.py:153
  24.9 6.8 %all-to-all-start = ((bf16[8,2,42,128]{3,1,2,0:T(2,128)(2,1)}), bf16[8,2,42,128]{3,1,2,0:T(2,128)(2,1)S(1)}, u32[]{:S(2)}, u32[]{:S(2)}) async-start(bf16[8,2,42,128]{3,1,2,0:T(2,128)(2,1)} %broadcast_in_dim.9), calls=%async_computation | async-start | bytes 344064 | tf_op jit(solution)/shard_map/all_to_all | solution.py:155
  31.9 8.3 %all-to-all-done = bf16[8,2,42,128]{3,1,2,0:T(2,128)(2,1)S(1)} async-done(((bf16[8,2,42,128]{3,1,2,0:T(2,128)(2,1)}), bf16[8,2,42,128]{3,1,2,0:T(2,128)(2,1)S(1)}, u32[]{:S(2)}, u32[]{:S(2)}) %all-to-all-start) | async-done | bytes 172064 | tf_op jit(solution)/shard_map/all_to_all | solution.py:155
  41.2 4.4 %all-to-all-start.1 = ((bf16[4,672,128]{2,1,0:T(8,128)(2,1)}), bf16[4,672,128]{2,1,0:T(8,128)(2,1)S(1)}, u32[]{:S(2)}, u32[]{:S(2)}) async-start(bf16[4,672,128]{2,1,0:T(8,128)(2,1)} %broadcast_in_dim.11), calls=%async_computation.1 | async-start | bytes 1376256 | tf_op jit(solution)/shard_map/all_to_all | solution.py:157
  46.6 1.9 %collective-permute-start.1 = (bf16[512,128]{1,0:T(8,128)(2,1)S(1)}, bf16[512,128]{1,0:T(8,128)(2,1)}, u32[]{:S(2)}, u32[]{:S(2)}) collective-permute-start(bf16[512,128]{1,0:T(8,128)(2,1)S(1)} %pad_maximum_fusion.1), channel_id=1, source_target_pairs={{0,24},{12,36},{24,48},{36,60},{48,72},{60,84},{72,96},{84,108},{9... | collective-permute-start | bytes 393224 | tf_op jit(solution)/shard_map/ppermute | solution.py:33
  48.5 2.3 %collective-permute-start.2 = (bf16[512,128]{1,0:T(8,128)(2,1)S(1)}, bf16[512,128]{1,0:T(8,128)(2,1)}, u32[]{:S(2)}, u32[]{:S(2)}) collective-permute-start(bf16[512,128]{1,0:T(8,128)(2,1)S(1)} %pad_maximum_fusion.1), channel_id=1, source_target_pairs={{0,12},{12,24},{24,36},{36,48},{48,60},{60,72},{72,84},{84,96},{96... | collective-permute-start | bytes 393224 | tf_op jit(solution)/shard_map/ppermute | solution.py:33
  51.5 11.6 %collective-permute-done.1.refs_4_ = bf16[512,128]{1,0:T(8,128)(2,1)} collective-permute-done((bf16[512,128]{1,0:T(8,128)(2,1)S(1)}, bf16[512,128]{1,0:T(8,128)(2,1)}, u32[]{:S(2)}, u32[]{:S(2)}) %collective-permute-start.1) | collective-permute-done | bytes 131104 | tf_op jit(solution)/shard_map/ppermute | solution.py:33
  63.1 6.3 %collective-permute-done.2.refs_5_ = bf16[512,128]{1,0:T(8,128)(2,1)} collective-permute-done((bf16[512,128]{1,0:T(8,128)(2,1)S(1)}, bf16[512,128]{1,0:T(8,128)(2,1)}, u32[]{:S(2)}, u32[]{:S(2)}) %collective-permute-start.2) | collective-permute-done | bytes 131104 | tf_op jit(solution)/shard_map/ppermute | solution.py:33
  69.3 5.7 %shard_map.78 = (bf16[2,2,1280,256]{3,2,1,0:T(8,128)(2,1)}, bf16[512,128]{1,0:T(8,128)(2,1)}, bf16[512,128]{1,0:T(8,128)(2,1)}, f32[512,128]{1,0:T(8,128)}) custom-call(s32[1]{0:T(128)} %bitcast.core_ref, bf16[256,256]{1,0:T(8,128)(2,1)} %refs_0_.1, bf16[256,512]{1,0:T(8,128)(2,1)} %refs_1_.1, bf16[256,512]{1,0:T(8,128)(2,1)} %refs_2_.1, ...), custom_call_target="tpu_custom_call" | custom-call | tf_op jit(solution)/shard_map/pallas_call | solution.py:170
  75.1 1.9 %collective-permute-start.8 = (bf16[512,128]{1,0:T(8,128)(2,1)}, bf16[512,128]{1,0:T(8,128)(2,1)}, u32[]{:S(2)}, u32[]{:S(2)}) collective-permute-start(bf16[512,128]{1,0:T(8,128)(2,1)} %get-tuple-element.8), channel_id=1, source_target_pairs={{12,0},{24,12},{36,24},{48,36},{60,48},{72,60},{84,72},{96,84},{10... | collective-permute-start | bytes 393224 | tf_op jit(solution)/shard_map/ppermute | solution.py:33
  77.0 1.9 %collective-permute-start.9 = (bf16[512,128]{1,0:T(8,128)(2,1)}, bf16[512,128]{1,0:T(8,128)(2,1)}, u32[]{:S(2)}, u32[]{:S(2)}) collective-permute-start(bf16[512,128]{1,0:T(8,128)(2,1)} %get-tuple-element.9), channel_id=1, source_target_pairs={{24,0},{36,12},{48,24},{60,36},{72,48},{84,60},{96,72},{108,84},{1... | collective-permute-start | bytes 393224 | tf_op jit(solution)/shard_map/ppermute | solution.py:33
  81.1 7.3 %collective-permute-done.9.back2_ref = bf16[512,128]{1,0:T(8,128)(2,1)} collective-permute-done((bf16[512,128]{1,0:T(8,128)(2,1)}, bf16[512,128]{1,0:T(8,128)(2,1)}, u32[]{:S(2)}, u32[]{:S(2)}) %collective-permute-start.9) | collective-permute-done | bytes 131104 | tf_op jit(solution)/shard_map/ppermute | solution.py:33
  89.5 3.5 %shard_map.80 = bf16[2688,128]{1,0:T(8,128)(2,1)} custom-call(s32[1]{0:T(128)} %bitcast.core_ref, bf16[256,2688]{1,0:T(8,128)(2,1)} %own_ref.1, bf16[256,2688]{1,0:T(8,128)(2,1)} %copy-done.1, f32[512,128]{1,0:T(8,128)} %get-tuple-element.7.part_ref, bf16[512,128]{1,0:T(8,128)(2,1)} %collective-permute-done.8.back1_ref, ...), custom_call_target="tpu_custom_call" | custom-call | tf_op jit(solution)/shard_map/pallas_call | solution.py:191
  93.0 10.5 %all-to-all-start.2 = ((bf16[4,672,128]{2,1,0:T(8,128)(2,1)}), bf16[4,672,128]{2,1,0:T(8,128)(2,1)S(1)}, u32[]{:S(2)}, u32[]{:S(2)}) async-start(bf16[4,672,128]{2,1,0:T(8,128)(2,1)} %bitcast.32), calls=%async_computation.2 | async-start | bytes 1376256 | tf_op jit(solution)/shard_map/all_to_all | solution.py:199
  104.1 1.9 %collective-permute-start.5 = (bf16[512,128]{1,0:T(8,128)(2,1)S(1)}, bf16[512,128]{1,0:T(8,128)(2,1)S(1)}, u32[]{:S(2)}, u32[]{:S(2)}) collective-permute-start(bf16[512,128]{1,0:T(8,128)(2,1)S(1)} %pad_maximum_fusion.2.v0_ref), channel_id=1, source_target_pairs={{0,24},{12,36},{24,48},{36,60},{48,72},{60,84},{72,96},{84,108},{9... | collective-permute-start | bytes 393224 | tf_op jit(solution)/shard_map/ppermute | solution.py:33
  106.0 1.9 %collective-permute-start.6 = (bf16[512,128]{1,0:T(8,128)(2,1)S(1)}, bf16[512,128]{1,0:T(8,128)(2,1)S(1)}, u32[]{:S(2)}, u32[]{:S(2)}) collective-permute-start(bf16[512,128]{1,0:T(8,128)(2,1)S(1)} %pad_maximum_fusion.2.v0_ref), channel_id=1, source_target_pairs={{0,12},{12,24},{24,36},{36,48},{48,60},{60,72},{72,84},{84,96},{96... | collective-permute-start | bytes 393224 | tf_op jit(solution)/shard_map/ppermute | solution.py:33
  107.9 13.8 %collective-permute-done.5.v2_ref = bf16[512,128]{1,0:T(8,128)(2,1)S(1)} collective-permute-done((bf16[512,128]{1,0:T(8,128)(2,1)S(1)}, bf16[512,128]{1,0:T(8,128)(2,1)S(1)}, u32[]{:S(2)}, u32[]{:S(2)}) %collective-permute-start.5) | collective-permute-done | bytes 131104 | tf_op jit(solution)/shard_map/ppermute | solution.py:33
  121.8 5.5 %collective-permute-done.6.v1_ref = bf16[512,128]{1,0:T(8,128)(2,1)S(1)} collective-permute-done((bf16[512,128]{1,0:T(8,128)(2,1)S(1)}, bf16[512,128]{1,0:T(8,128)(2,1)S(1)}, u32[]{:S(2)}, u32[]{:S(2)}) %collective-permute-start.6) | collective-permute-done | bytes 131104 | tf_op jit(solution)/shard_map/ppermute | solution.py:33
  128.0 3.2 %shard_map.79 = bf16[2,256,256]{2,1,0:T(8,128)(2,1)} custom-call(s32[1]{0:T(128)} %bitcast.core_ref, bf16[2,2,1280,256]{3,2,1,0:T(8,128)(2,1)} %get-tuple-element.6.probs_ref, bf16[512,128]{1,0:T(8,128)(2,1)} %copy-done.6, bf16[512,128]{1,0:T(8,128)(2,1)} %copy-done.7, bf16[512,128]{1,0:T(8,128)(2,1)} %copy-done.5), custom_call_target="tpu_custom_call" | custom-call | tf_op jit(solution)/shard_map/pallas_call | solution.py:205
  132.0 10.7 %all-to-all-start.3 = ((bf16[32,21,128]{2,1,0:T(8,128)(2,1)}), bf16[32,21,128]{2,1,0:T(8,128)(2,1)S(1)}, u32[]{:S(2)}, u32[]{:S(2)}) async-start(bf16[32,21,128]{2,1,0:T(8,128)(2,1)} %reshape.40), calls=%async_computation.3 | async-start | bytes 393216 | tf_op jit(solution)/shard_map/all_to_all | solution.py:201
  142.7 2.1 %collective-permute-start.7 = (bf16[256,256]{1,0:T(8,128)(2,1)S(1)}, bf16[256,256]{1,0:T(8,128)(2,1)S(1)}, u32[]{:S(2)}, u32[]{:S(2)}) collective-permute-start(bf16[256,256]{1,0:T(8,128)(2,1)S(1)} %slice_bitcast_fusion), channel_id=1, source_target_pairs={{0,6},{6,0},{1,7},{7,1},{2,8},{8,2},{3,9},{9,3},{4,10},{10,4},{5,1... | collective-permute-start | bytes 393224 | tf_op jit(solution)/shard_map/ppermute | solution.py:212
  146.7 14.3 %all-to-all-done.3 = bf16[32,21,128]{2,1,0:T(8,128)(2,1)S(1)} async-done(((bf16[32,21,128]{2,1,0:T(8,128)(2,1)}), bf16[32,21,128]{2,1,0:T(8,128)(2,1)S(1)}, u32[]{:S(2)}, u32[]{:S(2)}) %all-to-all-start.3) | async-done | bytes 172064 | tf_op jit(solution)/shard_map/all_to_all | solution.py:201
  (57 shorter events, 16.2 us)
Async XLA Ops:
  0.6 8.4 %copy-start.8 = (bf16[21,256]{1,0:T(8,128)(2,1)S(1)}, bf16[21,256]{1,0:T(8,128)(2,1)}, u32[]{:S(2)}) copy-start(bf16[21,256]{1,0:T(8,128)(2,1)} %w_ref.1) | copy-start | bytes 32260
  2.5 6.5 %collective-permute-start = (bf16[256,768]{1,0:T(8,128)(2,1)}, bf16[256,768]{1,0:T(8,128)(2,1)S(1)}, u32[]{:S(2)}, u32[]{:S(2)}) collective-permute-start(bf16[256,768]{1,0:T(8,128)(2,1)} %shard_map.77), channel_id=1, source_target_pairs={{0,6},{6,0},{1,7},{7,1},{2,8},{8,2},{3,9},{9,3},{4,10},{10,4},{5,1... | collective-permute-start | bytes 1179656 | tf_op jit(solution)/shard_map/ppermute | solution.py:147
  5.1 83.3 %collective-permute-start.4 = (bf16[256,2688]{1,0:T(8,128)(2,1)}, bf16[256,2688]{1,0:T(8,128)(2,1)S(1)}, u32[]{:S(2)}, u32[]{:S(2)}) collective-permute-start(bf16[256,2688]{1,0:T(8,128)(2,1)} %own_ref.1), channel_id=1, source_target_pairs={{0,6},{6,0},{1,7},{7,1},{2,8},{8,2},{3,9},{9,3},{4,10},{10,4},{5,1... | collective-permute-start | bytes 4128776 | tf_op jit(solution)/shard_map/ppermute | solution.py:160
  9.0 15.9 %copy-start.4 = (bf16[256,768]{1,0:T(8,128)(2,1)}, bf16[256,768]{1,0:T(8,128)(2,1)S(1)}, u32[]{:S(2)}) copy-start(bf16[256,768]{1,0:T(8,128)(2,1)S(1)} %collective-permute-done.refs_3_) | copy-start | bytes 1179652
  9.0 15.0 %collective-permute-start.3 = (bf16[42,128]{1,0:T(8,128)(2,1)S(1)}, bf16[42,128]{1,0:T(8,128)(2,1)S(1)}, u32[]{:S(2)}, u32[]{:S(2)}) collective-permute-start(bf16[42,128]{1,0:T(8,128)(2,1)S(1)} %pad_maximum_fusion.5), channel_id=1, source_target_pairs={{0,96},{96,0},{1,97},{97,1},{2,98},{98,2},{3,99},{99,3},{4,100},{1... | collective-permute-start | bytes 32264 | tf_op jit(solution)/shard_map/ppermute | solution.py:153
  24.9 15.3 %all-to-all-start = ((bf16[8,2,42,128]{3,1,2,0:T(2,128)(2,1)}), bf16[8,2,42,128]{3,1,2,0:T(2,128)(2,1)S(1)}, u32[]{:S(2)}, u32[]{:S(2)}) async-start(bf16[8,2,42,128]{3,1,2,0:T(2,128)(2,1)} %broadcast_in_dim.9), calls=%async_computation | async-start | bytes 344064 | tf_op jit(solution)/shard_map/all_to_all | solution.py:155
  41.2 37.7 %copy-start = (bf16[256,2688]{1,0:T(8,128)(2,1)S(1)}, bf16[256,2688]{1,0:T(8,128)(2,1)}, u32[]{:S(2)}) copy-start(bf16[256,2688]{1,0:T(8,128)(2,1)} %own_ref.1) | copy-start | bytes 4128772
  41.2 37.7 %all-to-all-start.1 = ((bf16[4,672,128]{2,1,0:T(8,128)(2,1)}), bf16[4,672,128]{2,1,0:T(8,128)(2,1)S(1)}, u32[]{:S(2)}, u32[]{:S(2)}) async-start(bf16[4,672,128]{2,1,0:T(8,128)(2,1)} %broadcast_in_dim.11), calls=%async_computation.1 | async-start | bytes 1376256 | tf_op jit(solution)/shard_map/all_to_all | solution.py:157
  46.6 16.5 %collective-permute-start.1 = (bf16[512,128]{1,0:T(8,128)(2,1)S(1)}, bf16[512,128]{1,0:T(8,128)(2,1)}, u32[]{:S(2)}, u32[]{:S(2)}) collective-permute-start(bf16[512,128]{1,0:T(8,128)(2,1)S(1)} %pad_maximum_fusion.1), channel_id=1, source_target_pairs={{0,24},{12,36},{24,48},{36,60},{48,72},{60,84},{72,96},{84,108},{9... | collective-permute-start | bytes 393224 | tf_op jit(solution)/shard_map/ppermute | solution.py:33
  48.5 20.8 %collective-permute-start.2 = (bf16[512,128]{1,0:T(8,128)(2,1)S(1)}, bf16[512,128]{1,0:T(8,128)(2,1)}, u32[]{:S(2)}, u32[]{:S(2)}) collective-permute-start(bf16[512,128]{1,0:T(8,128)(2,1)S(1)} %pad_maximum_fusion.1), channel_id=1, source_target_pairs={{0,12},{12,24},{24,36},{36,48},{48,60},{60,72},{72,84},{84,96},{96... | collective-permute-start | bytes 393224 | tf_op jit(solution)/shard_map/ppermute | solution.py:33
  75.1 6.0 %collective-permute-start.8 = (bf16[512,128]{1,0:T(8,128)(2,1)}, bf16[512,128]{1,0:T(8,128)(2,1)}, u32[]{:S(2)}, u32[]{:S(2)}) collective-permute-start(bf16[512,128]{1,0:T(8,128)(2,1)} %get-tuple-element.8), channel_id=1, source_target_pairs={{12,0},{24,12},{36,24},{48,36},{60,48},{72,60},{84,72},{96,84},{10... | collective-permute-start | bytes 393224 | tf_op jit(solution)/shard_map/ppermute | solution.py:33
  77.0 11.4 %collective-permute-start.9 = (bf16[512,128]{1,0:T(8,128)(2,1)}, bf16[512,128]{1,0:T(8,128)(2,1)}, u32[]{:S(2)}, u32[]{:S(2)}) collective-permute-start(bf16[512,128]{1,0:T(8,128)(2,1)} %get-tuple-element.9), channel_id=1, source_target_pairs={{24,0},{36,12},{48,24},{60,36},{72,48},{84,60},{96,72},{108,84},{1... | collective-permute-start | bytes 393224 | tf_op jit(solution)/shard_map/ppermute | solution.py:33
  88.4 1.1 copy-start.1
  93.0 10.6 %copy-start.2 = (bf16[256,2688]{1,0:T(8,128)(2,1)S(1)}, bf16[256,2688]{1,0:T(8,128)(2,1)}, u32[]{:S(2)}) copy-start(bf16[256,2688]{1,0:T(8,128)(2,1)} %copy-done.1) | copy-start | bytes 4128772
  93.0 38.2 %all-to-all-start.2 = ((bf16[4,672,128]{2,1,0:T(8,128)(2,1)}), bf16[4,672,128]{2,1,0:T(8,128)(2,1)S(1)}, u32[]{:S(2)}, u32[]{:S(2)}) async-start(bf16[4,672,128]{2,1,0:T(8,128)(2,1)} %bitcast.32), calls=%async_computation.2 | async-start | bytes 1376256 | tf_op jit(solution)/shard_map/all_to_all | solution.py:199
  104.1 23.3 %copy-start.5 = (bf16[512,128]{1,0:T(8,128)(2,1)}, bf16[512,128]{1,0:T(8,128)(2,1)S(1)}, u32[]{:S(2)}) copy-start(bf16[512,128]{1,0:T(8,128)(2,1)S(1)} %pad_maximum_fusion.2.v0_ref) | copy-start | bytes 393220
  104.1 17.7 %collective-permute-start.5 = (bf16[512,128]{1,0:T(8,128)(2,1)S(1)}, bf16[512,128]{1,0:T(8,128)(2,1)S(1)}, u32[]{:S(2)}, u32[]{:S(2)}) collective-permute-start(bf16[512,128]{1,0:T(8,128)(2,1)S(1)} %pad_maximum_fusion.2.v0_ref), channel_id=1, source_target_pairs={{0,24},{12,36},{24,48},{36,60},{48,72},{60,84},{72,96},{84,108},{9... | collective-permute-start | bytes 393224 | tf_op jit(solution)/shard_map/ppermute | solution.py:33
  106.0 21.3 %collective-permute-start.6 = (bf16[512,128]{1,0:T(8,128)(2,1)S(1)}, bf16[512,128]{1,0:T(8,128)(2,1)S(1)}, u32[]{:S(2)}, u32[]{:S(2)}) collective-permute-start(bf16[512,128]{1,0:T(8,128)(2,1)S(1)} %pad_maximum_fusion.2.v0_ref), channel_id=1, source_target_pairs={{0,12},{12,24},{24,36},{36,48},{48,60},{60,72},{72,84},{84,96},{96... | collective-permute-start | bytes 393224 | tf_op jit(solution)/shard_map/ppermute | solution.py:33
  121.8 5.6 %copy-start.6 = (bf16[512,128]{1,0:T(8,128)(2,1)}, bf16[512,128]{1,0:T(8,128)(2,1)S(1)}, u32[]{:S(2)}) copy-start(bf16[512,128]{1,0:T(8,128)(2,1)S(1)} %collective-permute-done.5.v2_ref) | copy-start | bytes 393220
  127.3 0.6 copy-start.7
  131.1 11.6 %copy-start.3 = (bf16[2,256,256]{2,1,0:T(8,128)(2,1)S(1)}, bf16[2,256,256]{2,1,0:T(8,128)(2,1)}, u32[]{:S(2)}) copy-start(bf16[2,256,256]{2,1,0:T(8,128)(2,1)} %shard_map.79) | copy-start | bytes 786436
  132.0 29.0 %all-to-all-start.3 = ((bf16[32,21,128]{2,1,0:T(8,128)(2,1)}), bf16[32,21,128]{2,1,0:T(8,128)(2,1)S(1)}, u32[]{:S(2)}, u32[]{:S(2)}) async-start(bf16[32,21,128]{2,1,0:T(8,128)(2,1)} %reshape.40), calls=%async_computation.3 | async-start | bytes 393216 | tf_op jit(solution)/shard_map/all_to_all | solution.py:201
  142.7 3.2 %collective-permute-start.7 = (bf16[256,256]{1,0:T(8,128)(2,1)S(1)}, bf16[256,256]{1,0:T(8,128)(2,1)S(1)}, u32[]{:S(2)}, u32[]{:S(2)}) collective-permute-start(bf16[256,256]{1,0:T(8,128)(2,1)S(1)} %slice_bitcast_fusion), channel_id=1, source_target_pairs={{0,6},{6,0},{1,7},{7,1},{2,8},{8,2},{3,9},{9,3},{4,10},{10,4},{5,1... | collective-permute-start | bytes 393224 | tf_op jit(solution)/shard_map/ppermute | solution.py:212

commit v4 on v3

--- a/solution.py
+++ b/solution.py
@@ -39,16 +39,13 @@
     )
 
 
-def prepare_kernel(core_ref, k_ref, q_ref, g_ref, w_ref, out_ref):
+def prepare_kernel(core_ref, k_ref, q_ref, g_ref, out_ref):
     other = 1 - core_ref[0]
     at = 0
-    for ref in (k_ref, q_ref, g_ref, w_ref):
+    for ref in (k_ref, q_ref, g_ref):
         width = ref.shape[1] // 2
-        out_ref[: ref.shape[0], at : at + width] = ref[:, part_of(other, width)]
+        out_ref[:, at : at + width] = ref[:, part_of(other, width)]
         at += width
-    out_ref[w_ref.shape[0] :, at - width :] = jnp.zeros(
-        (out_ref.shape[0] - w_ref.shape[0], width), out_ref.dtype
-    )
 
 
 def part_of(index, size):
@@ -127,7 +124,6 @@
     nx, nz, ny = (lax.axis_size(a) for a in CHIPS)
     core = lax.axis_index("c")
     first = core == 0
-    low = lax.axis_index("zh") == 0
     chip = (lax.axis_index("x") * nz + lax.axis_index("zh")) * ny + lax.axis_index("y")
     factor = math.log2(math.e) / math.sqrt(HD)
     span = WINDOW + rows
@@ -140,20 +136,18 @@
 
     send = pl.pallas_call(
         prepare_kernel,
-        out_shape=struct((rows, 2 * kv + 2 * qw), BF16),
-        in_specs=[SMEM] + [VMEM] * 4,
+        out_shape=struct((rows, kv + 2 * qw), BF16),
+        in_specs=[SMEM] + [VMEM] * 3,
         out_specs=VMEM,
-    )(core_arg, keys, queries, grads, weight)
+    )(core_arg, keys, queries, grads)
     got = lax.ppermute(send, "c", SWAP)
     k_chip = ordered(first, mine_of(keys), got[:, :kv])
     k_two = chip_shift(k_chip, 2)
     k_one = chip_shift(k_chip, 1)
 
-    w_chip = ordered(first, mine_of(weight), got[:cut, kv + 2 * qw :])
-    w_far = lax.ppermute(w_chip, "zh", SWAP)
-    w_pair = ordered(low, w_chip[None], w_far[None])
-    w_y = lax.all_to_all(jnp.broadcast_to(w_pair[None], (ny, *w_pair.shape)), "y", 0, 0)
-    w_y = w_y.transpose(1, 0, 2, 3).reshape(-1, kv)
+    tile = weight.reshape(cut, 2, kv).transpose(1, 0, 2)[None]
+    tile = jnp.broadcast_to(tile, (nz * ny, *tile.shape[1:])).reshape(-1, cut, kv)
+    w_y = lax.all_to_all(tile, ("zh", "y", "c"), 0, 0).reshape(-1, kv)
     w_x = lax.all_to_all(jnp.broadcast_to(w_y[None], (nx, *w_y.shape)), "x", 0, 0)
     w_full = w_x.reshape(-1, kv)
 

time: 163 us -> 162 us (level)
  the two profiles are of different devices: /device:TPU:67 before, /device:TPU:198 now
where the time goes in v4:
time: 162 us; the launch traced here: 161 us
  waiting for transfers between devices  79.9 us (49%)
  starting transfers between devices  55.9 us (35%)
  Pallas kernels  14.3 us (9%)
  local copies, waits for them, and re-layouts  5.17 us (3%)
  other arithmetic  3.59 us (2%)
    ppermute x6, waiting for transfers between devices, chip_shift(): return lax.ppermute(block, CHIPS, route)  50.5 us
    all_to_all x1, starting transfers between devices, per_device(): w_y = lax.all_to_all(tile, ('zh', 'y', 'c'), 0, 0).reshape(-1, kv)  17.6 us
    all_to_all x1, waiting for transfers between devices, per_device(): w_y = lax.all_to_all(tile, ('zh', 'y', 'c'), 0, 0).reshape(-1, kv)  15.3 us
    all_to_all x1, waiting for transfers between devices, per_device(): lax.all_to_all(term.reshape(nz * ny * 2, cut, kv), ('zh', 'y', 'c'), 0, 0)  12.9 us
    ppermute x6, starting transfers between devices, chip_shift(): return lax.ppermute(block, CHIPS, route)  12.7 us
    all_to_all x1, starting transfers between devices, per_device(): term = lax.all_to_all(term.reshape(nx, -1, kv), 'x', 0, 0)  10.8 us
    pallas_call x1, Pallas kernels, per_device(): pl.pallas_call(functools.partial(attend_kernel, rows, factor), out_shape=...  5.7 us
    all_to_all x1, starting transfers between devices, per_device(): lax.all_to_all(jnp.broadcast_to(w_y[None], (nx, *w_y.shape)), 'x', 0, 0)  4.77 us
  transfers between devices with their start and end apart: 13, of which 9 were waited for; matrix products, arithmetic and copies ran while one was open for 4% of the time, Pallas kernels for 6%

profile of v4, /device:TPU:198, one launch (start us, length us, event | category | flops | bytes accessed | tf_op | source)
XLA Modules:
  0.0 160.8 jit_solution(5335862404803381087)
XLA Ops:
  0.7 2.0 %shard_map.77 = bf16[256,640]{1,0:T(8,128)(2,1)} custom-call(s32[1]{0:T(128)} %bitcast.core_ref, bf16[256,256]{1,0:T(8,128)(2,1)} %refs_0_.1, bf16[256,512]{1,0:T(8,128)(2,1)} %refs_1_.1, bf16[256,512]{1,0:T(8,128)(2,1)} %refs_2_.1), custom_call_target="tpu_custom_call" | custom-call | tf_op jit(solution)/shard_map/pallas_call | solution.py:137
  2.6 1.9 %collective-permute-start = (bf16[256,640]{1,0:T(8,128)(2,1)}, bf16[256,640]{1,0:T(8,128)(2,1)}, u32[]{:S(2)}, u32[]{:S(2)}) collective-permute-start(bf16[256,640]{1,0:T(8,128)(2,1)} %shard_map.77), channel_id=1, source_target_pairs={{0,6},{6,0},{1,7},{7,1},{2,8},{8,2},{3,9},{9,3},{4,10},{10,4},{5,1... | collective-permute-start | bytes 983048 | tf_op jit(solution)/shard_map/ppermute | solution.py:143
  6.0 17.6 %all-to-all-start = ((bf16[32,21,128]{2,1,0:T(8,128)(2,1)}), bf16[32,21,128]{2,1,0:T(8,128)(2,1)S(1)}, u32[]{:S(2)}, u32[]{:S(2)}) async-start(bf16[32,21,128]{2,1,0:T(8,128)(2,1)} %bitcast.2), calls=%async_computation | async-start | bytes 393216 | tf_op jit(solution)/shard_map/all_to_all | solution.py:150
  23.6 2.2 %collective-permute-start.3 = (bf16[256,2688]{1,0:T(8,128)(2,1)S(1)}, bf16[256,2688]{1,0:T(8,128)(2,1)S(1)}, u32[]{:S(2)}, u32[]{:S(2)}) collective-permute-start(bf16[256,2688]{1,0:T(8,128)(2,1)S(1)} %copy-done), channel_id=1, source_target_pairs={{0,6},{6,0},{1,7},{7,1},{2,8},{8,2},{3,9},{9,3},{4,10},{10,4},{5,1... | collective-permute-start | bytes 4128776 | tf_op jit(solution)/shard_map/ppermute | solution.py:154
  26.5 15.3 %all-to-all-done = bf16[32,21,128]{2,1,0:T(8,128)(2,1)S(1)} async-done(((bf16[32,21,128]{2,1,0:T(8,128)(2,1)}), bf16[32,21,128]{2,1,0:T(8,128)(2,1)S(1)}, u32[]{:S(2)}, u32[]{:S(2)}) %all-to-all-start) | async-done | bytes 172064 | tf_op jit(solution)/shard_map/all_to_all | solution.py:150
  42.8 4.8 %all-to-all-start.1 = ((bf16[4,672,128]{2,1,0:T(8,128)(2,1)}), bf16[4,672,128]{2,1,0:T(8,128)(2,1)S(1)}, u32[]{:S(2)}, u32[]{:S(2)}) async-start(bf16[4,672,128]{2,1,0:T(8,128)(2,1)} %broadcast_in_dim.11), calls=%async_computation.1 | async-start | bytes 1376256 | tf_op jit(solution)/shard_map/all_to_all | solution.py:151
  48.5 2.5 %collective-permute-start.1 = (bf16[512,128]{1,0:T(8,128)(2,1)S(1)}, bf16[512,128]{1,0:T(8,128)(2,1)}, u32[]{:S(2)}, u32[]{:S(2)}) collective-permute-start(bf16[512,128]{1,0:T(8,128)(2,1)S(1)} %pad_maximum_fusion.1), channel_id=1, source_target_pairs={{0,24},{12,36},{24,48},{36,60},{48,72},{60,84},{72,96},{84,108},{9... | collective-permute-start | bytes 393224 | tf_op jit(solution)/shard_map/ppermute | solution.py:33
  51.1 2.5 %collective-permute-start.2 = (bf16[512,128]{1,0:T(8,128)(2,1)S(1)}, bf16[512,128]{1,0:T(8,128)(2,1)}, u32[]{:S(2)}, u32[]{:S(2)}) collective-permute-start(bf16[512,128]{1,0:T(8,128)(2,1)S(1)} %pad_maximum_fusion.1), channel_id=1, source_target_pairs={{0,12},{12,24},{24,36},{36,48},{48,60},{60,72},{72,84},{84,96},{96... | collective-permute-start | bytes 393224 | tf_op jit(solution)/shard_map/ppermute | solution.py:33
  54.3 13.3 %collective-permute-done.1.refs_4_ = bf16[512,128]{1,0:T(8,128)(2,1)} collective-permute-done((bf16[512,128]{1,0:T(8,128)(2,1)S(1)}, bf16[512,128]{1,0:T(8,128)(2,1)}, u32[]{:S(2)}, u32[]{:S(2)}) %collective-permute-start.1) | collective-permute-done | bytes 131104 | tf_op jit(solution)/shard_map/ppermute | solution.py:33
  67.6 9.0 %collective-permute-done.2.refs_5_ = bf16[512,128]{1,0:T(8,128)(2,1)} collective-permute-done((bf16[512,128]{1,0:T(8,128)(2,1)S(1)}, bf16[512,128]{1,0:T(8,128)(2,1)}, u32[]{:S(2)}, u32[]{:S(2)}) %collective-permute-start.2) | collective-permute-done | bytes 131104 | tf_op jit(solution)/shard_map/ppermute | solution.py:33
  76.6 5.7 %shard_map.78 = (bf16[2,2,1280,256]{3,2,1,0:T(8,128)(2,1)}, bf16[512,128]{1,0:T(8,128)(2,1)}, bf16[512,128]{1,0:T(8,128)(2,1)}, f32[512,128]{1,0:T(8,128)}) custom-call(s32[1]{0:T(128)} %bitcast.core_ref, bf16[256,256]{1,0:T(8,128)(2,1)} %refs_0_.1, bf16[256,512]{1,0:T(8,128)(2,1)} %refs_1_.1, bf16[256,512]{1,0:T(8,128)(2,1)} %refs_2_.1, ...), custom_call_target="tpu_custom_call" | custom-call | tf_op jit(solution)/shard_map/pallas_call | solution.py:164
  82.3 1.9 %collective-permute-start.7 = (bf16[512,128]{1,0:T(8,128)(2,1)}, bf16[512,128]{1,0:T(8,128)(2,1)}, u32[]{:S(2)}, u32[]{:S(2)}) collective-permute-start(bf16[512,128]{1,0:T(8,128)(2,1)} %get-tuple-element.8), channel_id=1, source_target_pairs={{12,0},{24,12},{36,24},{48,36},{60,48},{72,60},{84,72},{96,84},{10... | collective-permute-start | bytes 393224 | tf_op jit(solution)/shard_map/ppermute | solution.py:33
  84.2 1.9 %collective-permute-start.8 = (bf16[512,128]{1,0:T(8,128)(2,1)}, bf16[512,128]{1,0:T(8,128)(2,1)}, u32[]{:S(2)}, u32[]{:S(2)}) collective-permute-start(bf16[512,128]{1,0:T(8,128)(2,1)} %get-tuple-element.9), channel_id=1, source_target_pairs={{24,0},{36,12},{48,24},{60,36},{72,48},{84,60},{96,72},{108,84},{1... | collective-permute-start | bytes 393224 | tf_op jit(solution)/shard_map/ppermute | solution.py:33
  86.7 3.7 %collective-permute-done.7.back1_ref = bf16[512,128]{1,0:T(8,128)(2,1)} collective-permute-done((bf16[512,128]{1,0:T(8,128)(2,1)}, bf16[512,128]{1,0:T(8,128)(2,1)}, u32[]{:S(2)}, u32[]{:S(2)}) %collective-permute-start.7) | collective-permute-done | bytes 131104 | tf_op jit(solution)/shard_map/ppermute | solution.py:33
  93.4 3.5 %shard_map.80 = bf16[2688,128]{1,0:T(8,128)(2,1)} custom-call(s32[1]{0:T(128)} %bitcast.core_ref, bf16[256,2688]{1,0:T(8,128)(2,1)} %own_ref.1, bf16[256,2688]{1,0:T(8,128)(2,1)} %copy-done.1, f32[512,128]{1,0:T(8,128)} %get-tuple-element.7.part_ref, bf16[512,128]{1,0:T(8,128)(2,1)} %collective-permute-done.7.back1_ref, ...), custom_call_target="tpu_custom_call" | custom-call | tf_op jit(solution)/shard_map/pallas_call | solution.py:185
  96.9 10.8 %all-to-all-start.2 = ((bf16[4,672,128]{2,1,0:T(8,128)(2,1)}), bf16[4,672,128]{2,1,0:T(8,128)(2,1)S(1)}, u32[]{:S(2)}, u32[]{:S(2)}) async-start(bf16[4,672,128]{2,1,0:T(8,128)(2,1)} %bitcast.25), calls=%async_computation.2 | async-start | bytes 1376256 | tf_op jit(solution)/shard_map/all_to_all | solution.py:193
  108.3 1.9 %collective-permute-start.4 = (bf16[512,128]{1,0:T(8,128)(2,1)S(1)}, bf16[512,128]{1,0:T(8,128)(2,1)S(1)}, u32[]{:S(2)}, u32[]{:S(2)}) collective-permute-start(bf16[512,128]{1,0:T(8,128)(2,1)S(1)} %pad_maximum_fusion.2.v0_ref), channel_id=1, source_target_pairs={{0,24},{12,36},{24,48},{36,60},{48,72},{60,84},{72,96},{84,108},{9... | collective-permute-start | bytes 393224 | tf_op jit(solution)/shard_map/ppermute | solution.py:33
  110.2 1.9 %collective-permute-start.5 = (bf16[512,128]{1,0:T(8,128)(2,1)S(1)}, bf16[512,128]{1,0:T(8,128)(2,1)S(1)}, u32[]{:S(2)}, u32[]{:S(2)}) collective-permute-start(bf16[512,128]{1,0:T(8,128)(2,1)S(1)} %pad_maximum_fusion.2.v0_ref), channel_id=1, source_target_pairs={{0,12},{12,24},{24,36},{36,48},{48,60},{60,72},{72,84},{84,96},{96... | collective-permute-start | bytes 393224 | tf_op jit(solution)/shard_map/ppermute | solution.py:33
  112.1 15.9 %collective-permute-done.4.v2_ref = bf16[512,128]{1,0:T(8,128)(2,1)S(1)} collective-permute-done((bf16[512,128]{1,0:T(8,128)(2,1)S(1)}, bf16[512,128]{1,0:T(8,128)(2,1)S(1)}, u32[]{:S(2)}, u32[]{:S(2)}) %collective-permute-start.4) | collective-permute-done | bytes 131104 | tf_op jit(solution)/shard_map/ppermute | solution.py:33
  128.1 6.6 %collective-permute-done.5.v1_ref = bf16[512,128]{1,0:T(8,128)(2,1)S(1)} collective-permute-done((bf16[512,128]{1,0:T(8,128)(2,1)S(1)}, bf16[512,128]{1,0:T(8,128)(2,1)S(1)}, u32[]{:S(2)}, u32[]{:S(2)}) %collective-permute-start.5) | collective-permute-done | bytes 131104 | tf_op jit(solution)/shard_map/ppermute | solution.py:33
  135.3 3.2 %shard_map.79 = bf16[2,256,256]{2,1,0:T(8,128)(2,1)} custom-call(s32[1]{0:T(128)} %bitcast.core_ref, bf16[2,2,1280,256]{3,2,1,0:T(8,128)(2,1)} %get-tuple-element.6.probs_ref, bf16[512,128]{1,0:T(8,128)(2,1)} %copy-done.6, bf16[512,128]{1,0:T(8,128)(2,1)} %copy-done.7, bf16[512,128]{1,0:T(8,128)(2,1)} %copy-done.4), custom_call_target="tpu_custom_call" | custom-call | tf_op jit(solution)/shard_map/pallas_call | solution.py:199
  139.4 3.9 %all-to-all-start.3 = ((bf16[32,21,128]{2,1,0:T(8,128)(2,1)}), bf16[32,21,128]{2,1,0:T(8,128)(2,1)S(1)}, u32[]{:S(2)}, u32[]{:S(2)}) async-start(bf16[32,21,128]{2,1,0:T(8,128)(2,1)} %reshape.46), calls=%async_computation.3 | async-start | bytes 393216 | tf_op jit(solution)/shard_map/all_to_all | solution.py:195
  143.3 2.1 %collective-permute-start.6 = (bf16[256,256]{1,0:T(8,128)(2,1)S(1)}, bf16[256,256]{1,0:T(8,128)(2,1)S(1)}, u32[]{:S(2)}, u32[]{:S(2)}) collective-permute-start(bf16[256,256]{1,0:T(8,128)(2,1)S(1)} %slice_bitcast_fusion), channel_id=1, source_target_pairs={{0,6},{6,0},{1,7},{7,1},{2,8},{8,2},{3,9},{9,3},{4,10},{10,4},{5,1... | collective-permute-start | bytes 393224 | tf_op jit(solution)/shard_map/ppermute | solution.py:206
  147.3 12.9 %all-to-all-done.3 = bf16[32,21,128]{2,1,0:T(8,128)(2,1)S(1)} async-done(((bf16[32,21,128]{2,1,0:T(8,128)(2,1)}), bf16[32,21,128]{2,1,0:T(8,128)(2,1)S(1)}, u32[]{:S(2)}, u32[]{:S(2)}) %all-to-all-start.3) | async-done | bytes 172064 | tf_op jit(solution)/shard_map/all_to_all | solution.py:195
  (49 shorter events, 12.9 us)
Async XLA Ops:
  0.6 22.9 %copy-start = (bf16[256,2688]{1,0:T(8,128)(2,1)S(1)}, bf16[256,2688]{1,0:T(8,128)(2,1)}, u32[]{:S(2)}) copy-start(bf16[256,2688]{1,0:T(8,128)(2,1)} %own_ref.1) | copy-start | bytes 4128772
  0.6 25.1 %copy-start.5 = (s32[32768]{0:T(1024)S(1)}, s32[32768]{0:T(1024)}, u32[]{:S(2)}) copy-start(s32[32768]{0:T(1024)} %param.11) | copy-start | bytes 393220
  2.6 45.0 %collective-permute-start = (bf16[256,640]{1,0:T(8,128)(2,1)}, bf16[256,640]{1,0:T(8,128)(2,1)}, u32[]{:S(2)}, u32[]{:S(2)}) collective-permute-start(bf16[256,640]{1,0:T(8,128)(2,1)} %shard_map.77), channel_id=1, source_target_pairs={{0,6},{6,0},{1,7},{7,1},{2,8},{8,2},{3,9},{9,3},{4,10},{10,4},{5,1... | collective-permute-start | bytes 983048 | tf_op jit(solution)/shard_map/ppermute | solution.py:143
  6.0 35.8 %all-to-all-start = ((bf16[32,21,128]{2,1,0:T(8,128)(2,1)}), bf16[32,21,128]{2,1,0:T(8,128)(2,1)S(1)}, u32[]{:S(2)}, u32[]{:S(2)}) async-start(bf16[32,21,128]{2,1,0:T(8,128)(2,1)} %bitcast.2), calls=%async_computation | async-start | bytes 393216 | tf_op jit(solution)/shard_map/all_to_all | solution.py:150
  23.6 68.8 %collective-permute-start.3 = (bf16[256,2688]{1,0:T(8,128)(2,1)S(1)}, bf16[256,2688]{1,0:T(8,128)(2,1)S(1)}, u32[]{:S(2)}, u32[]{:S(2)}) collective-permute-start(bf16[256,2688]{1,0:T(8,128)(2,1)S(1)} %copy-done), channel_id=1, source_target_pairs={{0,6},{6,0},{1,7},{7,1},{2,8},{8,2},{3,9},{9,3},{4,10},{10,4},{5,1... | collective-permute-start | bytes 4128776 | tf_op jit(solution)/shard_map/ppermute | solution.py:154
  42.8 43.3 %all-to-all-start.1 = ((bf16[4,672,128]{2,1,0:T(8,128)(2,1)}), bf16[4,672,128]{2,1,0:T(8,128)(2,1)S(1)}, u32[]{:S(2)}, u32[]{:S(2)}) async-start(bf16[4,672,128]{2,1,0:T(8,128)(2,1)} %broadcast_in_dim.11), calls=%async_computation.1 | async-start | bytes 1376256 | tf_op jit(solution)/shard_map/all_to_all | solution.py:151
  48.5 19.1 %collective-permute-start.1 = (bf16[512,128]{1,0:T(8,128)(2,1)S(1)}, bf16[512,128]{1,0:T(8,128)(2,1)}, u32[]{:S(2)}, u32[]{:S(2)}) collective-permute-start(bf16[512,128]{1,0:T(8,128)(2,1)S(1)} %pad_maximum_fusion.1), channel_id=1, source_target_pairs={{0,24},{12,36},{24,48},{36,60},{48,72},{60,84},{72,96},{84,108},{9... | collective-permute-start | bytes 393224 | tf_op jit(solution)/shard_map/ppermute | solution.py:33
  51.1 25.5 %collective-permute-start.2 = (bf16[512,128]{1,0:T(8,128)(2,1)S(1)}, bf16[512,128]{1,0:T(8,128)(2,1)}, u32[]{:S(2)}, u32[]{:S(2)}) collective-permute-start(bf16[512,128]{1,0:T(8,128)(2,1)S(1)} %pad_maximum_fusion.1), channel_id=1, source_target_pairs={{0,12},{12,24},{24,36},{36,48},{48,60},{60,72},{72,84},{84,96},{96... | collective-permute-start | bytes 393224 | tf_op jit(solution)/shard_map/ppermute | solution.py:33
  82.3 8.1 %collective-permute-start.7 = (bf16[512,128]{1,0:T(8,128)(2,1)}, bf16[512,128]{1,0:T(8,128)(2,1)}, u32[]{:S(2)}, u32[]{:S(2)}) collective-permute-start(bf16[512,128]{1,0:T(8,128)(2,1)} %get-tuple-element.8), channel_id=1, source_target_pairs={{12,0},{24,12},{36,24},{48,36},{60,48},{72,60},{84,72},{96,84},{10... | collective-permute-start | bytes 393224 | tf_op jit(solution)/shard_map/ppermute | solution.py:33
  84.2 8.1 %collective-permute-start.8 = (bf16[512,128]{1,0:T(8,128)(2,1)}, bf16[512,128]{1,0:T(8,128)(2,1)}, u32[]{:S(2)}, u32[]{:S(2)}) collective-permute-start(bf16[512,128]{1,0:T(8,128)(2,1)} %get-tuple-element.9), channel_id=1, source_target_pairs={{24,0},{36,12},{48,24},{60,36},{72,48},{84,60},{96,72},{108,84},{1... | collective-permute-start | bytes 393224 | tf_op jit(solution)/shard_map/ppermute | solution.py:33
  92.3 1.1 copy-start.1
  96.9 10.8 %copy-start.2 = (bf16[256,2688]{1,0:T(8,128)(2,1)S(1)}, bf16[256,2688]{1,0:T(8,128)(2,1)}, u32[]{:S(2)}) copy-start(bf16[256,2688]{1,0:T(8,128)(2,1)} %copy-done.1) | copy-start | bytes 4128772
  96.9 41.6 %all-to-all-start.2 = ((bf16[4,672,128]{2,1,0:T(8,128)(2,1)}), bf16[4,672,128]{2,1,0:T(8,128)(2,1)S(1)}, u32[]{:S(2)}, u32[]{:S(2)}) async-start(bf16[4,672,128]{2,1,0:T(8,128)(2,1)} %bitcast.25), calls=%async_computation.2 | async-start | bytes 1376256 | tf_op jit(solution)/shard_map/all_to_all | solution.py:193
  108.3 26.4 %copy-start.4 = (bf16[512,128]{1,0:T(8,128)(2,1)}, bf16[512,128]{1,0:T(8,128)(2,1)S(1)}, u32[]{:S(2)}) copy-start(bf16[512,128]{1,0:T(8,128)(2,1)S(1)} %pad_maximum_fusion.2.v0_ref) | copy-start | bytes 393220
  108.3 19.8 %collective-permute-start.4 = (bf16[512,128]{1,0:T(8,128)(2,1)S(1)}, bf16[512,128]{1,0:T(8,128)(2,1)S(1)}, u32[]{:S(2)}, u32[]{:S(2)}) collective-permute-start(bf16[512,128]{1,0:T(8,128)(2,1)S(1)} %pad_maximum_fusion.2.v0_ref), channel_id=1, source_target_pairs={{0,24},{12,36},{24,48},{36,60},{48,72},{60,84},{72,96},{84,108},{9... | collective-permute-start | bytes 393224 | tf_op jit(solution)/shard_map/ppermute | solution.py:33
  110.2 24.5 %collective-permute-start.5 = (bf16[512,128]{1,0:T(8,128)(2,1)S(1)}, bf16[512,128]{1,0:T(8,128)(2,1)S(1)}, u32[]{:S(2)}, u32[]{:S(2)}) collective-permute-start(bf16[512,128]{1,0:T(8,128)(2,1)S(1)} %pad_maximum_fusion.2.v0_ref), channel_id=1, source_target_pairs={{0,12},{12,24},{24,36},{36,48},{48,60},{60,72},{72,84},{84,96},{96... | collective-permute-start | bytes 393224 | tf_op jit(solution)/shard_map/ppermute | solution.py:33
  128.1 6.6 %copy-start.6 = (bf16[512,128]{1,0:T(8,128)(2,1)}, bf16[512,128]{1,0:T(8,128)(2,1)S(1)}, u32[]{:S(2)}) copy-start(bf16[512,128]{1,0:T(8,128)(2,1)S(1)} %collective-permute-done.4.v2_ref) | copy-start | bytes 393220
  134.7 0.6 copy-start.7
  138.5 4.7 %copy-start.3 = (bf16[2,256,256]{2,1,0:T(8,128)(2,1)S(1)}, bf16[2,256,256]{2,1,0:T(8,128)(2,1)}, u32[]{:S(2)}) copy-start(bf16[2,256,256]{2,1,0:T(8,128)(2,1)} %shard_map.79) | copy-start | bytes 786436
  139.4 20.8 %all-to-all-start.3 = ((bf16[32,21,128]{2,1,0:T(8,128)(2,1)}), bf16[32,21,128]{2,1,0:T(8,128)(2,1)S(1)}, u32[]{:S(2)}, u32[]{:S(2)}) async-start(bf16[32,21,128]{2,1,0:T(8,128)(2,1)} %reshape.46), calls=%async_computation.3 | async-start | bytes 393216 | tf_op jit(solution)/shard_map/all_to_all | solution.py:195
  143.3 3.2 %collective-permute-start.6 = (bf16[256,256]{1,0:T(8,128)(2,1)S(1)}, bf16[256,256]{1,0:T(8,128)(2,1)S(1)}, u32[]{:S(2)}, u32[]{:S(2)}) collective-permute-start(bf16[256,256]{1,0:T(8,128)(2,1)S(1)} %slice_bitcast_fusion), channel_id=1, source_target_pairs={{0,6},{6,0},{1,7},{7,1},{2,8},{8,2},{3,9},{9,3},{4,10},{10,4},{5,1... | collective-permute-start | bytes 393224 | tf_op jit(solution)/shard_map/ppermute | solution.py:206

commit v5 on v4

--- a/solution.py
+++ b/solution.py
@@ -33,16 +33,16 @@
     return lax.ppermute(block, CHIPS, route)
 
 
-def ordered(first, own, other, axis=0):
-    return jnp.concatenate(
-        [jnp.where(first, own, other), jnp.where(first, other, own)], axis=axis
-    )
-
-
-def prepare_kernel(core_ref, k_ref, q_ref, g_ref, out_ref):
+def ordered(core, own, other):
+    slot = lax.broadcasted_iota(jnp.int32, (2, *own.shape), 0)
+    both = jnp.where(slot == core, own[None], other[None])
+    return both.reshape(-1, *own.shape[1:])
+
+
+def prepare_kernel(core_ref, q_ref, g_ref, out_ref):
     other = 1 - core_ref[0]
     at = 0
-    for ref in (k_ref, q_ref, g_ref):
+    for ref in (q_ref, g_ref):
         width = ref.shape[1] // 2
         out_ref[:, at : at + width] = ref[:, part_of(other, width)]
         at += width
@@ -53,17 +53,14 @@
 
 
 def attend_kernel(rows, factor, core_ref, *refs):
-    k_ref, q_ref, g_ref, got_ref, k2_ref, k1_ref, low_ref = refs[:7]
+    k2_ref, k1_ref, k0_ref, q_ref, g_ref, got_ref, low_ref = refs[:7]
     probs_ref, part2_ref, part1_ref, part0_ref, win, total = refs[7:]
     chip_rows = 2 * rows
     span = win.shape[0] - rows
-    kv, qw = k_ref.shape[1] // 2, q_ref.shape[1] // 2
+    qw = q_ref.shape[1] // 2
     core = core_ref[0]
-    win[:chip_rows] = k2_ref[...]
-    win[chip_rows : 2 * chip_rows] = k1_ref[...]
-    home = win.at[2 * chip_rows :]
-    home[part_of(core, rows)] = k_ref[:, part_of(core, kv)]
-    home[part_of(1 - core, rows)] = got_ref[:, :kv]
+    for i, ref in enumerate((k2_ref, k1_ref, k0_ref)):
+        win[i * chip_rows : (i + 1) * chip_rows] = ref[...]
     total[...] = jnp.zeros_like(total)
     u = lax.broadcasted_iota(jnp.int32, (span, rows), 0)
     t = lax.broadcasted_iota(jnp.int32, (span, rows), 1) + (span - rows)
@@ -77,8 +74,8 @@
                 q = q_ref[:, part_of(core * (qw // HD) + h, HD)]
                 g = g_ref[:, part_of(core * (qw // HD) + h, HD)]
             else:
-                q = got_ref[:, kv + h * HD : kv + (h + 1) * HD]
-                g = got_ref[:, kv + qw + h * HD : kv + qw + (h + 1) * HD]
+                q = got_ref[:, h * HD : (h + 1) * HD]
+                g = got_ref[:, qw + h * HD : qw + (h + 1) * HD]
             s = jnp.where(allowed, dot(keys, q, 1, 1), -1e30)
             w = jnp.exp2((s - jnp.max(s, axis=0, keepdims=True)) * factor)
             p = (w * (1.0 / jnp.sum(w, axis=0, keepdims=True))).astype(BF16)
@@ -89,17 +86,23 @@
     part0_ref[...] = total[2 * chip_rows :]
 
 
-def output_kernel(rows, core_ref, probs_ref, v2_ref, v1_ref, v0_ref, out_ref, win):
+def output_kernel(rows, slot, core_ref, probs_ref, v2_ref, v1_ref, v0_ref, *rest):
+    *got, out_ref, win = rest
     chip_rows = 2 * rows
     span = win.shape[0] - rows
+    width = probs_ref.shape[1] * HD
+    core = core_ref[0]
     for i, ref in enumerate((v2_ref, v1_ref, v0_ref)):
         win[i * chip_rows : (i + 1) * chip_rows] = ref[...]
-    for slot in range(2):
-        j = core_ref[0] if slot == 0 else 1 - core_ref[0]
-        values = win[pl.ds(pl.multiple_of(j * rows, rows), span)]
-        for h in range(probs_ref.shape[1]):
-            o = dot(values, probs_ref[slot, h], 0, 0)
-            out_ref[slot, :, h * HD : (h + 1) * HD] = o.T.astype(BF16)
+    j = core if slot == 0 else 1 - core
+    values = win[pl.ds(pl.multiple_of(j * rows, rows), span)]
+    out = [dot(values, probs_ref[slot, h], 0, 0).T for h in range(probs_ref.shape[1])]
+    out = jnp.concatenate(out, axis=1).astype(BF16)
+    if slot == 0:
+        out_ref[:, part_of(core, width)] = out
+        out_ref[:, part_of(1 - core, width)] = got[0][...]
+    else:
+        out_ref[...] = out
 
 
 def outer_kernel(rows, core_ref, own_ref, got_ref, part_ref, back1_ref, back2_ref, out_ref, vg):
@@ -130,28 +133,25 @@
     whole = span + rows
     core_arg = core.astype(jnp.int32)[None]
 
-    def mine_of(a):
-        w = a.shape[1] // 2
-        return jnp.where(first, a[:, :w], a[:, w:])
+    k_got = lax.ppermute(jnp.where(first, keys[:, kv:], keys[:, :kv]), "c", SWAP)
+    k_chip = ordered(core, jnp.where(first, keys[:, :kv], keys[:, kv:]), k_got)
+    k_two = chip_shift(k_chip, 2)
+    k_one = chip_shift(k_chip, 1)
 
     send = pl.pallas_call(
         prepare_kernel,
-        out_shape=struct((rows, kv + 2 * qw), BF16),
-        in_specs=[SMEM] + [VMEM] * 3,
+        out_shape=struct((rows, 2 * qw), BF16),
+        in_specs=[SMEM] + [VMEM] * 2,
         out_specs=VMEM,
-    )(core_arg, keys, queries, grads)
+    )(core_arg, queries, grads)
     got = lax.ppermute(send, "c", SWAP)
-    k_chip = ordered(first, mine_of(keys), got[:, :kv])
-    k_two = chip_shift(k_chip, 2)
-    k_one = chip_shift(k_chip, 1)
+    hidden_got = lax.ppermute(hidden, "c", SWAP)
 
     tile = weight.reshape(cut, 2, kv).transpose(1, 0, 2)[None]
     tile = jnp.broadcast_to(tile, (nz * ny, *tile.shape[1:])).reshape(-1, cut, kv)
     w_y = lax.all_to_all(tile, ("zh", "y", "c"), 0, 0).reshape(-1, kv)
     w_x = lax.all_to_all(jnp.broadcast_to(w_y[None], (nx, *w_y.shape)), "x", 0, 0)
     w_full = w_x.reshape(-1, kv)
-
-    hidden_got = lax.ppermute(hidden, "c", SWAP)
 
     padding = 2 * chip_rows
     padded = jnp.concatenate([jnp.full((padding,), -1, jnp.int32), segments], axis=0)
@@ -172,13 +172,15 @@
         in_specs=[SMEM] + [VMEM] * 7,
         out_specs=[VMEM] * 4,
         scratch_shapes=[pltpu.VMEM((whole, kv), BF16), pltpu.VMEM((whole, kv), F32)],
-    )(core_arg, keys, queries, grads, got, k_two, k_one, begin)
+    )(core_arg, k_two, k_one, k_chip, queries, grads, got, begin)
     back2 = chip_shift(part2, -2)
     back1 = chip_shift(part1, -1)
 
     v_own = jnp.dot(hidden, w_full, preferred_element_type=F32).astype(BF16)
     v_other = jnp.dot(hidden_got, w_full, preferred_element_type=F32).astype(BF16)
-    v_chip = ordered(first, v_own, v_other)
+    v_chip = jnp.concatenate(
+        [jnp.where(first, v_own, v_other), jnp.where(first, v_other, v_own)], axis=0
+    )
     v_two = chip_shift(v_chip, 2)
     v_one = chip_shift(v_chip, 1)
 
@@ -196,15 +198,18 @@
     term = jnp.sum(term.astype(F32).reshape(nz * ny, 2, cut, kv), axis=0)
     weight_grad = jnp.concatenate([term[0], term[1]], axis=1)
 
-    output = pl.pallas_call(
-        functools.partial(output_kernel, rows),
-        out_shape=struct((2, rows, qw), BF16),
-        in_specs=[SMEM] + [VMEM] * 4,
-        out_specs=VMEM,
-        scratch_shapes=[pltpu.VMEM((whole, kv), BF16)],
-    )(core_arg, probs, v_two, v_one, v_chip)
-    out_got = lax.ppermute(output[1], "c", SWAP)
-    attention = ordered(first, output[0], out_got, axis=1)
+    def outputs(slot, *got):
+        return pl.pallas_call(
+            functools.partial(output_kernel, rows, slot),
+            out_shape=struct((rows, qw * (1 + len(got))), BF16),
+            in_specs=[SMEM] + [VMEM] * (4 + len(got)),
+            out_specs=VMEM,
+            scratch_shapes=[pltpu.VMEM((whole, kv), BF16)],
+        )(core_arg, probs, v_two, v_one, v_chip, *got)
+
+    out_send = outputs(1)
+    out_got = lax.ppermute(out_send, "c", SWAP)
+    attention = outputs(0, out_got)
     return attention, weight_grad
 
 

time: 162 us -> 188 us (1.16)
  the two profiles are of different devices: /device:TPU:198 before, /device:TPU:67 now
where the time goes in v5:
time: 188 us; the launch traced here: 187 us
  waiting for transfers between devices  85.4 us (45%)
  starting transfers between devices  71.7 us (38%)
  Pallas kernels  17.1 us (9%)
  local copies, waits for them, and re-layouts  7.31 us (4%)
  other arithmetic  4.03 us (2%)
    ppermute x6, waiting for transfers between devices, chip_shift(): return lax.ppermute(block, CHIPS, route)  60.8 us
    all_to_all x1, starting transfers between devices, per_device(): w_y = lax.all_to_all(tile, ('zh', 'y', 'c'), 0, 0).reshape(-1, kv)  19.1 us
    all_to_all x1, starting transfers between devices, per_device(): lax.all_to_all(term.reshape(nz * ny * 2, cut, kv), ('zh', 'y', 'c'), 0, 0)  18 us
    all_to_all x1, waiting for transfers between devices, per_device(): w_y = lax.all_to_all(tile, ('zh', 'y', 'c'), 0, 0).reshape(-1, kv)  16.6 us
    ppermute x6, starting transfers between devices, chip_shift(): return lax.ppermute(block, CHIPS, route)  16.3 us
    all_to_all x1, waiting for transfers between devices, per_device(): term = lax.all_to_all(term.reshape(nx, -1, kv), 'x', 0, 0)  6.81 us
    pallas_call x2, Pallas kernels, outputs(): pl.pallas_call(functools.partial(output_kernel, rows, slot), out_shape=st...  6.02 us
    pallas_call x1, Pallas kernels, per_device(): pl.pallas_call(functools.partial(attend_kernel, rows, factor), out_shape=...  5.76 us
  transfers between devices with their start and end apart: 14, of which 9 were waited for; matrix products, arithmetic and copies ran while one was open for 3% of the time, Pallas kernels for 9%

profile of v5, /device:TPU:67, one launch (start us, length us, event | category | flops | bytes accessed | tf_op | source)
XLA Modules:
  0.0 187.4 jit_solution(1756866558085737942)
XLA Ops:
  0.6 2.7 %collective-permute-start.4 = (bf16[256,2688]{1,0:T(8,128)(2,1)}, bf16[256,2688]{1,0:T(8,128)(2,1)S(1)}, u32[]{:S(2)}, u32[]{:S(2)}) collective-permute-start(bf16[256,2688]{1,0:T(8,128)(2,1)} %own_ref.1), channel_id=1, source_target_pairs={{0,6},{6,0},{1,7},{7,1},{2,8},{8,2},{3,9},{9,3},{4,10},{10,4},{5,1... | collective-permute-start | bytes 4128776 | tf_op jit(solution)/shard_map/ppermute | solution.py:148
  4.3 1.9 %collective-permute-start = (bf16[256,128]{1,0:T(8,128)(2,1)S(1)}, bf16[256,128]{1,0:T(8,128)(2,1)S(1)}, u32[]{:S(2)}, u32[]{:S(2)}) collective-permute-start(bf16[256,128]{1,0:T(8,128)(2,1)S(1)} %get-tuple-element.13), channel_id=1, source_target_pairs={{0,6},{6,0},{1,7},{7,1},{2,8},{8,2},{3,9},{9,3},{4,10},{10,4},{5,1... | collective-permute-start | bytes 196616 | tf_op jit(solution)/shard_map/ppermute | solution.py:136
  7.9 2.4 %collective-permute-start.3 = (bf16[256,512]{1,0:T(8,128)(2,1)}, bf16[256,512]{1,0:T(8,128)(2,1)S(1)}, u32[]{:S(2)}, u32[]{:S(2)}) collective-permute-start(bf16[256,512]{1,0:T(8,128)(2,1)} %shard_map.77), channel_id=1, source_target_pairs={{0,6},{6,0},{1,7},{7,1},{2,8},{8,2},{3,9},{9,3},{4,10},{10,4},{5,1... | collective-permute-start | bytes 786440 | tf_op jit(solution)/shard_map/ppermute | solution.py:147
  11.8 19.1 %all-to-all-start = ((bf16[32,21,128]{2,1,0:T(8,128)(2,1)}), bf16[32,21,128]{2,1,0:T(8,128)(2,1)S(1)}, u32[]{:S(2)}, u32[]{:S(2)}) async-start(bf16[32,21,128]{2,1,0:T(8,128)(2,1)} %bitcast.4), calls=%async_computation | async-start | bytes 393216 | tf_op jit(solution)/shard_map/all_to_all | solution.py:152
  31.5 16.6 %all-to-all-done = bf16[32,21,128]{2,1,0:T(8,128)(2,1)S(1)} async-done(((bf16[32,21,128]{2,1,0:T(8,128)(2,1)}), bf16[32,21,128]{2,1,0:T(8,128)(2,1)S(1)}, u32[]{:S(2)}, u32[]{:S(2)}) %all-to-all-start) | async-done | bytes 172064 | tf_op jit(solution)/shard_map/all_to_all | solution.py:152
  49.1 4.3 %all-to-all-start.1 = ((bf16[4,672,128]{2,1,0:T(8,128)(2,1)}), bf16[4,672,128]{2,1,0:T(8,128)(2,1)S(1)}, u32[]{:S(2)}, u32[]{:S(2)}) async-start(bf16[4,672,128]{2,1,0:T(8,128)(2,1)} %broadcast_in_dim.50), calls=%async_computation.1 | async-start | bytes 1376256 | tf_op jit(solution)/shard_map/all_to_all | solution.py:153
  53.8 1.9 %collective-permute-start.1 = (bf16[512,128]{1,0:T(8,128)(2,1)S(1)}, bf16[512,128]{1,0:T(8,128)(2,1)S(1)}, u32[]{:S(2)}, u32[]{:S(2)}) collective-permute-start(bf16[512,128]{1,0:T(8,128)(2,1)S(1)} %bitcast_select_fusion.refs_2_), channel_id=1, source_target_pairs={{0,24},{12,36},{24,48},{36,60},{48,72},{60,84},{72,96},{84,108},{9... | collective-permute-start | bytes 393224 | tf_op jit(solution)/shard_map/ppermute | solution.py:33
  55.7 3.3 %collective-permute-start.2 = (bf16[512,128]{1,0:T(8,128)(2,1)S(1)}, bf16[512,128]{1,0:T(8,128)(2,1)S(1)}, u32[]{:S(2)}, u32[]{:S(2)}) collective-permute-start(bf16[512,128]{1,0:T(8,128)(2,1)S(1)} %bitcast_select_fusion.refs_2_), channel_id=1, source_target_pairs={{0,12},{12,24},{24,36},{36,48},{48,60},{60,72},{72,84},{84,96},{96... | collective-permute-start | bytes 393224 | tf_op jit(solution)/shard_map/ppermute | solution.py:33
  59.6 17.1 %collective-permute-done.1.refs_0_ = bf16[512,128]{1,0:T(8,128)(2,1)S(1)} collective-permute-done((bf16[512,128]{1,0:T(8,128)(2,1)S(1)}, bf16[512,128]{1,0:T(8,128)(2,1)S(1)}, u32[]{:S(2)}, u32[]{:S(2)}) %collective-permute-start.1) | collective-permute-done | bytes 131104 | tf_op jit(solution)/shard_map/ppermute | solution.py:33
  76.7 2.7 %collective-permute-done.2.refs_1_ = bf16[512,128]{1,0:T(8,128)(2,1)S(1)} collective-permute-done((bf16[512,128]{1,0:T(8,128)(2,1)S(1)}, bf16[512,128]{1,0:T(8,128)(2,1)S(1)}, u32[]{:S(2)}, u32[]{:S(2)}) %collective-permute-start.2) | collective-permute-done | bytes 131104 | tf_op jit(solution)/shard_map/ppermute | solution.py:33
  80.8 5.8 %shard_map.78 = (bf16[2,2,1280,256]{3,2,1,0:T(8,128)(2,1)}, bf16[512,128]{1,0:T(8,128)(2,1)}, bf16[512,128]{1,0:T(8,128)(2,1)}, f32[512,128]{1,0:T(8,128)}) custom-call(s32[1]{0:T(128)} %bitcast.core_ref, bf16[512,128]{1,0:T(8,128)(2,1)} %copy-done.9, bf16[512,128]{1,0:T(8,128)(2,1)} %copy-done.10, bf16[512,128]{1,0:T(8,128)(2,1)} %copy-done.4, ...), custom_call_target="tpu_custom_call" | custom-call | tf_op jit(solution)/shard_map/pallas_call | solution.py:164
  90.4 10.8 %collective-permute-done.8.back1_ref = bf16[512,128]{1,0:T(8,128)(2,1)S(1)} collective-permute-done((bf16[512,128]{1,0:T(8,128)(2,1)}, bf16[512,128]{1,0:T(8,128)(2,1)S(1)}, u32[]{:S(2)}, u32[]{:S(2)}) %collective-permute-start.8) | collective-permute-done | bytes 131104 | tf_op jit(solution)/shard_map/ppermute | solution.py:33
  101.2 2.9 %collective-permute-done.9.back2_ref = bf16[512,128]{1,0:T(8,128)(2,1)S(1)} collective-permute-done((bf16[512,128]{1,0:T(8,128)(2,1)}, bf16[512,128]{1,0:T(8,128)(2,1)S(1)}, u32[]{:S(2)}, u32[]{:S(2)}) %collective-permute-start.9) | collective-permute-done | bytes 131104 | tf_op jit(solution)/shard_map/ppermute | solution.py:33
  105.3 3.5 %shard_map.81 = bf16[2688,128]{1,0:T(8,128)(2,1)} custom-call(s32[1]{0:T(128)} %bitcast.core_ref, bf16[256,2688]{1,0:T(8,128)(2,1)} %own_ref.1, bf16[256,2688]{1,0:T(8,128)(2,1)} %copy-done.1, f32[512,128]{1,0:T(8,128)} %get-tuple-element.7.part_ref, bf16[512,128]{1,0:T(8,128)(2,1)} %copy-done.11, bf16[512,128]{1,0:T(8,128)(2,1)} %copy-done.12), custom_call_target="tpu_custom_call" | custom-call | tf_op jit(solution)/shard_map/pallas_call | solution.py:187
  108.9 4.3 %all-to-all-start.2 = ((bf16[4,672,128]{2,1,0:T(8,128)(2,1)}), bf16[4,672,128]{2,1,0:T(8,128)(2,1)}, u32[]{:S(2)}, u32[]{:S(2)}) async-start(bf16[4,672,128]{2,1,0:T(8,128)(2,1)} %bitcast.21), calls=%async_computation.2 | async-start | bytes 1376256 | tf_op jit(solution)/shard_map/all_to_all | solution.py:195
  113.7 6.8 %all-to-all-done.2 = bf16[4,672,128]{2,1,0:T(8,128)(2,1)} async-done(((bf16[4,672,128]{2,1,0:T(8,128)(2,1)}), bf16[4,672,128]{2,1,0:T(8,128)(2,1)}, u32[]{:S(2)}, u32[]{:S(2)}) %all-to-all-start.2) | async-done | bytes 688160 | tf_op jit(solution)/shard_map/all_to_all | solution.py:195
  122.5 18.0 %all-to-all-start.3 = ((bf16[32,21,128]{2,1,0:T(8,128)(2,1)}), bf16[32,21,128]{2,1,0:T(8,128)(2,1)S(1)}, u32[]{:S(2)}, u32[]{:S(2)}) async-start(bf16[32,21,128]{2,1,0:T(8,128)(2,1)} %reshape.52), calls=%async_computation.3 | async-start | bytes 393216 | tf_op jit(solution)/shard_map/all_to_all | solution.py:197
  141.1 4.2 %collective-permute-start.5 = (bf16[512,128]{1,0:T(8,128)(2,1)S(1)}, bf16[512,128]{1,0:T(8,128)(2,1)S(1)}, u32[]{:S(2)}, u32[]{:S(2)}) collective-permute-start(bf16[512,128]{1,0:T(8,128)(2,1)S(1)} %pad_maximum_fusion.v0_ref), channel_id=1, source_target_pairs={{0,24},{12,36},{24,48},{36,60},{48,72},{60,84},{72,96},{84,108},{9... | collective-permute-start | bytes 393224 | tf_op jit(solution)/shard_map/ppermute | solution.py:33
  145.3 3.1 %collective-permute-start.6 = (bf16[512,128]{1,0:T(8,128)(2,1)S(1)}, bf16[512,128]{1,0:T(8,128)(2,1)S(1)}, u32[]{:S(2)}, u32[]{:S(2)}) collective-permute-start(bf16[512,128]{1,0:T(8,128)(2,1)S(1)} %pad_maximum_fusion.v0_ref), channel_id=1, source_target_pairs={{0,12},{12,24},{24,36},{36,48},{48,60},{60,72},{72,84},{84,96},{96... | collective-permute-start | bytes 393224 | tf_op jit(solution)/shard_map/ppermute | solution.py:33
  148.4 20.4 %collective-permute-done.5.v2_ref = bf16[512,128]{1,0:T(8,128)(2,1)S(1)} collective-permute-done((bf16[512,128]{1,0:T(8,128)(2,1)S(1)}, bf16[512,128]{1,0:T(8,128)(2,1)S(1)}, u32[]{:S(2)}, u32[]{:S(2)}) %collective-permute-start.5) | collective-permute-done | bytes 131104 | tf_op jit(solution)/shard_map/ppermute | solution.py:33
  168.8 6.8 %collective-permute-done.6.v1_ref = bf16[512,128]{1,0:T(8,128)(2,1)S(1)} collective-permute-done((bf16[512,128]{1,0:T(8,128)(2,1)S(1)}, bf16[512,128]{1,0:T(8,128)(2,1)S(1)}, u32[]{:S(2)}, u32[]{:S(2)}) %collective-permute-start.6) | collective-permute-done | bytes 131104 | tf_op jit(solution)/shard_map/ppermute | solution.py:33
  176.3 2.9 %shard_map.79 = bf16[256,256]{1,0:T(8,128)(2,1)} custom-call(s32[1]{0:T(128)} %bitcast.core_ref, bf16[2,2,1280,256]{3,2,1,0:T(8,128)(2,1)} %get-tuple-element.6.probs_ref, bf16[512,128]{1,0:T(8,128)(2,1)} %copy-done.6, bf16[512,128]{1,0:T(8,128)(2,1)} %copy-done.7, bf16[512,128]{1,0:T(8,128)(2,1)} %copy-done.3), custom_call_target="tpu_custom_call" | custom-call | tf_op jit(solution)/shard_map/pallas_call | solution.py:202
  179.2 2.6 %collective-permute-start.7 = (bf16[256,256]{1,0:T(8,128)(2,1)}, bf16[256,256]{1,0:T(8,128)(2,1)S(1)}, u32[]{:S(2)}, u32[]{:S(2)}) collective-permute-start(bf16[256,256]{1,0:T(8,128)(2,1)} %shard_map.79), channel_id=1, source_target_pairs={{0,6},{6,0},{1,7},{7,1},{2,8},{8,2},{3,9},{9,3},{4,10},{10,4},{5,1... | collective-permute-start | bytes 393224 | tf_op jit(solution)/shard_map/ppermute | solution.py:211
  183.7 3.1 %shard_map.80 = bf16[256,512]{1,0:T(8,128)(2,1)} custom-call(s32[1]{0:T(128)} %bitcast.core_ref, bf16[2,2,1280,256]{3,2,1,0:T(8,128)(2,1)} %get-tuple-element.6.probs_ref, bf16[512,128]{1,0:T(8,128)(2,1)} %copy-done.6, bf16[512,128]{1,0:T(8,128)(2,1)} %copy-done.7, bf16[512,128]{1,0:T(8,128)(2,1)} %copy-done.3, bf16[256,256]{1,0:T(8,128)(2,1)} %copy-done.13), custom_call_target="tpu_custom_call" | custom-call | tf_op jit(solution)/shard_map/pallas_call | solution.py:202
  (64 shorter events, 19.1 us)
Async XLA Ops:
  0.6 30.3 %copy-start.5 = (s32[32768]{0:T(1024)S(1)}, s32[32768]{0:T(1024)}, u32[]{:S(2)}) copy-start(s32[32768]{0:T(1024)} %param.11) | copy-start | bytes 393220
  0.6 103.5 %collective-permute-start.4 = (bf16[256,2688]{1,0:T(8,128)(2,1)}, bf16[256,2688]{1,0:T(8,128)(2,1)S(1)}, u32[]{:S(2)}, u32[]{:S(2)}) collective-permute-start(bf16[256,2688]{1,0:T(8,128)(2,1)} %own_ref.1), channel_id=1, source_target_pairs={{0,6},{6,0},{1,7},{7,1},{2,8},{8,2},{3,9},{9,3},{4,10},{10,4},{5,1... | collective-permute-start | bytes 4128776 | tf_op jit(solution)/shard_map/ppermute | solution.py:148
  4.3 49.3 %collective-permute-start = (bf16[256,128]{1,0:T(8,128)(2,1)S(1)}, bf16[256,128]{1,0:T(8,128)(2,1)S(1)}, u32[]{:S(2)}, u32[]{:S(2)}) collective-permute-start(bf16[256,128]{1,0:T(8,128)(2,1)S(1)} %get-tuple-element.13), channel_id=1, source_target_pairs={{0,6},{6,0},{1,7},{7,1},{2,8},{8,2},{3,9},{9,3},{4,10},{10,4},{5,1... | collective-permute-start | bytes 196616 | tf_op jit(solution)/shard_map/ppermute | solution.py:136
  7.9 71.5 %collective-permute-start.3 = (bf16[256,512]{1,0:T(8,128)(2,1)}, bf16[256,512]{1,0:T(8,128)(2,1)S(1)}, u32[]{:S(2)}, u32[]{:S(2)}) collective-permute-start(bf16[256,512]{1,0:T(8,128)(2,1)} %shard_map.77), channel_id=1, source_target_pairs={{0,6},{6,0},{1,7},{7,1},{2,8},{8,2},{3,9},{9,3},{4,10},{10,4},{5,1... | collective-permute-start | bytes 786440 | tf_op jit(solution)/shard_map/ppermute | solution.py:147
  11.8 36.3 %all-to-all-start = ((bf16[32,21,128]{2,1,0:T(8,128)(2,1)}), bf16[32,21,128]{2,1,0:T(8,128)(2,1)S(1)}, u32[]{:S(2)}, u32[]{:S(2)}) async-start(bf16[32,21,128]{2,1,0:T(8,128)(2,1)} %bitcast.4), calls=%async_computation | async-start | bytes 393216 | tf_op jit(solution)/shard_map/all_to_all | solution.py:152
  49.1 59.8 %all-to-all-start.1 = ((bf16[4,672,128]{2,1,0:T(8,128)(2,1)}), bf16[4,672,128]{2,1,0:T(8,128)(2,1)S(1)}, u32[]{:S(2)}, u32[]{:S(2)}) async-start(bf16[4,672,128]{2,1,0:T(8,128)(2,1)} %broadcast_in_dim.50), calls=%async_computation.1 | async-start | bytes 1376256 | tf_op jit(solution)/shard_map/all_to_all | solution.py:153
  53.8 25.7 %copy-start.4 = (bf16[512,128]{1,0:T(8,128)(2,1)}, bf16[512,128]{1,0:T(8,128)(2,1)S(1)}, u32[]{:S(2)}) copy-start(bf16[512,128]{1,0:T(8,128)(2,1)S(1)} %bitcast_select_fusion.refs_2_) | copy-start | bytes 393220
  53.8 23.0 %collective-permute-start.1 = (bf16[512,128]{1,0:T(8,128)(2,1)S(1)}, bf16[512,128]{1,0:T(8,128)(2,1)S(1)}, u32[]{:S(2)}, u32[]{:S(2)}) collective-permute-start(bf16[512,128]{1,0:T(8,128)(2,1)S(1)} %bitcast_select_fusion.refs_2_), channel_id=1, source_target_pairs={{0,24},{12,36},{24,48},{36,60},{48,72},{60,84},{72,96},{84,108},{9... | collective-permute-start | bytes 393224 | tf_op jit(solution)/shard_map/ppermute | solution.py:33
  55.7 23.7 %collective-permute-start.2 = (bf16[512,128]{1,0:T(8,128)(2,1)S(1)}, bf16[512,128]{1,0:T(8,128)(2,1)S(1)}, u32[]{:S(2)}, u32[]{:S(2)}) collective-permute-start(bf16[512,128]{1,0:T(8,128)(2,1)S(1)} %bitcast_select_fusion.refs_2_), channel_id=1, source_target_pairs={{0,12},{12,24},{24,36},{36,48},{48,60},{60,72},{72,84},{84,96},{96... | collective-permute-start | bytes 393224 | tf_op jit(solution)/shard_map/ppermute | solution.py:33
  76.7 2.7 %copy-start.9 = (bf16[512,128]{1,0:T(8,128)(2,1)}, bf16[512,128]{1,0:T(8,128)(2,1)S(1)}, u32[]{:S(2)}) copy-start(bf16[512,128]{1,0:T(8,128)(2,1)S(1)} %collective-permute-done.1.refs_0_) | copy-start | bytes 393220
  80.1 0.7 copy-start.8
  86.5 14.7 %collective-permute-start.8 = (bf16[512,128]{1,0:T(8,128)(2,1)}, bf16[512,128]{1,0:T(8,128)(2,1)S(1)}, u32[]{:S(2)}, u32[]{:S(2)}) collective-permute-start(bf16[512,128]{1,0:T(8,128)(2,1)} %get-tuple-element.8), channel_id=1, source_target_pairs={{12,0},{24,12},{36,24},{48,36},{60,48},{72,60},{84,72},{96,84},{10... | collective-permute-start | bytes 393224 | tf_op jit(solution)/shard_map/ppermute | solution.py:33
  88.5 15.7 %collective-permute-start.9 = (bf16[512,128]{1,0:T(8,128)(2,1)}, bf16[512,128]{1,0:T(8,128)(2,1)S(1)}, u32[]{:S(2)}, u32[]{:S(2)}) collective-permute-start(bf16[512,128]{1,0:T(8,128)(2,1)} %get-tuple-element.9), channel_id=1, source_target_pairs={{24,0},{36,12},{48,24},{60,36},{72,48},{84,60},{96,72},{108,84},{1... | collective-permute-start | bytes 393224 | tf_op jit(solution)/shard_map/ppermute | solution.py:33
  101.2 3.0 %copy-start.11 = (bf16[512,128]{1,0:T(8,128)(2,1)}, bf16[512,128]{1,0:T(8,128)(2,1)S(1)}, u32[]{:S(2)}) copy-start(bf16[512,128]{1,0:T(8,128)(2,1)S(1)} %collective-permute-done.8.back1_ref) | copy-start | bytes 393220
  104.2 1.2 copy-start.1
  108.9 4.3 %copy-start = (bf16[256,2688]{1,0:T(8,128)(2,1)S(1)}, bf16[256,2688]{1,0:T(8,128)(2,1)}, u32[]{:S(2)}) copy-start(bf16[256,2688]{1,0:T(8,128)(2,1)} %own_ref.1) | copy-start | bytes 4128772
  108.9 11.7 %all-to-all-start.2 = ((bf16[4,672,128]{2,1,0:T(8,128)(2,1)}), bf16[4,672,128]{2,1,0:T(8,128)(2,1)}, u32[]{:S(2)}, u32[]{:S(2)}) async-start(bf16[4,672,128]{2,1,0:T(8,128)(2,1)} %bitcast.21), calls=%async_computation.2 | async-start | bytes 1376256 | tf_op jit(solution)/shard_map/all_to_all | solution.py:195
  113.2 27.4 %copy-start.2 = (bf16[256,2688]{1,0:T(8,128)(2,1)S(1)}, bf16[256,2688]{1,0:T(8,128)(2,1)}, u32[]{:S(2)}) copy-start(bf16[256,2688]{1,0:T(8,128)(2,1)} %copy-done.1) | copy-start | bytes 4128772
  122.5 64.3 %all-to-all-start.3 = ((bf16[32,21,128]{2,1,0:T(8,128)(2,1)}), bf16[32,21,128]{2,1,0:T(8,128)(2,1)S(1)}, u32[]{:S(2)}, u32[]{:S(2)}) async-start(bf16[32,21,128]{2,1,0:T(8,128)(2,1)} %reshape.52), calls=%async_computation.3 | async-start | bytes 393216 | tf_op jit(solution)/shard_map/all_to_all | solution.py:197
  141.1 34.5 %copy-start.3 = (bf16[512,128]{1,0:T(8,128)(2,1)}, bf16[512,128]{1,0:T(8,128)(2,1)S(1)}, u32[]{:S(2)}) copy-start(bf16[512,128]{1,0:T(8,128)(2,1)S(1)} %pad_maximum_fusion.v0_ref) | copy-start | bytes 393220
  141.1 27.7 %collective-permute-start.5 = (bf16[512,128]{1,0:T(8,128)(2,1)S(1)}, bf16[512,128]{1,0:T(8,128)(2,1)S(1)}, u32[]{:S(2)}, u32[]{:S(2)}) collective-permute-start(bf16[512,128]{1,0:T(8,128)(2,1)S(1)} %pad_maximum_fusion.v0_ref), channel_id=1, source_target_pairs={{0,24},{12,36},{24,48},{36,60},{48,72},{60,84},{72,96},{84,108},{9... | collective-permute-start | bytes 393224 | tf_op jit(solution)/shard_map/ppermute | solution.py:33
  145.3 30.4 %collective-permute-start.6 = (bf16[512,128]{1,0:T(8,128)(2,1)S(1)}, bf16[512,128]{1,0:T(8,128)(2,1)S(1)}, u32[]{:S(2)}, u32[]{:S(2)}) collective-permute-start(bf16[512,128]{1,0:T(8,128)(2,1)S(1)} %pad_maximum_fusion.v0_ref), channel_id=1, source_target_pairs={{0,12},{12,24},{24,36},{36,48},{48,60},{60,72},{72,84},{84,96},{96... | collective-permute-start | bytes 393224 | tf_op jit(solution)/shard_map/ppermute | solution.py:33
  168.8 6.8 %copy-start.6 = (bf16[512,128]{1,0:T(8,128)(2,1)}, bf16[512,128]{1,0:T(8,128)(2,1)S(1)}, u32[]{:S(2)}) copy-start(bf16[512,128]{1,0:T(8,128)(2,1)S(1)} %collective-permute-done.5.v2_ref) | copy-start | bytes 393220
  179.2 3.8 %collective-permute-start.7 = (bf16[256,256]{1,0:T(8,128)(2,1)}, bf16[256,256]{1,0:T(8,128)(2,1)S(1)}, u32[]{:S(2)}, u32[]{:S(2)}) collective-permute-start(bf16[256,256]{1,0:T(8,128)(2,1)} %shard_map.79), channel_id=1, source_target_pairs={{0,6},{6,0},{1,7},{7,1},{2,8},{8,2},{3,9},{9,3},{4,10},{10,4},{5,1... | collective-permute-start | bytes 393224 | tf_op jit(solution)/shard_map/ppermute | solution.py:211
  (4 other events, 2.6 us)

commit v6 on v5

--- a/solution.py
+++ b/solution.py
@@ -54,7 +54,7 @@
 
 def attend_kernel(rows, factor, core_ref, *refs):
     k2_ref, k1_ref, k0_ref, q_ref, g_ref, got_ref, low_ref = refs[:7]
-    probs_ref, part2_ref, part1_ref, part0_ref, win, total = refs[7:]
+    *probs_refs, part2_ref, part1_ref, part0_ref, win, total = refs[7:]
     chip_rows = 2 * rows
     span = win.shape[0] - rows
     qw = q_ref.shape[1] // 2
@@ -79,7 +79,7 @@
             s = jnp.where(allowed, dot(keys, q, 1, 1), -1e30)
             w = jnp.exp2((s - jnp.max(s, axis=0, keepdims=True)) * factor)
             p = (w * (1.0 / jnp.sum(w, axis=0, keepdims=True))).astype(BF16)
-            probs_ref[slot, h] = p
+            probs_refs[slot][h] = p
             total[at] += dot(p, g, 1, 0)
     part2_ref[...] = total[:chip_rows].astype(BF16)
     part1_ref[...] = total[chip_rows : 2 * chip_rows].astype(BF16)
@@ -90,13 +90,13 @@
     *got, out_ref, win = rest
     chip_rows = 2 * rows
     span = win.shape[0] - rows
-    width = probs_ref.shape[1] * HD
+    width = probs_ref.shape[0] * HD
     core = core_ref[0]
     for i, ref in enumerate((v2_ref, v1_ref, v0_ref)):
         win[i * chip_rows : (i + 1) * chip_rows] = ref[...]
     j = core if slot == 0 else 1 - core
     values = win[pl.ds(pl.multiple_of(j * rows, rows), span)]
-    out = [dot(values, probs_ref[slot, h], 0, 0).T for h in range(probs_ref.shape[1])]
+    out = [dot(values, probs_ref[h], 0, 0).T for h in range(probs_ref.shape[0])]
     out = jnp.concatenate(out, axis=1).astype(BF16)
     if slot == 0:
         out_ref[:, part_of(core, width)] = out
@@ -161,16 +161,17 @@
     begin = jnp.maximum(begin, jnp.arange(1, rows + 1, dtype=jnp.int32)[None])
     begin = jnp.where(first, begin, begin[::-1])
 
-    probs, part2, part1, part0 = pl.pallas_call(
+    *probs, part2, part1, part0 = pl.pallas_call(
         functools.partial(attend_kernel, rows, factor),
         out_shape=(
-            struct((2, group, span, rows), BF16),
+            struct((group, span, rows), BF16),
+            struct((group, span, rows), BF16),
             struct((chip_rows, kv), BF16),
             struct((chip_rows, kv), BF16),
             struct((chip_rows, kv), F32),
         ),
         in_specs=[SMEM] + [VMEM] * 7,
-        out_specs=[VMEM] * 4,
+        out_specs=[VMEM] * 5,
         scratch_shapes=[pltpu.VMEM((whole, kv), BF16), pltpu.VMEM((whole, kv), F32)],
     )(core_arg, k_two, k_one, k_chip, queries, grads, got, begin)
     back2 = chip_shift(part2, -2)
@@ -194,9 +195,13 @@
 
     term = lax.all_to_all(term.reshape(nx, -1, kv), "x", 0, 0)
     term = jnp.sum(term.astype(F32), axis=0).astype(BF16)
-    term = lax.all_to_all(term.reshape(nz * ny * 2, cut, kv), ("zh", "y", "c"), 0, 0)
-    term = jnp.sum(term.astype(F32).reshape(nz * ny, 2, cut, kv), axis=0)
-    weight_grad = jnp.concatenate([term[0], term[1]], axis=1)
+    term = term.reshape(nz, ny * 2, cut, kv).transpose(1, 0, 2, 3)
+    term = lax.all_to_all(term, ("y", "c"), 0, 0)
+    term = jnp.sum(term.astype(F32).reshape(ny, 2, nz, cut, kv), axis=0)
+    term = jnp.concatenate([term[0], term[1]], axis=2)
+    low = lax.axis_index("zh") == 0
+    far = lax.ppermute(jnp.where(low, term[1], term[0]), "zh", SWAP)
+    weight_grad = jnp.where(low, term[0], term[1]) + far
 
     def outputs(slot, *got):
         return pl.pallas_call(
@@ -205,7 +210,7 @@
             in_specs=[SMEM] + [VMEM] * (4 + len(got)),
             out_specs=VMEM,
             scratch_shapes=[pltpu.VMEM((whole, kv), BF16)],
-        )(core_arg, probs, v_two, v_one, v_chip, *got)
+        )(core_arg, probs[slot], v_two, v_one, v_chip, *got)
 
     out_send = outputs(1)
     out_got = lax.ppermute(out_send, "c", SWAP)

time: 188 us -> 185 us (0.984)
  the two profiles are of different devices: /device:TPU:67 before, /device:TPU:71 now
where the time goes in v6:
time: 185 us; the launch traced here: 184 us
  starting transfers between devices  78.2 us (42%)
  waiting for transfers between devices  76.9 us (42%)
  Pallas kernels  16.2 us (9%)
  local copies, waits for them, and re-layouts  7.49 us (4%)
  other arithmetic  3.07 us (2%)
    ppermute x6, waiting for transfers between devices, chip_shift(): return lax.ppermute(block, CHIPS, route)  53.3 us
    all_to_all x1, starting transfers between devices, per_device(): w_y = lax.all_to_all(tile, ('zh', 'y', 'c'), 0, 0).reshape(-1, kv)  19.1 us
    all_to_all x1, waiting for transfers between devices, per_device(): w_y = lax.all_to_all(tile, ('zh', 'y', 'c'), 0, 0).reshape(-1, kv)  16.6 us
    ppermute x6, starting transfers between devices, chip_shift(): return lax.ppermute(block, CHIPS, route)  16.3 us
    all_to_all x1, starting transfers between devices, per_device(): term = lax.all_to_all(term, ('y', 'c'), 0, 0)  12.7 us
    ppermute x1, starting transfers between devices, per_device(): far = lax.ppermute(jnp.where(low, term[1], term[0]), 'zh', SWAP)  11.8 us
    all_to_all x1, waiting for transfers between devices, per_device(): term = lax.all_to_all(term.reshape(nx, -1, kv), 'x', 0, 0)  7.03 us
    pallas_call x1, Pallas kernels, per_device(): pl.pallas_call(functools.partial(attend_kernel, rows, factor), out_shape=...  5.79 us
  transfers between devices with their start and end apart: 15, of which 8 were waited for; matrix products, arithmetic and copies ran while one was open for 3% of the time, Pallas kernels for 9%

profile of v6, /device:TPU:71, one launch (start us, length us, event | category | flops | bytes accessed | tf_op | source)
XLA Modules:
  0.0 183.9 jit_solution(9741104256291291096)
XLA Ops:
  0.6 2.7 %collective-permute-start.4 = (bf16[256,2688]{1,0:T(8,128)(2,1)}, bf16[256,2688]{1,0:T(8,128)(2,1)S(1)}, u32[]{:S(2)}, u32[]{:S(2)}) collective-permute-start(bf16[256,2688]{1,0:T(8,128)(2,1)} %own_ref.1), channel_id=1, source_target_pairs={{0,6},{6,0},{1,7},{7,1},{2,8},{8,2},{3,9},{9,3},{4,10},{10,4},{5,1... | collective-permute-start | bytes 4128776 | tf_op jit(solution)/shard_map/ppermute | solution.py:148
  4.3 1.9 %collective-permute-start = (bf16[256,128]{1,0:T(8,128)(2,1)S(1)}, bf16[256,128]{1,0:T(8,128)(2,1)S(1)}, u32[]{:S(2)}, u32[]{:S(2)}) collective-permute-start(bf16[256,128]{1,0:T(8,128)(2,1)S(1)} %get-tuple-element.15), channel_id=1, source_target_pairs={{0,6},{6,0},{1,7},{7,1},{2,8},{8,2},{3,9},{9,3},{4,10},{10,4},{5,1... | collective-permute-start | bytes 196616 | tf_op jit(solution)/shard_map/ppermute | solution.py:136
  7.9 2.4 %collective-permute-start.3 = (bf16[256,512]{1,0:T(8,128)(2,1)}, bf16[256,512]{1,0:T(8,128)(2,1)S(1)}, u32[]{:S(2)}, u32[]{:S(2)}) collective-permute-start(bf16[256,512]{1,0:T(8,128)(2,1)} %shard_map.77), channel_id=1, source_target_pairs={{0,6},{6,0},{1,7},{7,1},{2,8},{8,2},{3,9},{9,3},{4,10},{10,4},{5,1... | collective-permute-start | bytes 786440 | tf_op jit(solution)/shard_map/ppermute | solution.py:147
  11.8 19.1 %all-to-all-start = ((bf16[32,21,128]{2,1,0:T(8,128)(2,1)}), bf16[32,21,128]{2,1,0:T(8,128)(2,1)S(1)}, u32[]{:S(2)}, u32[]{:S(2)}) async-start(bf16[32,21,128]{2,1,0:T(8,128)(2,1)} %bitcast.4), calls=%async_computation | async-start | bytes 393216 | tf_op jit(solution)/shard_map/all_to_all | solution.py:152
  31.5 16.6 %all-to-all-done = bf16[32,21,128]{2,1,0:T(8,128)(2,1)S(1)} async-done(((bf16[32,21,128]{2,1,0:T(8,128)(2,1)}), bf16[32,21,128]{2,1,0:T(8,128)(2,1)S(1)}, u32[]{:S(2)}, u32[]{:S(2)}) %all-to-all-start) | async-done | bytes 172064 | tf_op jit(solution)/shard_map/all_to_all | solution.py:152
  49.1 4.2 %all-to-all-start.1 = ((bf16[4,672,128]{2,1,0:T(8,128)(2,1)}), bf16[4,672,128]{2,1,0:T(8,128)(2,1)S(1)}, u32[]{:S(2)}, u32[]{:S(2)}) async-start(bf16[4,672,128]{2,1,0:T(8,128)(2,1)} %broadcast_in_dim.50), calls=%async_computation.1 | async-start | bytes 1376256 | tf_op jit(solution)/shard_map/all_to_all | solution.py:153
  55.6 3.3 %collective-permute-start.2 = (bf16[512,128]{1,0:T(8,128)(2,1)S(1)}, bf16[512,128]{1,0:T(8,128)(2,1)S(1)}, u32[]{:S(2)}, u32[]{:S(2)}) collective-permute-start(bf16[512,128]{1,0:T(8,128)(2,1)S(1)} %bitcast_select_fusion.refs_2_), channel_id=1, source_target_pairs={{0,12},{12,24},{24,36},{36,48},{48,60},{60,72},{72,84},{84,96},{96... | collective-permute-start | bytes 393224 | tf_op jit(solution)/shard_map/ppermute | solution.py:33
  59.6 17.4 %collective-permute-done.1.refs_0_ = bf16[512,128]{1,0:T(8,128)(2,1)S(1)} collective-permute-done((bf16[512,128]{1,0:T(8,128)(2,1)S(1)}, bf16[512,128]{1,0:T(8,128)(2,1)S(1)}, u32[]{:S(2)}, u32[]{:S(2)}) %collective-permute-start.1) | collective-permute-done | bytes 131104 | tf_op jit(solution)/shard_map/ppermute | solution.py:33
  76.9 3.1 %collective-permute-done.2.refs_1_ = bf16[512,128]{1,0:T(8,128)(2,1)S(1)} collective-permute-done((bf16[512,128]{1,0:T(8,128)(2,1)S(1)}, bf16[512,128]{1,0:T(8,128)(2,1)S(1)}, u32[]{:S(2)}, u32[]{:S(2)}) %collective-permute-start.2) | collective-permute-done | bytes 131104 | tf_op jit(solution)/shard_map/ppermute | solution.py:33
  81.4 5.8 %shard_map.78 = (bf16[2,1280,256]{2,1,0:T(8,128)(2,1)}, bf16[2,1280,256]{2,1,0:T(8,128)(2,1)}, bf16[512,128]{1,0:T(8,128)(2,1)}, bf16[512,128]{1,0:T(8,128)(2,1)}, f32[512,128]{1,0:T(8,128)}) custom-call(s32[1]{0:T(128)} %bitcast.core_ref, bf16[512,128]{1,0:T(8,128)(2,1)} %copy-done.10, bf16[512,128]{1,0:T(8,128)(2,1)} %copy-done.11, ...), custom_call_target="tpu_custom_call" | custom-call | tf_op jit(solution)/shard_map/pallas_call | solution.py:164
  91.0 8.9 %collective-permute-done.8.back1_ref = bf16[512,128]{1,0:T(8,128)(2,1)S(1)} collective-permute-done((bf16[512,128]{1,0:T(8,128)(2,1)}, bf16[512,128]{1,0:T(8,128)(2,1)S(1)}, u32[]{:S(2)}, u32[]{:S(2)}) %collective-permute-start.8) | collective-permute-done | bytes 131104 | tf_op jit(solution)/shard_map/ppermute | solution.py:33
  100.0 3.2 %collective-permute-done.9.back2_ref = bf16[512,128]{1,0:T(8,128)(2,1)S(1)} collective-permute-done((bf16[512,128]{1,0:T(8,128)(2,1)}, bf16[512,128]{1,0:T(8,128)(2,1)S(1)}, u32[]{:S(2)}, u32[]{:S(2)}) %collective-permute-start.9) | collective-permute-done | bytes 131104 | tf_op jit(solution)/shard_map/ppermute | solution.py:33
  104.3 3.5 %shard_map.81 = bf16[2688,128]{1,0:T(8,128)(2,1)} custom-call(s32[1]{0:T(128)} %bitcast.core_ref, bf16[256,2688]{1,0:T(8,128)(2,1)} %own_ref.1, bf16[256,2688]{1,0:T(8,128)(2,1)} %copy-done.1, f32[512,128]{1,0:T(8,128)} %get-tuple-element.9.part_ref, bf16[512,128]{1,0:T(8,128)(2,1)} %copy-done.12, bf16[512,128]{1,0:T(8,128)(2,1)} %copy-done.13), custom_call_target="tpu_custom_call" | custom-call | tf_op jit(solution)/shard_map/pallas_call | solution.py:188
  107.8 4.1 %all-to-all-start.2 = ((bf16[4,672,128]{2,1,0:T(8,128)(2,1)}), bf16[4,672,128]{2,1,0:T(8,128)(2,1)S(1)}, u32[]{:S(2)}, u32[]{:S(2)}) async-start(bf16[4,672,128]{2,1,0:T(8,128)(2,1)} %bitcast.28), calls=%async_computation.2 | async-start | bytes 1376256 | tf_op jit(solution)/shard_map/all_to_all | solution.py:196
  112.4 7.0 %all-to-all-done.2 = bf16[4,672,128]{2,1,0:T(8,128)(2,1)S(1)} async-done(((bf16[4,672,128]{2,1,0:T(8,128)(2,1)}), bf16[4,672,128]{2,1,0:T(8,128)(2,1)S(1)}, u32[]{:S(2)}, u32[]{:S(2)}) %all-to-all-start.2) | async-done | bytes 688160 | tf_op jit(solution)/shard_map/all_to_all | solution.py:196
  120.5 12.7 %all-to-all-start.3 = ((bf16[16,2,21,128]{3,1,2,0:T(2,128)(2,1)}), bf16[16,2,21,128]{3,1,2,0:T(2,128)(2,1)S(1)}, u32[]{:S(2)}, u32[]{:S(2)}) async-start(bf16[16,2,21,128]{3,1,2,0:T(2,128)(2,1)} %copy.15), calls=%async_computation.3 | async-start | bytes 344064 | tf_op jit(solution)/shard_map/all_to_all | solution.py:199
  133.8 4.2 %collective-permute-start.5 = (bf16[512,128]{1,0:T(8,128)(2,1)S(1)}, bf16[512,128]{1,0:T(8,128)(2,1)S(1)}, u32[]{:S(2)}, u32[]{:S(2)}) collective-permute-start(bf16[512,128]{1,0:T(8,128)(2,1)S(1)} %pad_maximum_fusion.v0_ref), channel_id=1, source_target_pairs={{0,24},{12,36},{24,48},{36,60},{48,72},{60,84},{72,96},{84,108},{9... | collective-permute-start | bytes 393224 | tf_op jit(solution)/shard_map/ppermute | solution.py:33
  137.9 3.1 %collective-permute-start.6 = (bf16[512,128]{1,0:T(8,128)(2,1)S(1)}, bf16[512,128]{1,0:T(8,128)(2,1)S(1)}, u32[]{:S(2)}, u32[]{:S(2)}) collective-permute-start(bf16[512,128]{1,0:T(8,128)(2,1)S(1)} %pad_maximum_fusion.v0_ref), channel_id=1, source_target_pairs={{0,12},{12,24},{24,36},{36,48},{48,60},{60,72},{72,84},{84,96},{96... | collective-permute-start | bytes 393224 | tf_op jit(solution)/shard_map/ppermute | solution.py:33
  141.1 13.5 %collective-permute-done.5.v2_ref = bf16[512,128]{1,0:T(8,128)(2,1)S(1)} collective-permute-done((bf16[512,128]{1,0:T(8,128)(2,1)S(1)}, bf16[512,128]{1,0:T(8,128)(2,1)S(1)}, u32[]{:S(2)}, u32[]{:S(2)}) %collective-permute-start.5) | collective-permute-done | bytes 131104 | tf_op jit(solution)/shard_map/ppermute | solution.py:33
  154.6 7.2 %collective-permute-done.6.v1_ref = bf16[512,128]{1,0:T(8,128)(2,1)S(1)} collective-permute-done((bf16[512,128]{1,0:T(8,128)(2,1)S(1)}, bf16[512,128]{1,0:T(8,128)(2,1)S(1)}, u32[]{:S(2)}, u32[]{:S(2)}) %collective-permute-start.6) | collective-permute-done | bytes 131104 | tf_op jit(solution)/shard_map/ppermute | solution.py:33
  162.4 2.5 %shard_map.79 = bf16[256,256]{1,0:T(8,128)(2,1)} custom-call(s32[1]{0:T(128)} %bitcast.core_ref, bf16[2,1280,256]{2,1,0:T(8,128)(2,1)} %get-tuple-element.8.probs_ref, bf16[512,128]{1,0:T(8,128)(2,1)} %copy-done.6, bf16[512,128]{1,0:T(8,128)(2,1)} %copy-done.7, bf16[512,128]{1,0:T(8,128)(2,1)} %copy-done.3), custom_call_target="tpu_custom_call" | custom-call | tf_op jit(solution)/shard_map/pallas_call | solution.py:207
  165.0 2.9 %collective-permute-start.7 = (bf16[256,256]{1,0:T(8,128)(2,1)}, bf16[256,256]{1,0:T(8,128)(2,1)S(1)}, u32[]{:S(2)}, u32[]{:S(2)}) collective-permute-start(bf16[256,256]{1,0:T(8,128)(2,1)} %shard_map.79), channel_id=1, source_target_pairs={{0,6},{6,0},{1,7},{7,1},{2,8},{8,2},{3,9},{9,3},{4,10},{10,4},{5,1... | collective-permute-start | bytes 393224 | tf_op jit(solution)/shard_map/ppermute | solution.py:216
  168.1 11.8 %collective-permute-start.10 = (f32[21,256]{1,0:T(8,128)S(1)}, f32[21,256]{1,0:T(8,128)S(1)}, u32[]{:S(2)}, u32[]{:S(2)}) collective-permute-start(f32[21,256]{1,0:T(8,128)S(1)} %select_bitcast_fusion), channel_id=1, source_target_pairs={{0,96},{96,0},{1,97},{97,1},{2,98},{98,2},{3,99},{99,3},{4,100},{1... | collective-permute-start | bytes 64520 | tf_op jit(solution)/shard_map/ppermute | solution.py:203
  180.6 2.6 %shard_map.80 = bf16[256,512]{1,0:T(8,128)(2,1)} custom-call(s32[1]{0:T(128)} %bitcast.core_ref, bf16[2,1280,256]{2,1,0:T(8,128)(2,1)} %get-tuple-element.7.probs_ref, bf16[512,128]{1,0:T(8,128)(2,1)} %copy-done.6, bf16[512,128]{1,0:T(8,128)(2,1)} %copy-done.7, bf16[512,128]{1,0:T(8,128)(2,1)} %copy-done.3, bf16[256,256]{1,0:T(8,128)(2,1)} %copy-done.9), custom_call_target="tpu_custom_call" | custom-call | tf_op jit(solution)/shard_map/pallas_call | solution.py:207
  (69 shorter events, 19.1 us)
Async XLA Ops:
  0.6 30.3 %copy-start.5 = (s32[32768]{0:T(1024)S(1)}, s32[32768]{0:T(1024)}, u32[]{:S(2)}) copy-start(s32[32768]{0:T(1024)} %param.11) | copy-start | bytes 393220
  0.6 102.5 %collective-permute-start.4 = (bf16[256,2688]{1,0:T(8,128)(2,1)}, bf16[256,2688]{1,0:T(8,128)(2,1)S(1)}, u32[]{:S(2)}, u32[]{:S(2)}) collective-permute-start(bf16[256,2688]{1,0:T(8,128)(2,1)} %own_ref.1), channel_id=1, source_target_pairs={{0,6},{6,0},{1,7},{7,1},{2,8},{8,2},{3,9},{9,3},{4,10},{10,4},{5,1... | collective-permute-start | bytes 4128776 | tf_op jit(solution)/shard_map/ppermute | solution.py:148
  4.3 49.3 %collective-permute-start = (bf16[256,128]{1,0:T(8,128)(2,1)S(1)}, bf16[256,128]{1,0:T(8,128)(2,1)S(1)}, u32[]{:S(2)}, u32[]{:S(2)}) collective-permute-start(bf16[256,128]{1,0:T(8,128)(2,1)S(1)} %get-tuple-element.15), channel_id=1, source_target_pairs={{0,6},{6,0},{1,7},{7,1},{2,8},{8,2},{3,9},{9,3},{4,10},{10,4},{5,1... | collective-permute-start | bytes 196616 | tf_op jit(solution)/shard_map/ppermute | solution.py:136
  7.9 72.1 %collective-permute-start.3 = (bf16[256,512]{1,0:T(8,128)(2,1)}, bf16[256,512]{1,0:T(8,128)(2,1)S(1)}, u32[]{:S(2)}, u32[]{:S(2)}) collective-permute-start(bf16[256,512]{1,0:T(8,128)(2,1)} %shard_map.77), channel_id=1, source_target_pairs={{0,6},{6,0},{1,7},{7,1},{2,8},{8,2},{3,9},{9,3},{4,10},{10,4},{5,1... | collective-permute-start | bytes 786440 | tf_op jit(solution)/shard_map/ppermute | solution.py:147
  11.8 36.3 %all-to-all-start = ((bf16[32,21,128]{2,1,0:T(8,128)(2,1)}), bf16[32,21,128]{2,1,0:T(8,128)(2,1)S(1)}, u32[]{:S(2)}, u32[]{:S(2)}) async-start(bf16[32,21,128]{2,1,0:T(8,128)(2,1)} %bitcast.4), calls=%async_computation | async-start | bytes 393216 | tf_op jit(solution)/shard_map/all_to_all | solution.py:152
  49.1 58.7 %all-to-all-start.1 = ((bf16[4,672,128]{2,1,0:T(8,128)(2,1)}), bf16[4,672,128]{2,1,0:T(8,128)(2,1)S(1)}, u32[]{:S(2)}, u32[]{:S(2)}) async-start(bf16[4,672,128]{2,1,0:T(8,128)(2,1)} %broadcast_in_dim.50), calls=%async_computation.1 | async-start | bytes 1376256 | tf_op jit(solution)/shard_map/all_to_all | solution.py:153
  53.7 26.3 %copy-start.4 = (bf16[512,128]{1,0:T(8,128)(2,1)}, bf16[512,128]{1,0:T(8,128)(2,1)S(1)}, u32[]{:S(2)}) copy-start(bf16[512,128]{1,0:T(8,128)(2,1)S(1)} %bitcast_select_fusion.refs_2_) | copy-start | bytes 393220
  53.7 23.2 %collective-permute-start.1 = (bf16[512,128]{1,0:T(8,128)(2,1)S(1)}, bf16[512,128]{1,0:T(8,128)(2,1)S(1)}, u32[]{:S(2)}, u32[]{:S(2)}) collective-permute-start(bf16[512,128]{1,0:T(8,128)(2,1)S(1)} %bitcast_select_fusion.refs_2_), channel_id=1, source_target_pairs={{0,24},{12,36},{24,48},{36,60},{48,72},{60,84},{72,96},{84,108},{9... | collective-permute-start | bytes 393224 | tf_op jit(solution)/shard_map/ppermute | solution.py:33
  55.6 24.4 %collective-permute-start.2 = (bf16[512,128]{1,0:T(8,128)(2,1)S(1)}, bf16[512,128]{1,0:T(8,128)(2,1)S(1)}, u32[]{:S(2)}, u32[]{:S(2)}) collective-permute-start(bf16[512,128]{1,0:T(8,128)(2,1)S(1)} %bitcast_select_fusion.refs_2_), channel_id=1, source_target_pairs={{0,12},{12,24},{24,36},{36,48},{48,60},{60,72},{72,84},{84,96},{96... | collective-permute-start | bytes 393224 | tf_op jit(solution)/shard_map/ppermute | solution.py:33
  76.9 3.1 %copy-start.10 = (bf16[512,128]{1,0:T(8,128)(2,1)}, bf16[512,128]{1,0:T(8,128)(2,1)S(1)}, u32[]{:S(2)}) copy-start(bf16[512,128]{1,0:T(8,128)(2,1)S(1)} %collective-permute-done.1.refs_0_) | copy-start | bytes 393220
  87.2 12.8 %collective-permute-start.8 = (bf16[512,128]{1,0:T(8,128)(2,1)}, bf16[512,128]{1,0:T(8,128)(2,1)S(1)}, u32[]{:S(2)}, u32[]{:S(2)}) collective-permute-start(bf16[512,128]{1,0:T(8,128)(2,1)} %get-tuple-element.10), channel_id=1, source_target_pairs={{12,0},{24,12},{36,24},{48,36},{60,48},{72,60},{84,72},{96,84},{10... | collective-permute-start | bytes 393224 | tf_op jit(solution)/shard_map/ppermute | solution.py:33
  89.1 14.0 %collective-permute-start.9 = (bf16[512,128]{1,0:T(8,128)(2,1)}, bf16[512,128]{1,0:T(8,128)(2,1)S(1)}, u32[]{:S(2)}, u32[]{:S(2)}) collective-permute-start(bf16[512,128]{1,0:T(8,128)(2,1)} %get-tuple-element.11), channel_id=1, source_target_pairs={{24,0},{36,12},{48,24},{60,36},{72,48},{84,60},{96,72},{108,84},{1... | collective-permute-start | bytes 393224 | tf_op jit(solution)/shard_map/ppermute | solution.py:33
  100.0 3.2 %copy-start.12 = (bf16[512,128]{1,0:T(8,128)(2,1)}, bf16[512,128]{1,0:T(8,128)(2,1)S(1)}, u32[]{:S(2)}) copy-start(bf16[512,128]{1,0:T(8,128)(2,1)S(1)} %collective-permute-done.8.back1_ref) | copy-start | bytes 393220
  103.1 1.2 copy-start.1
  107.8 4.1 %copy-start = (bf16[256,2688]{1,0:T(8,128)(2,1)S(1)}, bf16[256,2688]{1,0:T(8,128)(2,1)}, u32[]{:S(2)}) copy-start(bf16[256,2688]{1,0:T(8,128)(2,1)} %own_ref.1) | copy-start | bytes 4128772
  107.8 11.6 %all-to-all-start.2 = ((bf16[4,672,128]{2,1,0:T(8,128)(2,1)}), bf16[4,672,128]{2,1,0:T(8,128)(2,1)S(1)}, u32[]{:S(2)}, u32[]{:S(2)}) async-start(bf16[4,672,128]{2,1,0:T(8,128)(2,1)} %bitcast.28), calls=%async_computation.2 | async-start | bytes 1376256 | tf_op jit(solution)/shard_map/all_to_all | solution.py:196
  112.4 20.8 %copy-start.2 = (bf16[256,2688]{1,0:T(8,128)(2,1)S(1)}, bf16[256,2688]{1,0:T(8,128)(2,1)}, u32[]{:S(2)}) copy-start(bf16[256,2688]{1,0:T(8,128)(2,1)} %copy-done.1) | copy-start | bytes 4128772
  120.5 47.4 %all-to-all-start.3 = ((bf16[16,2,21,128]{3,1,2,0:T(2,128)(2,1)}), bf16[16,2,21,128]{3,1,2,0:T(2,128)(2,1)S(1)}, u32[]{:S(2)}, u32[]{:S(2)}) async-start(bf16[16,2,21,128]{3,1,2,0:T(2,128)(2,1)} %copy.15), calls=%async_computation.3 | async-start | bytes 344064 | tf_op jit(solution)/shard_map/all_to_all | solution.py:199
  133.8 28.0 %copy-start.3 = (bf16[512,128]{1,0:T(8,128)(2,1)}, bf16[512,128]{1,0:T(8,128)(2,1)S(1)}, u32[]{:S(2)}) copy-start(bf16[512,128]{1,0:T(8,128)(2,1)S(1)} %pad_maximum_fusion.v0_ref) | copy-start | bytes 393220
  133.8 20.8 %collective-permute-start.5 = (bf16[512,128]{1,0:T(8,128)(2,1)S(1)}, bf16[512,128]{1,0:T(8,128)(2,1)S(1)}, u32[]{:S(2)}, u32[]{:S(2)}) collective-permute-start(bf16[512,128]{1,0:T(8,128)(2,1)S(1)} %pad_maximum_fusion.v0_ref), channel_id=1, source_target_pairs={{0,24},{12,36},{24,48},{36,60},{48,72},{60,84},{72,96},{84,108},{9... | collective-permute-start | bytes 393224 | tf_op jit(solution)/shard_map/ppermute | solution.py:33
  137.9 23.8 %collective-permute-start.6 = (bf16[512,128]{1,0:T(8,128)(2,1)S(1)}, bf16[512,128]{1,0:T(8,128)(2,1)S(1)}, u32[]{:S(2)}, u32[]{:S(2)}) collective-permute-start(bf16[512,128]{1,0:T(8,128)(2,1)S(1)} %pad_maximum_fusion.v0_ref), channel_id=1, source_target_pairs={{0,12},{12,24},{24,36},{36,48},{48,60},{60,72},{72,84},{84,96},{96... | collective-permute-start | bytes 393224 | tf_op jit(solution)/shard_map/ppermute | solution.py:33
  154.6 7.2 %copy-start.6 = (bf16[512,128]{1,0:T(8,128)(2,1)}, bf16[512,128]{1,0:T(8,128)(2,1)S(1)}, u32[]{:S(2)}) copy-start(bf16[512,128]{1,0:T(8,128)(2,1)S(1)} %collective-permute-done.5.v2_ref) | copy-start | bytes 393220
  165.0 15.0 %collective-permute-start.7 = (bf16[256,256]{1,0:T(8,128)(2,1)}, bf16[256,256]{1,0:T(8,128)(2,1)S(1)}, u32[]{:S(2)}, u32[]{:S(2)}) collective-permute-start(bf16[256,256]{1,0:T(8,128)(2,1)} %shard_map.79), channel_id=1, source_target_pairs={{0,6},{6,0},{1,7},{7,1},{2,8},{8,2},{3,9},{9,3},{4,10},{10,4},{5,1... | collective-permute-start | bytes 393224 | tf_op jit(solution)/shard_map/ppermute | solution.py:216
  168.1 15.1 %collective-permute-start.10 = (f32[21,256]{1,0:T(8,128)S(1)}, f32[21,256]{1,0:T(8,128)S(1)}, u32[]{:S(2)}, u32[]{:S(2)}) collective-permute-start(f32[21,256]{1,0:T(8,128)S(1)} %select_bitcast_fusion), channel_id=1, source_target_pairs={{0,96},{96,0},{1,97},{97,1},{2,98},{98,2},{3,99},{99,3},{4,100},{1... | collective-permute-start | bytes 64520 | tf_op jit(solution)/shard_map/ppermute | solution.py:203
  (5 other events, 3.3 us)
